TPU v7x, 32 devices: a whole 2x2x4 slice. The times are simulated.
32 devices in a mesh: wide: 16 (over z, x, core), narrow: 2 (over y).
Axes of the slice: x: 2, y: 2, z: 4, core: 2. Of those that a mesh axis runs over, the one named last changes fastest.
Arguments:
- frames: bfloat16 [4096, 1024], P(('wide', 'narrow')), may hold values from -13 to 13
- lengths: int32 [32, 4], P(('wide', 'narrow')), may hold values from 1 to 96, 128 in all within a row
- out_grad: bfloat16 [4096, 1024], P(('wide', 'narrow')), may hold values from -6 to 6
- up_weight: float32 [2, 1024, 4096], P(None, ('wide', 'narrow')), may hold values from -0.1875 to 0.1875
- down_weight: float32 [2, 4096, 1024], P(None, ('wide', 'narrow')), may hold values from -0.09375 to 0.09375
- square_weight: float32 [8, 1024, 1024], P(None, ('wide', 'narrow')), may hold values from -0.75 to 0.75
- chan_weight: float32 [45, 1024], P(None, ('wide', 'narrow')), may hold values from -1.2 to 1.3
- up_moment: float32 [2, 1024, 4096], P(None, ('wide', 'narrow')), may hold values from -80 to 80
- down_moment: float32 [2, 4096, 1024], P(None, ('wide', 'narrow')), may hold values from -80 to 80
- square_moment: float32 [8, 1024, 1024], P(None, ('wide', 'narrow')), may hold values from -80 to 80
- chan_moment: float32 [45, 1024], P(None, ('wide', 'narrow')), may hold values from -80 to 80
- up_average: float32 [2, 1024, 4096], P(None, ('wide', 'narrow')), may hold values from -0.1875 to 0.1875
- down_average: float32 [2, 4096, 1024], P(None, ('wide', 'narrow')), may hold values from -0.09375 to 0.09375
- square_average: float32 [8, 1024, 1024], P(None, ('wide', 'narrow')), may hold values from -0.1875 to 0.1875
- chan_average: float32 [45, 1024], P(None, ('wide', 'narrow')), may hold values from -3 to 3
Outputs:
- output: bfloat16 [4096, 1024], P(('wide', 'narrow'))
- frames_grad: bfloat16 [4096, 1024], P(('wide', 'narrow'))
- up_grad: float32 [2, 1024, 4096], P(None, ('wide', 'narrow'))
- down_grad: float32 [2, 4096, 1024], P(None, ('wide', 'narrow'))
- square_grad: float32 [8, 1024, 1024], P(None, ('wide', 'narrow'))
- chan_grad: float32 [45, 1024], P(None, ('wide', 'narrow'))
- up_moment_new: float32 [2, 1024, 4096], P(None, ('wide', 'narrow'))
- down_moment_new: float32 [2, 4096, 1024], P(None, ('wide', 'narrow'))
- square_moment_new: float32 [8, 1024, 1024], P(None, ('wide', 'narrow'))
- chan_moment_new: float32 [45, 1024], P(None, ('wide', 'narrow'))
- up_weight_new: float32 [2, 1024, 4096], P(None, ('wide', 'narrow'))
- down_weight_new: float32 [2, 4096, 1024], P(None, ('wide', 'narrow'))
- square_weight_new: float32 [8, 1024, 1024], P(None, ('wide', 'narrow'))
- chan_weight_new: float32 [45, 1024], P(None, ('wide', 'narrow'))
- up_average_new: float32 [2, 1024, 4096], P(None, ('wide', 'narrow'))
- down_average_new: float32 [2, 4096, 1024], P(None, ('wide', 'narrow'))
- square_average_new: float32 [8, 1024, 1024], P(None, ('wide', 'narrow'))
- chan_average_new: float32 [45, 1024], P(None, ('wide', 'narrow'))
- bias_grad: float32 [2, 1024], P(None, ('wide', 'narrow'))
Inputs may be any that keep to these rules, and one draw needn't show every extreme that they name: `lengths`: each row sums to 128; its largest entry is 96.
All inputs are finite; a program needn't handle non-finite values.
Results may differ from a plain program's by a relative error of at most 0.018.
Values may be sent and summed in bfloat16 or wider, within the bound.
No kernel may reach another device: no remote copies, remote signals or barrier semaphores. Data moves between devices by JAX's collectives and lax.ppermute only.
A program may use at most 256 MiB of HBM per device.

v0:
```python
import jax
import jax.numpy as jnp
from jax import lax
from jax.sharding import PartitionSpec as P

HEADS = 16


EPSILON = 1e-05
MOMENTUM_DECAY = 0.9
AVERAGE_DECAY = 0.9
RATE_UP = 0.05
RATE_DOWN = 0.026
RATE_SQUARE = 0.05
RATE_CHANNEL = 0.5
MASKED_SCORE = -1e30


def matmul(left, right):
    return jnp.dot(left, right, preferred_element_type=jnp.float32)


def rows_inner(left, right):
    return lax.dot_general(
        left, right, (((0,), (0,)), ((), ())), preferred_element_type=jnp.float32
    )


def cols_inner(left, right):
    return lax.dot_general(
        left, right, (((1,), (1,)), ((), ())), preferred_element_type=jnp.float32
    )


def swish_unit(values):
    return values * jax.nn.sigmoid(values)


def layer_norm(values, gain_row, shift_row):
    centre = values - jnp.mean(values, axis=-1, keepdims=True)
    spread = jnp.mean(centre * centre, axis=-1, keepdims=True)
    return centre * lax.rsqrt(spread + EPSILON) * gain_row + shift_row


def item_segments(length_row, slot_count, item_count):
    bounds = jnp.cumsum(length_row[:item_count], dtype=jnp.int32)
    where_at = jnp.arange(slot_count, dtype=jnp.int32)
    return jnp.sum(
        (where_at[:, None] >= bounds[None, :]).astype(jnp.int32), axis=1, dtype=jnp.int32
    )


def offset_table(slot_count, model_width):
    offsets = jnp.arange(2 * slot_count - 1, dtype=jnp.float32) - (slot_count - 1)
    freqs = jnp.exp(
        -jnp.log(10000.0) * jnp.arange(0, model_width, 2, dtype=jnp.float32) / model_width
    )
    angles = offsets[:, None] * freqs[None, :]
    return jnp.concatenate([jnp.sin(angles), jnp.cos(angles)], axis=1)


def shift_relative_scores(unshifted_position_scores):
    slot_count = unshifted_position_scores.shape[-2]
    leading = unshifted_position_scores.shape[:-2]
    padded = jnp.pad(unshifted_position_scores, [(0, 0)] * len(leading) + [(0, 0), (0, 1)])
    flat_rows = padded.reshape(leading + (2 * slot_count * slot_count,))
    flat_rows = flat_rows[..., slot_count - 1 : slot_count - 1 + slot_count * (2 * slot_count - 1)]
    return flat_rows.reshape(leading + (slot_count, 2 * slot_count - 1))[..., :slot_count]


def depth_conv(glu_rows, tap_rows, segment):
    slot_count = glu_rows.shape[0]
    half_width = tap_rows.shape[0] // 2
    padded = jnp.pad(glu_rows, ((half_width, half_width), (0, 0)))
    segment_pad = jnp.pad(segment, (half_width, half_width), constant_values=-1)
    total = jnp.zeros_like(glu_rows)
    for tap_index in range(tap_rows.shape[0]):
        nearby = lax.slice_in_dim(padded, tap_index, tap_index + slot_count, axis=0)
        match = lax.slice_in_dim(segment_pad, tap_index, tap_index + slot_count, axis=0) == segment
        total = total + jnp.where(match[:, None], nearby, 0.0) * tap_rows[tap_index]
    return total


def attention_scores(
    query_c, query_position_side, key_rows, position_embed_rows, segment, score_scale
):
    content = jnp.einsum("thd,shd->hts", query_c, key_rows, preferred_element_type=jnp.float32)
    unshifted_position_scores = jnp.einsum(
        "yia,xia->iyx", query_position_side, position_embed_rows, preferred_element_type=jnp.float32
    )
    total = (content + shift_relative_scores(unshifted_position_scores)) * score_scale
    same_item = segment[:, None] == segment[None, :]
    return (jnp.where(same_item[None], total, MASKED_SCORE), unshifted_position_scores)


def ffn_forward(stream, gain_row, shift_row, up_matrix, down_matrix):
    normed = layer_norm(stream, gain_row, shift_row).astype(jnp.bfloat16)
    before = matmul(normed, up_matrix)
    active = swish_unit(before).astype(jnp.bfloat16)
    return (stream + 0.5 * matmul(active, down_matrix), (normed, before, active))


def ffn_backward(grad_stream, stream, gain_row, shift_row, up_matrix, down_matrix, saved_values):
    normed, before, active = saved_values
    grad_branch = (0.5 * grad_stream).astype(jnp.bfloat16)
    down_term = rows_inner(active, grad_branch)
    grad_active = cols_inner(grad_branch, down_matrix)
    _, swish_pull = jax.vjp(swish_unit, before)
    grad_before = swish_pull(grad_active)[0].astype(jnp.bfloat16)
    up_term = rows_inner(normed, grad_before)
    grad_normed = cols_inner(grad_before, up_matrix)
    _, norm_pull = jax.vjp(layer_norm, stream, gain_row, shift_row)
    grad_input, gain_term, shift_term = norm_pull(grad_normed)
    return (grad_stream + grad_input, up_term, down_term, gain_term, shift_term)


def attention_forward(
    stream,
    gain_row,
    shift_row,
    square_full,
    bias_content,
    bias_place,
    segment,
    head_count,
    score_scale,
):
    slot_count, model_width = stream.shape
    head_size = model_width // head_count
    normed = layer_norm(stream, gain_row, shift_row).astype(jnp.bfloat16)
    query_rows = matmul(normed, square_full[0])
    key_rows = (
        matmul(normed, square_full[1])
        .astype(jnp.bfloat16)
        .reshape(slot_count, head_count, head_size)
    )
    value_rows = (
        matmul(normed, square_full[2])
        .astype(jnp.bfloat16)
        .reshape(slot_count, head_count, head_size)
    )
    place_table = offset_table(slot_count, model_width).astype(jnp.bfloat16)
    position_embed_rows = (
        matmul(place_table, square_full[4])
        .astype(jnp.bfloat16)
        .reshape(2 * slot_count - 1, head_count, head_size)
    )
    query_c = (
        (query_rows + bias_content).astype(jnp.bfloat16).reshape(slot_count, head_count, head_size)
    )
    query_position_side = (
        (query_rows + bias_place).astype(jnp.bfloat16).reshape(slot_count, head_count, head_size)
    )
    scores, _ = attention_scores(
        query_c, query_position_side, key_rows, position_embed_rows, segment, score_scale
    )
    log_total = jax.nn.logsumexp(scores, axis=-1)
    soft_weights = jnp.exp(scores - log_total[..., None]).astype(jnp.bfloat16)
    mixed_rows = jnp.einsum(
        "hts,shd->thd", soft_weights, value_rows, preferred_element_type=jnp.float32
    )
    mixed_rows = mixed_rows.reshape(slot_count, model_width).astype(jnp.bfloat16)
    saved_values = (
        normed,
        query_c,
        query_position_side,
        key_rows,
        value_rows,
        place_table,
        position_embed_rows,
        log_total,
        mixed_rows,
    )
    return (stream + matmul(mixed_rows, square_full[3]), saved_values)


def attention_backward(
    grad_stream,
    stream,
    gain_row,
    shift_row,
    square_full,
    segment,
    head_count,
    score_scale,
    saved_values,
):
    (
        normed,
        query_c,
        query_position_side,
        key_rows,
        value_rows,
        place_table,
        position_embed_rows,
        log_total,
        mixed_rows,
    ) = saved_values
    slot_count, model_width = grad_stream.shape
    head_size = model_width // head_count
    grad_branch = grad_stream.astype(jnp.bfloat16)
    out_term = rows_inner(mixed_rows, grad_branch)
    grad_mixed = (
        cols_inner(grad_branch, square_full[3])
        .astype(jnp.bfloat16)
        .reshape(slot_count, head_count, head_size)
    )
    scores, unshifted_position_scores = attention_scores(
        query_c, query_position_side, key_rows, position_embed_rows, segment, score_scale
    )
    soft_weights = jnp.exp(scores - log_total[..., None])
    grad_soft = jnp.einsum(
        "thd,shd->hts", grad_mixed, value_rows, preferred_element_type=jnp.float32
    )
    grad_value = jnp.einsum(
        "hts,thd->shd",
        soft_weights.astype(jnp.bfloat16),
        grad_mixed,
        preferred_element_type=jnp.float32,
    )
    grad_scores = soft_weights * (
        grad_soft - jnp.sum(soft_weights * grad_soft, axis=-1, keepdims=True)
    )
    grad_scaled = grad_scores.astype(jnp.bfloat16) * score_scale
    grad_query_c = jnp.einsum(
        "hts,shd->thd", grad_scaled, key_rows, preferred_element_type=jnp.float32
    )
    grad_key = jnp.einsum("hts,thd->shd", grad_scaled, query_c, preferred_element_type=jnp.float32)
    _, shift_pull = jax.vjp(shift_relative_scores, unshifted_position_scores)
    unshifted_score_grad = shift_pull(grad_scaled.astype(jnp.float32))[0].astype(jnp.bfloat16)
    grad_query_p = jnp.einsum(
        "vnj,jvc->nvc",
        unshifted_score_grad,
        position_embed_rows,
        preferred_element_type=jnp.float32,
    )
    position_table_grad = jnp.einsum(
        "jwq,wjg->qjg",
        unshifted_score_grad,
        query_position_side,
        preferred_element_type=jnp.float32,
    )
    position_table_grad = position_table_grad.reshape(2 * slot_count - 1, model_width).astype(
        jnp.bfloat16
    )
    place_term = rows_inner(place_table, position_table_grad)
    bias_content_term = jnp.sum(grad_query_c, axis=0).reshape(model_width)
    bias_place_term = jnp.sum(grad_query_p, axis=0).reshape(model_width)
    grad_query = (grad_query_c + grad_query_p).reshape(slot_count, model_width).astype(jnp.bfloat16)
    grad_key_rows = grad_key.reshape(slot_count, model_width).astype(jnp.bfloat16)
    grad_value_rows = grad_value.reshape(slot_count, model_width).astype(jnp.bfloat16)
    query_term = rows_inner(normed, grad_query)
    key_term = rows_inner(normed, grad_key_rows)
    value_term = rows_inner(normed, grad_value_rows)
    grad_normed = cols_inner(grad_query, square_full[0]) + cols_inner(grad_key_rows, square_full[1])
    grad_normed = grad_normed + cols_inner(grad_value_rows, square_full[2])
    _, norm_pull = jax.vjp(layer_norm, stream, gain_row, shift_row)
    grad_input, gain_term, shift_term = norm_pull(grad_normed)
    square_terms = (query_term, key_term, value_term, out_term, place_term)
    return (
        grad_stream + grad_input,
        square_terms,
        gain_term,
        shift_term,
        bias_content_term,
        bias_place_term,
    )


def nesterov(weight, moment, average, grad_rows, rate, rate_scale):
    moment_new = MOMENTUM_DECAY * moment + grad_rows
    weight_new = weight - rate * rate_scale * (grad_rows + MOMENTUM_DECAY * moment_new)
    average_new = AVERAGE_DECAY * average + (1.0 - AVERAGE_DECAY) * weight_new
    return (moment_new, weight_new, average_new)


def shards(
    frames,
    lengths,
    out_grad,
    up_weight,
    down_weight,
    square_weight,
    chan_weight,
    up_moment,
    down_moment,
    square_moment,
    chan_moment,
    up_average,
    down_average,
    square_average,
    chan_average,
):
    slot_count = frames.shape[0]
    head_count = HEADS
    score_scale = (frames.shape[1] // head_count) ** (-0.5)
    item_count = lengths.shape[1] - 1
    tap_count = chan_weight.shape[0] - 14
    segment = item_segments(lengths[0], slot_count, item_count)
    valid = (segment < item_count).astype(jnp.float32)[:, None]
    lowered = (
        up_weight.astype(jnp.bfloat16),
        down_weight.astype(jnp.bfloat16),
        square_weight.astype(jnp.bfloat16),
        chan_weight.astype(jnp.bfloat16),
    )
    up_full, down_full, square_full, chan_full = (
        lax.all_gather(lowered[0], ("wide", "narrow"), axis=1, tiled=True),
        lax.all_gather(lowered[1], ("wide", "narrow"), axis=1, tiled=True),
        lax.all_gather(lowered[2], ("wide", "narrow"), axis=1, tiled=True),
        lax.all_gather(lowered[3], ("wide", "narrow"), axis=1, tiled=True),
    )
    chan_float = chan_full.astype(jnp.float32)
    stream_zero = frames.astype(jnp.float32)
    stream_one, saved_one = ffn_forward(
        stream_zero, chan_float[tap_count], chan_float[tap_count + 5], up_full[0], down_full[0]
    )
    stream_two, saved_attention = attention_forward(
        stream_one,
        chan_float[tap_count + 1],
        chan_float[tap_count + 6],
        square_full,
        chan_float[tap_count + 12],
        chan_float[tap_count + 13],
        segment,
        head_count,
        score_scale,
    )
    normed_conv = layer_norm(
        stream_two, chan_float[tap_count + 2], chan_float[tap_count + 7]
    ).astype(jnp.bfloat16)
    gate_first = matmul(normed_conv, square_full[5])
    gate_second = matmul(normed_conv, square_full[6])

    def conv_front(first_half, second_half, tap_rows):
        return depth_conv(first_half * jax.nn.sigmoid(second_half) * valid, tap_rows, segment)

    conv_rows = conv_front(gate_first, gate_second, chan_float[:tap_count])
    total_rows, frame_count = lax.psum(
        (jnp.sum(conv_rows * valid, axis=0), jnp.sum(valid)), ("wide", "narrow")
    )
    mean_rows = total_rows / frame_count
    centred = (conv_rows - mean_rows) * valid
    square_sum = lax.psum(jnp.sum(centred * centred, axis=0), ("wide", "narrow"))
    variance = square_sum / frame_count
    spread_inv = lax.rsqrt(variance + EPSILON)
    centred_rows = (conv_rows - mean_rows) * spread_inv
    batch_normed = centred_rows * chan_float[tap_count + 10] + chan_float[tap_count + 11]
    active_conv = swish_unit(batch_normed).astype(jnp.bfloat16)
    stream_three = stream_two + matmul(active_conv, square_full[7])
    stream_four, saved_four = ffn_forward(
        stream_three, chan_float[tap_count + 3], chan_float[tap_count + 8], up_full[1], down_full[1]
    )
    output = (
        layer_norm(stream_four, chan_float[tap_count + 4], chan_float[tap_count + 9]) * valid
    ).astype(jnp.bfloat16)
    back_up, back_down, back_square, back_chan = (
        lax.all_gather(lowered[0], ("wide", "narrow"), axis=1, tiled=True),
        lax.all_gather(lowered[1], ("wide", "narrow"), axis=1, tiled=True),
        lax.all_gather(lowered[2], ("wide", "narrow"), axis=1, tiled=True),
        lax.all_gather(lowered[3], ("wide", "narrow"), axis=1, tiled=True),
    )
    back_float = back_chan.astype(jnp.float32)
    grad_final = out_grad.astype(jnp.float32) * valid
    _, final_pull = jax.vjp(
        layer_norm, stream_four, back_float[tap_count + 4], back_float[tap_count + 9]
    )
    grad_four, gain_four, shift_four = final_pull(grad_final)
    grad_three, up_second, down_second, gain_three, shift_three = ffn_backward(
        grad_four,
        stream_three,
        back_float[tap_count + 3],
        back_float[tap_count + 8],
        back_up[1],
        back_down[1],
        saved_four,
    )
    grad_branch = grad_three.astype(jnp.bfloat16)
    conv_out_term = rows_inner(active_conv, grad_branch)
    grad_active = cols_inner(grad_branch, back_square[7])
    _, swish_pull = jax.vjp(swish_unit, batch_normed)
    grad_batch = swish_pull(grad_active)[0]
    batch_gain_term = jnp.sum(grad_batch * centred_rows, axis=0)
    batch_shift_term = jnp.sum(grad_batch, axis=0)
    grad_centred = grad_batch * back_float[tap_count + 10]
    sum_plain, sum_cross = lax.psum(
        (
            jnp.sum(grad_centred * valid, axis=0),
            jnp.sum(grad_centred * centred_rows * valid, axis=0),
        ),
        ("wide", "narrow"),
    )
    grad_conv = (
        valid
        * spread_inv
        * (grad_centred - sum_plain / frame_count - centred_rows * sum_cross / frame_count)
    )
    _, front_pull = jax.vjp(conv_front, gate_first, gate_second, back_float[:tap_count])
    grad_first, grad_second, tap_term = front_pull(grad_conv)
    grad_first = grad_first.astype(jnp.bfloat16)
    grad_second = grad_second.astype(jnp.bfloat16)
    first_term = rows_inner(normed_conv, grad_first)
    second_term = rows_inner(normed_conv, grad_second)
    grad_normed_conv = cols_inner(grad_first, back_square[5]) + cols_inner(
        grad_second, back_square[6]
    )
    _, conv_norm_pull = jax.vjp(
        layer_norm, stream_two, back_float[tap_count + 2], back_float[tap_count + 7]
    )
    grad_conv_input, gain_two, shift_two = conv_norm_pull(grad_normed_conv)
    grad_two = grad_three + grad_conv_input
    grad_one, attention_terms, gain_one, shift_one, bias_content_term, bias_place_term = (
        attention_backward(
            grad_two,
            stream_one,
            back_float[tap_count + 1],
            back_float[tap_count + 6],
            back_square,
            segment,
            head_count,
            score_scale,
            saved_attention,
        )
    )
    grad_zero, up_first, down_first, gain_zero, shift_zero = ffn_backward(
        grad_one,
        stream_zero,
        back_float[tap_count],
        back_float[tap_count + 5],
        back_up[0],
        back_down[0],
        saved_one,
    )
    frames_grad = grad_zero.astype(jnp.bfloat16)
    square_term = jnp.stack(list(attention_terms) + [first_term, second_term, conv_out_term])
    vector_terms = jnp.stack(
        [
            gain_zero,
            gain_one,
            gain_two,
            gain_three,
            gain_four,
            shift_zero,
            shift_one,
            shift_two,
            shift_three,
            shift_four,
            batch_gain_term,
            batch_shift_term,
            bias_content_term,
            bias_place_term,
        ]
    )
    chan_term = jnp.concatenate([tap_term, vector_terms], axis=0)
    up_term = jnp.stack([up_first, up_second])
    down_term = jnp.stack([down_first, down_second])
    up_grad, down_grad, square_grad, chan_grad = (
        lax.psum_scatter(up_term, ("wide", "narrow"), scatter_dimension=1, tiled=True),
        lax.psum_scatter(down_term, ("wide", "narrow"), scatter_dimension=1, tiled=True),
        lax.psum_scatter(square_term, ("wide", "narrow"), scatter_dimension=1, tiled=True),
        lax.psum_scatter(chan_term, ("wide", "narrow"), scatter_dimension=1, tiled=True),
    )
    rate_scale = lax.rsqrt(frame_count)
    up_new = nesterov(up_weight, up_moment, up_average, up_grad, RATE_UP, rate_scale)
    down_new = nesterov(down_weight, down_moment, down_average, down_grad, RATE_DOWN, rate_scale)
    square_new = nesterov(
        square_weight, square_moment, square_average, square_grad, RATE_SQUARE, rate_scale
    )
    chan_new = nesterov(chan_weight, chan_moment, chan_average, chan_grad, RATE_CHANNEL, rate_scale)
    bias_grad = chan_grad[tap_count + 12 : tap_count + 14]
    return (
        output,
        frames_grad,
        up_grad,
        down_grad,
        square_grad,
        chan_grad,
        up_new[0],
        down_new[0],
        square_new[0],
        chan_new[0],
        up_new[1],
        down_new[1],
        square_new[1],
        chan_new[1],
        up_new[2],
        down_new[2],
        square_new[2],
        chan_new[2],
        bias_grad,
    )


def solution(mesh):
    return jax.shard_map(
        shards,
        mesh=mesh,
        in_specs=(
            P(("wide", "narrow"), None),
            P(("wide", "narrow"), None),
            P(("wide", "narrow"), None),
            P(None, ("wide", "narrow"), None),
            P(None, ("wide", "narrow"), None),
            P(None, ("wide", "narrow"), None),
            P(None, ("wide", "narrow")),
            P(None, ("wide", "narrow"), None),
            P(None, ("wide", "narrow"), None),
            P(None, ("wide", "narrow"), None),
            P(None, ("wide", "narrow")),
            P(None, ("wide", "narrow"), None),
            P(None, ("wide", "narrow"), None),
            P(None, ("wide", "narrow"), None),
            P(None, ("wide", "narrow")),
        ),
        out_specs=(
            P(("wide", "narrow"), None),
            P(("wide", "narrow"), None),
            P(None, ("wide", "narrow"), None),
            P(None, ("wide", "narrow"), None),
            P(None, ("wide", "narrow"), None),
            P(None, ("wide", "narrow")),
            P(None, ("wide", "narrow"), None),
            P(None, ("wide", "narrow"), None),
            P(None, ("wide", "narrow"), None),
            P(None, ("wide", "narrow")),
            P(None, ("wide", "narrow"), None),
            P(None, ("wide", "narrow"), None),
            P(None, ("wide", "narrow"), None),
            P(None, ("wide", "narrow")),
            P(None, ("wide", "narrow"), None),
            P(None, ("wide", "narrow"), None),
            P(None, ("wide", "narrow"), None),
            P(None, ("wide", "narrow")),
            P(None, ("wide", "narrow")),
        ),
        check_vma=False,
    )
```

profile of v0, /device:TPU:0, one launch (start us, length us, event | category | flops | bytes accessed | tf_op | source)
XLA Modules:
  0.0 2905.9 jit_solution(17054627176118846827)
XLA Ops:
  14.4 73.2 %all_gather.16 = bf16[45,1024]{0,1:T(8,128)(2,1)S(1)} all-gather(bf16[45,32]{0,1:T(8,128)(2,1)S(1)} %convert_element_type.169), channel_id=1, replica_groups=mesh['wide'=16,'narrow'=2] {'wide','narrow'}, dimensions={1}, use_global_device_ids=true | all-gather | bytes 95040 | tf_op jit(solution)/shard_map/all_gather | solution.py:311
  98.1 5.7 slice_reduce_fusion.36
  103.8 5.8 slice_reduce_fusion.1
  109.6 20.4 all-gather.4.cloned.1.call-done
  130.0 4.7 fusion.2
  134.8 112.0 %all-gather.6.cloned.1.call-done = bf16[2,4096,1024]{2,1,0:T(8,128)(2,1)} async-done(((bf16[2,128,1024]{2,1,0:T(8,128)(2,1)}), bf16[2,4096,1024]{2,1,0:T(8,128)(2,1)}) %all-gather.6.cloned.1.call-update) | async-done | bytes 16777232 | tf_op jit(solution)/shard_map/all_gather | solution.py:309
  246.8 4.8 fusion.174
  252.6 110.4 %all-gather.8.cloned.1.call-done = bf16[8,1024,1024]{2,1,0:T(8,128)(2,1)} async-done(((bf16[8,32,1024]{2,1,0:T(8,128)(2,1)}), bf16[8,1024,1024]{2,1,0:T(8,128)(2,1)}) %all-gather.8.cloned.1.call-update) | async-done | bytes 16777232 | tf_op jit(solution)/shard_map/all_gather | solution.py:310
  371.3 4.6 reshape.530
  396.4 4.5 multiply_reduce_fusion.46
  400.9 38.9 %all-reduce.68 = (f32[1024]{0:T(1024)S(1)}, f32[]{:T(128)}) all-reduce(f32[1024]{0:T(1024)} %get-tuple-element.198, f32[]{:T(128)} %fusion.163), channel_id=1, replica_groups=mesh['wide'=16,'narrow'=2] {'wide','narrow'}, use_global_device_ids=true, to_apply=%region_11.12 | all-reduce | flops 1025 | bytes 8200 | tf_op jit(solution)/shard_map/psum | solution.py:339
  441.2 41.1 %psum.37 = f32[1024]{0:T(1024)} all-reduce(f32[1024]{0:T(1024)S(1)} %multiply_reduce_fusion.45), channel_id=1, replica_groups=mesh['wide'=16,'narrow'=2] {'wide','narrow'}, use_global_device_ids=true, to_apply=%region_15.16 | all-reduce | flops 1024 | bytes 8192 | tf_op jit(solution)/shard_map/psum | solution.py:344
  486.1 4.7 fusion.6
  490.9 5.6 fusion.178
  498.7 7.0 fusion.11
  514.6 39.8 %all-reduce.67 = (f32[1024]{0:T(1024)}, f32[1024]{0:T(1024)}) all-reduce(f32[1024]{0:T(1024)} %get-tuple-element.77, f32[1024]{0:T(1024)} %get-tuple-element.119), channel_id=1, replica_groups=mesh['wide'=16,'narrow'=2] {'wide','narrow'}, use_global_device_ids=true, to_apply=%region_27.28 | all-reduce | flops 2048 | bytes 16384 | tf_op jit(solution)/shard_map/psum | solution.py:386
  615.4 6.4 fusion.14
  623.2 6.4 fusion.167
  662.4 11.2 pad_maximum_fusion
  681.9 11.9 pad_maximum_fusion.1
  697.6 72.2 %reduce-scatter.13.cloned.1.call-done = f32[32,45]{1,0:T(8,128)} async-done(((f32[1024,45]{1,0:T(8,128)}), f32[32,45]{1,0:T(8,128)}) %reduce-scatter.13.cloned.1.call-update) | async-done | bytes 5776
  773.1 701.3 %reduce-scatter.11.cloned.1.call-done = f32[8,32,1024]{2,1,0:T(8,128)} async-done(((f32[8,1024,1024]{2,1,0:T(8,128)}), f32[8,32,1024]{2,1,0:T(8,128)}) %reduce-scatter.11.cloned.1.call-update) | async-done | bytes 1048592 | tf_op jit(solution)/shard_map/reduce_scatter | solution.py:460
  1478.4 706.1 %reduce-scatter.7.cloned.1.call-done = f32[2,32,4096]{2,1,0:T(8,128)} async-done(((f32[2,1024,4096]{2,1,0:T(8,128)}), f32[2,32,4096]{2,1,0:T(8,128)}) %reduce-scatter.7.cloned.1.call-update) | async-done | bytes 1048592 | tf_op jit(solution)/shard_map/reduce_scatter | solution.py:458
  2188.3 706.5 %reduce-scatter.9.cloned.1.call-done = f32[2,128,1024]{2,1,0:T(8,128)} async-done(((f32[2,4096,1024]{2,1,0:T(8,128)}), f32[2,128,1024]{2,1,0:T(8,128)}) %reduce-scatter.9.cloned.1.call-update) | async-done | bytes 1048592 | tf_op jit(solution)/shard_map/reduce_scatter | solution.py:459
  (540 shorter events, 182.9 us)
Async XLA Ops:
  7.2 122.8 %all-gather.4.cloned.1.call-start = ((), (), s32[]{:S(2)}) async-start(), calls=%async_computation.4 | async-start | bytes 17301504 | tf_op jit(solution)/shard_map/all_gather | solution.py:308
  9.3 237.5 %all-gather.6.cloned.1.call-start = ((), (), s32[]{:S(2)}) async-start(), calls=%async_computation.5 | async-start | bytes 17301504 | tf_op jit(solution)/shard_map/all_gather | solution.py:309
  11.5 351.6 %all-gather.8.cloned.1.call-start = ((), (), s32[]{:S(2)}) async-start(), calls=%async_computation.6 | async-start | bytes 17301504 | tf_op jit(solution)/shard_map/all_gather | solution.py:310
  13.7 756.0 %reduce-scatter.13.cloned.1.call-start = ((), (), s32[]{:S(2)}) async-start(), calls=%async_computation.10 | async-start | bytes 540672
  90.3 39.7 %copy-start.110 = (f32[128]{0:T(128)}, f32[128]{0:T(128)S(1)}, u32[]{:S(2)}) copy-start(f32[128]{0:T(128)S(1)} %broadcast_multiply_fusion.5) | copy-start | bytes 1540
  93.5 36.5 %copy-start.135 = (f32[128]{0:T(128)}, f32[128]{0:T(128)S(1)}, u32[]{:S(2)}) copy-start(f32[128]{0:T(128)S(1)} %fusion.152) | copy-start | bytes 1540
  98.1 31.9 %copy-start = (bf16[128,1024]{1,0:T(8,128)(2,1)S(1)}, bf16[128,1024]{1,0:T(8,128)(2,1)}, u32[]{:S(2)}) copy-start(bf16[128,1024]{1,0:T(8,128)(2,1)} %param.15) | copy-start | bytes 786436
  109.6 446.2 %copy-start.51 = (f32[1024]{0:T(1024)}, f32[1024]{0:T(1024)S(1)}, u32[]{:S(2)}) copy-start(f32[1024]{0:T(1024)S(1)} %get-tuple-element.131) | copy-start | bytes 12292
  134.8 116.8 %copy-start.22 = (f32[128,4096]{1,0:T(8,128)}, f32[128,4096]{1,0:T(8,128)S(1)}, u32[]{:S(2)}) copy-start(f32[128,4096]{1,0:T(8,128)S(1)} %fusion.2) | copy-start | bytes 6291460
  134.8 228.3 %copy-start.174 = (f32[1024]{0:T(1024)S(1)}, f32[1024]{0:T(1024)}, u32[]{:S(2)}) copy-start(f32[1024]{0:T(1024)} %get-tuple-element.165) | copy-start | bytes 12292
  134.8 231.2 %copy-start.42 = (bf16[255,512]{1,0:T(8,128)(2,1)S(1)}, bf16[255,512]{1,0:T(8,128)(2,1)}, u32[]{:S(2)}) copy-start(bf16[255,512]{1,0:T(8,128)(2,1)} %get-tuple-element.238) | copy-start | bytes 783364
  251.6 117.8 %copy-start.140 = (f32[128]{0:T(128)}, f32[128]{0:T(128)S(1)}, u32[]{:S(2)}) copy-start(f32[128]{0:T(128)S(1)} %broadcast_multiply_fusion.4) | copy-start | bytes 1540
  251.8 114.0 %copy-start.183 = (f32[128]{0:T(128)}, f32[128]{0:T(128)S(1)}, u32[]{:S(2)}) copy-start(f32[128]{0:T(128)S(1)} %multiply_reduce_fusion.48) | copy-start | bytes 1540
  251.9 117.6 %copy-start.170 = (f32[128]{0:T(128)}, f32[128]{0:T(128)S(1)}, u32[]{:S(2)}) copy-start(f32[128]{0:T(128)S(1)} %fusion.153) | copy-start | bytes 1540
  252.6 113.4 %copy-start.14 = (bf16[128,1024]{1,0:T(8,128)(2,1)}, bf16[128,1024]{1,0:T(8,128)(2,1)S(1)}, u32[]{:S(2)}) copy-start(bf16[128,1024]{1,0:T(8,128)(2,1)S(1)} %add_convert_fusion.6) | copy-start | bytes 786436
  440.4 115.5 %copy-start.48 = (f32[1024]{0:T(1024)}, f32[1024]{0:T(1024)S(1)}, u32[]{:S(2)}) copy-start(f32[1024]{0:T(1024)S(1)} %broadcast_divide_fusion.1) | copy-start | bytes 12292
  483.6 72.2 %copy-start.53 = (f32[1024]{0:T(1024)}, f32[1024]{0:T(1024)S(1)}, u32[]{:S(2)}) copy-start(f32[1024]{0:T(1024)S(1)} %add_rsqrt_fusion) | copy-start | bytes 12292
  509.3 57.1 %copy-start.60 = (f32[1024]{0:T(1024)S(1)}, f32[1024]{0:T(1024)}, u32[]{:S(2)}) copy-start(f32[1024]{0:T(1024)} %get-tuple-element.138) | copy-start | bytes 12292
  634.5 840.0 %reduce-scatter.11.cloned.1.call-start = ((), (), s32[]{:S(2)}) async-start(), calls=%async_computation.9 | async-start | bytes 34603008 | tf_op jit(solution)/shard_map/reduce_scatter | solution.py:460
  656.0 1528.6 %reduce-scatter.7.cloned.1.call-start = ((), (), s32[]{:S(2)}) async-start(), calls=%async_computation.7 | async-start | bytes 34603008 | tf_op jit(solution)/shard_map/reduce_scatter | solution.py:458
  673.6 2221.2 %reduce-scatter.9.cloned.1.call-start = ((), (), s32[]{:S(2)}) async-start(), calls=%async_computation.8 | async-start | bytes 34603008 | tf_op jit(solution)/shard_map/reduce_scatter | solution.py:459
  693.8 780.6 %copy-start.19 = (f32[8,32,1024]{2,1,0:T(8,128)S(1)}, f32[8,32,1024]{2,1,0:T(8,128)}, u32[]{:S(2)}) copy-start(f32[8,32,1024]{2,1,0:T(8,128)} %param.20) | copy-start | bytes 3145732
  694.5 1490.1 %copy-start.20 = (f32[2,32,4096]{2,1,0:T(8,128)S(1)}, f32[2,32,4096]{2,1,0:T(8,128)}, u32[]{:S(2)}) copy-start(f32[2,32,4096]{2,1,0:T(8,128)} %param.18) | copy-start | bytes 3145732
  697.6 2197.3 %copy-start.21 = (f32[2,128,1024]{2,1,0:T(8,128)S(1)}, f32[2,128,1024]{2,1,0:T(8,128)}, u32[]{:S(2)}) copy-start(f32[2,128,1024]{2,1,0:T(8,128)} %param.19) | copy-start | bytes 3145732
  (174 other events, 1543.0 us)
Sparse Core Ops, SparseCore 0:
  11.6 118.3 all-gather.3
  133.6 113.1 all-gather.5
  250.5 112.5 all-gather.7
  634.6 135.0 reduce-scatter.12
  772.5 701.8 reduce-scatter.10
  1477.3 707.2 reduce-scatter.6
  2187.5 707.2 reduce-scatter.8
where the time goes:
time: 2910 us
  waiting for transfers between devices  2430 us (84%)
  blocking collectives  193 us (7%)
  matrix products  138 us (5%)
  other arithmetic  83.3 us (3%)
  local copies, waits for them, and re-layouts  43.7 us (2%)
    reduce_scatter x1, waiting for transfers between devices, shards(): lax.psum_scatter(down_term, ('wide', 'narrow'), scatter_dimension=1, tile...  706 us
    reduce_scatter x1, waiting for transfers between devices, shards(): lax.psum_scatter(up_term, ('wide', 'narrow'), scatter_dimension=1, tiled=...  706 us
    reduce_scatter x1, waiting for transfers between devices, shards(): lax.psum_scatter(square_term, ('wide', 'narrow'), scatter_dimension=1, ti...  701 us
    all_gather x1, waiting for transfers between devices, shards(): lax.all_gather(lowered[1], ('wide', 'narrow'), axis=1, tiled=True)  112 us
    all_gather x1, waiting for transfers between devices, shards(): lax.all_gather(lowered[2], ('wide', 'narrow'), axis=1, tiled=True)  110 us
    all_gather x1, blocking collectives, shards(): lax.all_gather(lowered[3], ('wide', 'narrow'), axis=1, tiled=True)  73.2 us
    unnamed x8, waiting for transfers between devices  72.3 us
  transfers between devices with their start and end apart: 7, of which 7 were waited for; matrix products, arithmetic and copies ran while one was open for 4% of the time, Pallas kernels for 0%

commit v1 on v0

v1 whole, which is shorter than its diff:
```python
import jax
import jax.numpy as jnp
from jax import lax
from jax.sharding import Mesh
from jax.sharding import PartitionSpec as P

HEADS = 16
EPSILON = 1e-05
MOMENTUM_DECAY = 0.9
AVERAGE_DECAY = 0.9
RATE_UP = 0.05
RATE_DOWN = 0.026
RATE_SQUARE = 0.05
RATE_CHANNEL = 0.5
MASKED_SCORE = -1e30
BF16 = jnp.bfloat16
F32 = jnp.float32
ALL = ("z", "x", "c", "y")


def mm(left, right):
    return jnp.dot(left, right, preferred_element_type=F32)


def mm_tn(left, right):
    return lax.dot_general(left, right, (((0,), (0,)), ((), ())), preferred_element_type=F32)


def mm_nt(left, right):
    return lax.dot_general(left, right, (((1,), (1,)), ((), ())), preferred_element_type=F32)


def swap(values, axis, bit=1):
    size = lax.axis_size(axis)
    return lax.ppermute(values, axis, [(i, i ^ bit) for i in range(size)])


def swish_grad(values):
    sig = jax.nn.sigmoid(values)
    return sig * (1.0 + values * (1.0 - sig))


def normalize(values):
    centre = values - jnp.mean(values, axis=-1, keepdims=True)
    scale = lax.rsqrt(jnp.mean(centre * centre, axis=-1, keepdims=True) + EPSILON)
    return centre * scale, scale


def layer_norm(values, gain_row, shift_row):
    return normalize(values)[0] * gain_row + shift_row


def layer_norm_back(values, gain_row, grad):
    unit, scale = normalize(values)
    grad_unit = grad * gain_row
    inner = jnp.mean(grad_unit, axis=-1, keepdims=True)
    cross = jnp.mean(grad_unit * unit, axis=-1, keepdims=True)
    grad_in = scale * (grad_unit - inner - unit * cross)
    return grad_in, jnp.sum(grad * unit, axis=0), jnp.sum(grad, axis=0)


def team_gather(values, wide_team):
    half = values.shape[0] // 2
    from_x = swap(values, "x")
    from_c = swap(values, "c")
    if not wide_team:
        return [jnp.concatenate([values, from_c]), jnp.concatenate([from_x, swap(from_x, "c")])]
    from_y = swap(values, "y")
    far = jnp.concatenate([swap(from_x[:half], "y"), swap(from_y[half:], "x")])
    return [
        jnp.concatenate([values, from_c]),
        jnp.concatenate([from_x, swap(from_x, "c")]),
        jnp.concatenate([from_y, swap(from_y, "c")]),
        jnp.concatenate([far, swap(far, "c")]),
    ]


def team_gather_small(values, wide_team):
    near = [values, swap(values, "c")]
    across = swap(jnp.stack(near), "x")
    rows = near + [across[0], across[1]]
    if wide_team:
        side = swap(jnp.stack(rows), "y")
        rows = rows + [side[i] for i in range(4)]
    return rows


def team_scatter(pairs, wide_team):
    slots = pairs[0].shape[0] // 2
    half = slots // 2

    def chip_sum(pair):
        return pair[:slots] + swap(pair[slots:].astype(BF16), "c").astype(F32)

    if not wide_team:
        across = swap(chip_sum(pairs[1]).astype(BF16), "x")
        return chip_sum(pairs[0]) + across.astype(F32)
    far = chip_sum(pairs[3]).astype(BF16)
    far_x = swap(far[:half], "x").astype(F32)
    far_y = swap(far[half:], "y").astype(F32)
    to_y = chip_sum(pairs[2])
    to_x = chip_sum(pairs[1])
    to_y = jnp.concatenate([to_y[:half] + far_x, to_y[half:]]).astype(BF16)
    to_x = jnp.concatenate([to_x[:half], to_x[half:] + far_y]).astype(BF16)
    from_x, from_y = swap(to_x, "x"), swap(to_y, "y")
    return chip_sum(pairs[0]) + from_x.astype(F32) + from_y.astype(F32)


def item_segments(length_rows, slot_count):
    item_count = length_rows.shape[1] - 1
    bounds = jnp.cumsum(length_rows[:, :item_count], axis=1, dtype=jnp.int32)
    where_at = jnp.arange(slot_count, dtype=jnp.int32)
    return jnp.sum(
        (where_at[None, :, None] >= bounds[:, None, :]).astype(jnp.int32), axis=2, dtype=jnp.int32
    )


def offset_table(slot_count, model_width):
    offsets = jnp.arange(2 * slot_count - 1, dtype=F32) - (slot_count - 1)
    freqs = jnp.exp(-jnp.log(10000.0) * jnp.arange(0, model_width, 2, dtype=F32) / model_width)
    angles = offsets[:, None] * freqs[None, :]
    return jnp.concatenate([jnp.sin(angles), jnp.cos(angles)], axis=1)


def shift_scores(wide_scores):
    slots = wide_scores.shape[-2]
    lead = wide_scores.shape[:-2]
    padded = jnp.pad(wide_scores, [(0, 0)] * len(lead) + [(0, 0), (0, 1)])
    flat = padded.reshape(lead + (2 * slots * slots,))
    flat = flat[..., slots - 1 : slots - 1 + slots * (2 * slots - 1)]
    return flat.reshape(lead + (slots, 2 * slots - 1))[..., :slots]


def depth_conv(rows, taps, segment, flip):
    slots = rows.shape[1]
    tap_count = taps.shape[0]
    reach = tap_count // 2
    padded = jnp.pad(rows, ((0, 0), (reach, reach), (0, 0)))
    segment_pad = jnp.pad(segment, ((0, 0), (reach, reach)), constant_values=-1)
    total = jnp.zeros_like(rows)
    for k in range(tap_count):
        near = lax.slice_in_dim(padded, k, k + slots, axis=1)
        match = lax.slice_in_dim(segment_pad, k, k + slots, axis=1) == segment
        tap = taps[tap_count - 1 - k] if flip else taps[k]
        total = total + jnp.where(match[:, :, None], near, 0.0) * tap
    return total


def tap_grads(rows, grad, tap_count, segment):
    slots = rows.shape[1]
    reach = tap_count // 2
    padded = jnp.pad(rows, ((0, 0), (reach, reach), (0, 0)))
    segment_pad = jnp.pad(segment, ((0, 0), (reach, reach)), constant_values=-1)
    terms = []
    for k in range(tap_count):
        near = lax.slice_in_dim(padded, k, k + slots, axis=1)
        match = lax.slice_in_dim(segment_pad, k, k + slots, axis=1) == segment
        terms.append(jnp.sum(jnp.where(match[:, :, None], near, 0.0) * grad, axis=(0, 1)))
    return jnp.stack(terms)


def nesterov(weight, moment, average, grad_rows, rate, rate_scale):
    moment_new = MOMENTUM_DECAY * moment + grad_rows
    weight_new = weight - rate * rate_scale * (grad_rows + MOMENTUM_DECAY * moment_new)
    average_new = AVERAGE_DECAY * average + (1.0 - AVERAGE_DECAY) * weight_new
    return (moment_new, weight_new, average_new)


def make_step(planes, sides):
    wide_team = sides == 2
    team_axes = ("x", "c", "y") if wide_team else ("x", "c")
    team = 8 if wide_team else 4
    outer_bits = [("z", 1 << i) for i in range((planes - 1).bit_length())]
    if not wide_team:
        outer_bits += [("y", 1 << i) for i in range((sides - 1).bit_length())]
    head_aligned = wide_team and planes * 4 == HEADS

    def side_rows(rows):
        return rows if wide_team else lax.all_gather(rows, "y", axis=0, tiled=True)

    def side_scatter(rows):
        if wide_team:
            return rows
        return lax.psum_scatter(rows, "y", scatter_dimension=0, tiled=True)

    def split_hidden(rows):
        r, f = rows.shape
        return rows.reshape(r, planes, team, f // (planes * team)).transpose(2, 0, 1, 3).reshape(
            team, r, f // team
        )

    def join_hidden(blocks):
        _, r, f = blocks.shape
        return blocks.reshape(team, r, planes, f // planes).transpose(1, 2, 0, 3).reshape(
            r, team * f
        )

    def split_heads(rows):
        r, d = rows.shape
        if not head_aligned:
            return rows.reshape(r, team, d // team).transpose(1, 0, 2)
        size = d // HEADS
        rows = rows.reshape(r, sides, planes // sides, 2, 2, size)
        return rows.transpose(3, 4, 1, 0, 2, 5).reshape(team, r, d // team)

    def join_heads(blocks):
        _, r, f = blocks.shape
        if not head_aligned:
            return blocks.transpose(1, 0, 2).reshape(r, team * f)
        size = team * f // HEADS
        blocks = blocks.reshape(2, 2, sides, r, planes // sides, size)
        return blocks.transpose(3, 2, 4, 0, 1, 5).reshape(r, team * f)

    def team_swap(blocks):
        return lax.all_to_all(blocks, team_axes, split_axis=0, concat_axis=0, tiled=True)

    def plane_gather(rows):
        return lax.all_gather(rows, "z", axis=0, tiled=False)

    def plane_scatter(rows):
        return lax.psum_scatter(rows, "z", scatter_dimension=0, tiled=False)

    def outer_sum(values):
        for axis, bit in outer_bits:
            values = values + swap(values, axis, bit)
        return values

    def outer_moments(count, mean, spread):
        for axis, bit in outer_bits:
            packed = jnp.stack([count, mean, spread])
            other = swap(packed, axis, bit)
            total = count + other[0]
            gap = other[1] - mean
            spread = spread + other[2] + gap * gap * (count * other[0] / total)
            mean = (count * mean + other[0] * other[1]) / total
            count = total
        return count, mean, spread

    def step(
        frames,
        lengths,
        out_grad,
        up_weight,
        down_weight,
        square_weight,
        chan_weight,
        up_moment,
        down_moment,
        square_moment,
        chan_moment,
        up_average,
        down_average,
        square_average,
        chan_average,
    ):
        slots, width = frames.shape
        head_size = width // HEADS
        team_heads = HEADS // team
        score_scale = head_size ** (-0.5)
        item_count = lengths.shape[1] - 1
        chan_rows = chan_weight.shape[0]
        tap_count = chan_rows - 14
        hidden = up_weight.shape[2]
        team_hidden = hidden // team
        team_width = width // team
        buckets = team
        x_at, c_at, y_at = lax.axis_index("x"), lax.axis_index("c"), lax.axis_index("y")
        team_at = (x_at * 2 + c_at) * 2 + y_at if wide_team else x_at * 2 + c_at

        up_low = up_weight.astype(BF16)
        down_low = down_weight.astype(BF16)
        square_low = square_weight.astype(BF16)
        chan_low = chan_weight.astype(BF16)

        chan_side = chan_low if wide_team else lax.all_gather(chan_low, "y", axis=0)
        chan_flat = chan_side.reshape(-1)
        chan_size = chan_flat.shape[0]
        chan_lines = -(-chan_size // team_hidden)
        chan_flat = jnp.pad(chan_flat, (0, chan_lines * team_hidden - chan_size))
        chan_block = jnp.broadcast_to(
            chan_flat.reshape(1, chan_lines, team_hidden), (team, chan_lines, team_hidden)
        )
        first_up = split_hidden(side_rows(up_low[0]))
        rows_in = first_up.shape[1]
        first = team_swap(jnp.concatenate([first_up, chan_block], axis=1))
        first = jnp.concatenate(
            [
                first[:, :rows_in].reshape(team * rows_in, team_hidden),
                first[:, rows_in:].reshape(team * chan_lines, team_hidden),
            ]
        )
        first = plane_gather(first)
        up_one = first[:, : team * rows_in].reshape(width, team_hidden)
        chan_all = first[:, team * rows_in :].reshape(planes, team, chan_lines * team_hidden)
        chan_all = chan_all[:, :, :chan_size].reshape(
            planes, team, 1 if wide_team else sides, chan_rows, chan_weight.shape[1]
        )
        chan_float = chan_all.transpose(3, 0, 1, 2, 4).reshape(chan_rows, width).astype(F32)

        down_rows = side_rows(down_low[0]).shape[0]
        mix_low, conv_out_low = square_low[3], side_rows(square_low[7])
        conv_rows_in = conv_out_low.shape[0]
        if head_aligned:
            mix_side = lax.all_gather(mix_low, "y", axis=0, tiled=True)
            head_rows = mix_side.shape[0]
            second = plane_gather(jnp.concatenate([side_rows(down_low[0]), mix_side, conv_out_low]))
            mix_all = second[:, down_rows : down_rows + head_rows]
            per_side = planes // sides
            mix_full = lax.dynamic_slice_in_dim(mix_all, y_at * per_side, per_side, axis=0)
            mix_full = mix_full.reshape(team_width, width)
        else:
            head_rows = 0
            second = plane_gather(jnp.concatenate([side_rows(down_low[0]), conv_out_low]))
            mix_all = lax.all_gather(mix_low, ALL, axis=0, tiled=True)
            mix_full = lax.dynamic_slice_in_dim(mix_all, team_at * team_width, team_width, axis=0)
        down_one = second[:, :down_rows].reshape(team_hidden, width)
        conv_out = second[:, down_rows + head_rows :].reshape(team_width, width)

        third = jnp.concatenate(
            [split_heads(side_rows(square_low[i])) for i in (0, 1, 2, 4)]
            + [split_hidden(side_rows(square_low[i])) for i in (5, 6)],
            axis=2,
        )
        third = plane_gather(team_swap(third).reshape(-1, 6 * team_width))
        third = third.reshape(width, 6 * team_width)
        qkv_in = third[:, : 3 * team_width]
        place_in = third[:, 3 * team_width : 4 * team_width]
        gate_in = third[:, 4 * team_width :]

        up_two = plane_gather(
            team_swap(split_hidden(side_rows(up_low[1]))).reshape(-1, team_hidden)
        ).reshape(width, team_hidden)
        down_two = plane_gather(side_rows(down_low[1])).reshape(team_hidden, width)

        def own_hidden(rows):
            rows = rows.reshape(rows.shape[0], planes, team, -1)
            rows = lax.dynamic_index_in_dim(rows, team_at, axis=2, keepdims=False)
            return rows.reshape(rows.shape[0], team_width)

        def own_heads(rows):
            blocks = split_heads(rows)
            return lax.dynamic_index_in_dim(blocks, team_at, axis=0, keepdims=False)

        taps = own_hidden(chan_float[:tap_count])
        batch_rows = own_hidden(chan_float[tap_count + 10 : tap_count + 12])
        batch_gain, batch_shift = batch_rows[0], batch_rows[1]
        bias_rows = own_heads(chan_float[tap_count + 12 : tap_count + 14])
        bias_content, bias_place = bias_rows[0], bias_rows[1]
        gains = [chan_float[tap_count + j] for j in range(5)]
        shifts = [chan_float[tap_count + 5 + j] for j in range(5)]

        team_lengths = jnp.concatenate(team_gather_small(lengths, wide_team))
        segment = item_segments(team_lengths, slots)
        valid_team = (segment < item_count).astype(F32)[:, :, None]
        valid = valid_team[0]

        def gather(values):
            return team_gather(values, wide_team)

        def scatter(pairs):
            return team_scatter(pairs, wide_team)

        def feed_forward(stream, gain, shift, up, down):
            normed = gather(layer_norm(stream, gain, shift).astype(BF16))
            before = [mm(n, up) for n in normed]
            active = [(a * jax.nn.sigmoid(a)).astype(BF16) for a in before]
            branch = scatter([mm(s, down) for s in active])
            return stream + 0.5 * branch, (normed, before, active)

        def feed_backward(grad_stream, stream, gain, up, down, saved):
            normed, before, active = saved
            grads = gather((0.5 * grad_stream).astype(BF16))
            grad_before = [
                (mm_nt(g, down) * swish_grad(a)).astype(BF16) for g, a in zip(grads, before)
            ]
            grad_normed = scatter([mm_nt(g, up) for g in grad_before])
            down_term = mm_tn(jnp.concatenate(active), jnp.concatenate(grads))
            up_term = mm_tn(jnp.concatenate(normed), jnp.concatenate(grad_before))
            grad_in, gain_term, shift_term = layer_norm_back(stream, gain, grad_normed)
            return grad_stream + grad_in, up_term, down_term, gain_term, shift_term

        stream_zero = frames.astype(F32)
        stream_one, saved_one = feed_forward(stream_zero, gains[0], shifts[0], up_one, down_one)

        normed_two = gather(layer_norm(stream_one, gains[1], shifts[1]).astype(BF16))
        normed_two = jnp.concatenate(normed_two)
        qkv = mm(normed_two, qkv_in)
        query = qkv[:, :team_width]

        def to_heads(rows):
            return rows.reshape(-1, slots, team_heads, head_size).transpose(0, 2, 1, 3)

        def from_heads(rows):
            return rows.transpose(0, 2, 1, 3).reshape(-1, team_width)

        query_c = to_heads((query + bias_content).astype(BF16))
        query_p = to_heads((query + bias_place).astype(BF16))
        key = to_heads(qkv[:, team_width : 2 * team_width].astype(BF16))
        value = to_heads(qkv[:, 2 * team_width :].astype(BF16))
        table = offset_table(slots, width).astype(BF16)
        place = mm(table, place_in).astype(BF16).reshape(-1, team_heads, head_size)

        wide_scores = jnp.einsum("bhid,ohd->bhio", query_p, place, preferred_element_type=F32)
        content = jnp.einsum("bhid,bhjd->bhij", query_c, key, preferred_element_type=F32)
        scores = (content + shift_scores(wide_scores)) * score_scale
        same = segment[:, :, None] == segment[:, None, :]
        scores = jnp.where(same[:, None], scores, MASKED_SCORE)
        probs = jax.nn.softmax(scores, axis=-1)
        probs_low = probs.astype(BF16)
        mixed = jnp.einsum("bhij,bhjd->bhid", probs_low, value, preferred_element_type=F32)
        mixed = from_heads(mixed.astype(BF16))
        pair_rows = 2 * slots
        pair_count = team // 2

        def in_pairs(rows):
            return [rows[p * pair_rows : (p + 1) * pair_rows] for p in range(pair_count)]

        stream_two = stream_one + scatter([mm(m, mix_full) for m in in_pairs(mixed)])

        normed_three = gather(layer_norm(stream_two, gains[2], shifts[2]).astype(BF16))
        normed_three = jnp.concatenate(normed_three)
        gates = mm(normed_three, gate_in).reshape(buckets, slots, 2 * team_width)
        gate_a, gate_b = gates[:, :, :team_width], gates[:, :, team_width:]
        gate_sig = jax.nn.sigmoid(gate_b)
        glu = gate_a * gate_sig * valid_team
        conv = depth_conv(glu, taps, segment, False)
        local_count = jnp.sum(valid_team)
        local_mean = jnp.sum(conv * valid_team, axis=(0, 1)) / local_count
        local_gap = (conv - local_mean) * valid_team
        local_spread = jnp.sum(local_gap * local_gap, axis=(0, 1))
        count_row, mean, spread = outer_moments(
            jnp.broadcast_to(local_count, local_mean.shape), local_mean, local_spread
        )
        frame_count = count_row[0]
        spread_inv = lax.rsqrt(spread / frame_count + EPSILON)
        unit = (conv - mean) * spread_inv
        batch_normed = unit * batch_gain + batch_shift
        active_conv = (batch_normed * jax.nn.sigmoid(batch_normed)).astype(BF16)
        active_conv = active_conv.reshape(-1, team_width)
        stream_three = stream_two + scatter([mm(s, conv_out) for s in in_pairs(active_conv)])

        stream_four, saved_four = feed_forward(
            stream_three, gains[3], shifts[3], up_two, down_two
        )
        output = (layer_norm(stream_four, gains[4], shifts[4]) * valid).astype(BF16)

        grad_final = out_grad.astype(F32) * valid
        grad_four, gain_four, shift_four = layer_norm_back(stream_four, gains[4], grad_final)
        grad_three, up_second, down_second, gain_three, shift_three = feed_backward(
            grad_four, stream_three, gains[3], up_two, down_two, saved_four
        )
        down_second = plane_scatter(down_second.astype(BF16).reshape(planes, -1, width))
        up_second = plane_scatter(up_second.astype(BF16).reshape(planes, -1, team_hidden))

        grads = jnp.concatenate(gather(grad_three.astype(BF16)))
        conv_out_term = mm_tn(active_conv, grads)
        grad_active = mm_nt(grads, conv_out).reshape(buckets, slots, team_width)
        grad_batch = grad_active * swish_grad(batch_normed)
        batch_gain_term = jnp.sum(grad_batch * unit, axis=(0, 1))
        batch_shift_term = jnp.sum(grad_batch, axis=(0, 1))
        grad_unit = grad_batch * batch_gain
        sums = outer_sum(
            jnp.stack(
                [
                    jnp.sum(grad_unit * valid_team, axis=(0, 1)),
                    jnp.sum(grad_unit * unit * valid_team, axis=(0, 1)),
                ]
            )
        )
        grad_conv = (
            valid_team
            * spread_inv
            * (grad_unit - sums[0] / frame_count - unit * (sums[1] / frame_count))
        )
        tap_term = tap_grads(glu, grad_conv, tap_count, segment)
        grad_glu = depth_conv(grad_conv, taps, segment, True) * valid_team
        grad_a = (grad_glu * gate_sig).astype(BF16)
        grad_b = (grad_glu * gate_a * gate_sig * (1.0 - gate_sig)).astype(BF16)
        grad_gates = jnp.concatenate([grad_a, grad_b], axis=2).reshape(-1, 2 * team_width)
        gate_term = mm_tn(normed_three, grad_gates)
        grad_normed = scatter([mm_nt(g, gate_in) for g in in_pairs(grad_gates)])
        grad_in, gain_two, shift_two = layer_norm_back(stream_two, gains[2], grad_normed)
        grad_two = grad_three + grad_in

        grads = jnp.concatenate(gather(grad_two.astype(BF16)))
        mix_term = mm_tn(mixed, grads)
        grad_mixed = to_heads(mm_nt(grads, mix_full).astype(BF16))
        grad_probs = jnp.einsum("bhid,bhjd->bhij", grad_mixed, value, preferred_element_type=F32)
        grad_value = jnp.einsum(
            "bhij,bhid->bhjd", probs_low, grad_mixed, preferred_element_type=F32
        )
        grad_scores = probs * (
            grad_probs - jnp.sum(probs * grad_probs, axis=-1, keepdims=True)
        )
        grad_scaled = grad_scores.astype(BF16) * score_scale
        grad_qc = jnp.einsum("bhij,bhjd->bhid", grad_scaled, key, preferred_element_type=F32)
        grad_key = jnp.einsum("bhij,bhid->bhjd", grad_scaled, query_c, preferred_element_type=F32)
        _, shift_pull = jax.vjp(shift_scores, wide_scores)
        grad_wide = shift_pull(grad_scaled.astype(F32))[0].astype(BF16)
        grad_qp = jnp.einsum("bhio,ohd->bhid", grad_wide, place, preferred_element_type=F32)
        grad_place = jnp.einsum("bhio,bhid->ohd", grad_wide, query_p, preferred_element_type=F32)
        place_term = mm_tn(table, grad_place.reshape(-1, team_width).astype(BF16))
        bias_content_term = jnp.sum(grad_qc, axis=(0, 2)).reshape(team_width)
        bias_place_term = jnp.sum(grad_qp, axis=(0, 2)).reshape(team_width)
        grad_qkv = jnp.concatenate(
            [
                from_heads((grad_qc + grad_qp).astype(BF16)),
                from_heads(grad_key.astype(BF16)),
                from_heads(grad_value.astype(BF16)),
            ],
            axis=1,
        )
        qkv_term = mm_tn(normed_two, grad_qkv)
        grad_normed = scatter([mm_nt(g, qkv_in) for g in in_pairs(grad_qkv)])
        grad_in, gain_one, shift_one = layer_norm_back(stream_one, gains[1], grad_normed)
        grad_one = grad_two + grad_in

        mix_term = mix_term.astype(BF16)
        conv_out_term = conv_out_term.astype(BF16).reshape(planes, -1, width)
        if head_aligned:
            per_side = planes // sides
            spread_rows = jnp.zeros((planes, head_rows, width), BF16)
            spread_rows = lax.dynamic_update_slice_in_dim(
                spread_rows, mix_term.reshape(per_side, head_rows, width), y_at * per_side, axis=0
            )
            rows_term = plane_scatter(jnp.concatenate([spread_rows, conv_out_term], axis=1))
            mix_own = rows_term[:head_rows]
            mix_own = mix_own.astype(F32) + swap(mix_own, "y").astype(F32)
            per_device = head_rows // sides
            mix_grad = lax.dynamic_slice_in_dim(mix_own, y_at * per_device, per_device, axis=0)
            conv_out_grad = rows_term[head_rows:].astype(F32)
        else:
            spread_rows = jnp.zeros((width, width), BF16)
            spread_rows = lax.dynamic_update_slice_in_dim(
                spread_rows, mix_term, team_at * team_width, axis=0
            )
            mix_grad = lax.psum_scatter(spread_rows, ALL, scatter_dimension=0, tiled=True)
            mix_grad = mix_grad.astype(F32)
            conv_out_grad = side_scatter(plane_scatter(conv_out_term)).astype(F32)
        columns_term = jnp.concatenate([qkv_term, place_term, gate_term], axis=1).astype(BF16)
        columns_term = plane_scatter(columns_term.reshape(planes, -1, 6 * team_width))

        grad_zero, up_first, down_first, gain_zero, shift_zero = feed_backward(
            grad_one, stream_zero, gains[0], up_one, down_one, saved_one
        )
        frames_grad = grad_zero.astype(BF16)
        down_first = plane_scatter(down_first.astype(BF16).reshape(planes, -1, width))
        up_first = plane_scatter(up_first.astype(BF16).reshape(planes, -1, team_hidden))

        def from_team(rows, columns):
            return team_swap(rows.reshape(team, -1, columns))

        up_grad = jnp.stack(
            [
                side_scatter(join_hidden(from_team(rows, team_hidden))).astype(F32)
                for rows in (up_first, up_second)
            ]
        )
        down_grad = jnp.stack(
            [side_scatter(down_first).astype(F32), side_scatter(down_second).astype(F32)]
        )
        blocks = from_team(columns_term, 6 * team_width)

        def block(i):
            return blocks[:, :, i * team_width : (i + 1) * team_width]

        square_grad = jnp.stack(
            [side_scatter(join_heads(block(i))).astype(F32) for i in range(3)]
            + [mix_grad, side_scatter(join_heads(block(3))).astype(F32)]
            + [side_scatter(join_hidden(block(i))).astype(F32) for i in (4, 5)]
            + [conv_out_grad]
        )

        zero_blocks = jnp.zeros((team, 2, team_width), F32)
        bias_terms = join_heads(
            lax.dynamic_update_slice_in_dim(
                zero_blocks,
                jnp.stack([bias_content_term, bias_place_term])[None],
                team_at,
                axis=0,
            )
        )
        feature_terms = jnp.concatenate(
            [
                jnp.stack(
                    [
                        gain_zero,
                        gain_one,
                        gain_two,
                        gain_three,
                        gain_four,
                        shift_zero,
                        shift_one,
                        shift_two,
                        shift_three,
                        shift_four,
                    ]
                ),
                bias_terms,
            ]
        )
        feature_terms = jnp.sum(team_swap(split_hidden(feature_terms)), axis=0)
        chan_term = jnp.concatenate(
            [
                tap_term,
                feature_terms[:10],
                jnp.stack([batch_gain_term, batch_shift_term]),
                feature_terms[10:],
            ]
        )
        chan_term = outer_sum(chan_term).reshape(chan_rows, planes, -1)
        chan_term = lax.dynamic_index_in_dim(chan_term, lax.axis_index("z"), 1, keepdims=False)
        if not wide_team:
            chan_term = lax.dynamic_index_in_dim(
                chan_term.reshape(chan_rows, sides, -1), y_at, 1, keepdims=False
            )
        chan_grad = chan_term

        rate_scale = lax.rsqrt(frame_count)
        up_new = nesterov(up_weight, up_moment, up_average, up_grad, RATE_UP, rate_scale)
        down_new = nesterov(down_weight, down_moment, down_average, down_grad, RATE_DOWN, rate_scale)
        square_new = nesterov(
            square_weight, square_moment, square_average, square_grad, RATE_SQUARE, rate_scale
        )
        chan_new = nesterov(
            chan_weight, chan_moment, chan_average, chan_grad, RATE_CHANNEL, rate_scale
        )
        bias_grad = chan_grad[tap_count + 12 : tap_count + 14]
        return (
            output,
            frames_grad,
            up_grad,
            down_grad,
            square_grad,
            chan_grad,
            up_new[0],
            down_new[0],
            square_new[0],
            chan_new[0],
            up_new[1],
            down_new[1],
            square_new[1],
            chan_new[1],
            up_new[2],
            down_new[2],
            square_new[2],
            chan_new[2],
            bias_grad,
        )

    return step


def solution(mesh):
    wide, narrow = mesh.shape["wide"], mesh.shape["narrow"]
    planes = wide // 4
    inner = Mesh(mesh.devices.reshape(planes, 2, 2, narrow), ALL)
    token = P(ALL, None)
    matrix = P(None, ALL, None)
    vector = P(None, ALL)
    group = (matrix, matrix, matrix, vector)
    return jax.shard_map(
        make_step(planes, narrow),
        mesh=inner,
        in_specs=(token, token, token) + group * 3,
        out_specs=(token, token) + group * 4 + (vector,),
        check_vma=False,
    )
```

time: 2910 us -> 757 us (0.26)
  waiting for transfers between devices: 2430 us -> 140 us
  local copies, waits for them, and re-layouts: 43.7 us -> 236 us
  blocking collectives: 193 us -> 20.9 us
  starting transfers between devices: 0.67 us -> 126 us
  matrix products: 138 us -> 95.8 us
    reduce_scatter x3 -> x6, waiting for transfers between devices: 2110 us -> 0.07 us  [plane_scatter(): return lax.psum_scatter(rows, 'z', scatter_dimension=0, tiled=False)]
    all_gather x3 -> x5, waiting for transfers between devices: 243 us -> 43.1 us  [plane_gather(): return lax.all_gather(rows, 'z', axis=0, tiled=False)]
    psum x3 -> x0, blocking collectives: 120 us -> none  [the longest x1 41.1 us: shards(): lax.psum(jnp.sum(centred * centred, axis=0), ('wide', 'narrow'))]
    ppermute x0 -> x138, starting transfers between devices: none -> 102 us  [swap(): return lax.ppermute(values, axis, [(i, i ^ bit) for i in range(size)])]
    ppermute x0 -> x138, waiting for transfers between devices: none -> 86.2 us  [swap(): return lax.ppermute(values, axis, [(i, i ^ bit) for i in range(size)])]
    unnamed x8 -> x11, waiting for transfers between devices: 72.3 us -> 0.18 us
    all_gather x1, blocking collectives: 73.2 us -> 8.59 us  [step(): mix_side = lax.all_gather(mix_low, 'y', axis=0, tiled=True)]
    unnamed x394 -> x597, local copies, waits for them, and re-layouts: 12 us -> 71.1 us
  transfers between devices with their start and end apart: 7 -> 155, of which waited for: 7 -> 55; matrix products, arithmetic and copies ran while one was open for 4% -> 47% of each run, Pallas kernels for 0% -> 0%
where the time goes in v1:
time: 757 us; the launch traced here: 748 us
  local copies, waits for them, and re-layouts  236 us (31%)
  waiting for transfers between devices  140 us (18%)
  starting transfers between devices  126 us (17%)
  other arithmetic  110 us (15%)
  matrix products  95.8 us (13%)
  blocking collectives  20.9 us (3%)
  between operations  19.9 us (3%)
    ppermute x138, starting transfers between devices, swap(): return lax.ppermute(values, axis, [(i, i ^ bit) for i in range(size)])  102 us
    ppermute x138, waiting for transfers between devices, swap(): return lax.ppermute(values, axis, [(i, i ^ bit) for i in range(size)])  86.2 us
    unnamed x597, local copies, waits for them, and re-layouts  71.1 us
    all_gather x5, waiting for transfers between devices, plane_gather(): return lax.all_gather(rows, 'z', axis=0, tiled=False)  43.1 us
    mul x31, local copies, waits for them, and re-layouts, depth_conv(): total = total + jnp.where(match[:, :, None], near, 0.0) * tap  39.6 us
    dot_general x27, matrix products, mm(): return jnp.dot(left, right, preferred_element_type=F32)  29.3 us
    all_to_all x6, starting transfers between devices, team_swap(): lax.all_to_all(blocks, team_axes, split_axis=0, concat_axis=0, tiled=True)  22.6 us
    dot_general x26, matrix products, mm_nt(): lax.dot_general(left, right, (((1,), (1,)), ((), ())), preferred_element_...  22.6 us
  transfers between devices with their start and end apart: 155, of which 55 were waited for; matrix products, arithmetic and copies ran while one was open for 47% of the time, Pallas kernels for 0%

profile of v1, /device:TPU:0, one launch (start us, length us, event | category | flops | bytes accessed | tf_op | source)
XLA Modules:
  0.0 747.7 jit_solution(1208054574391312562)
XLA Ops:
  10.5 12.3 %all_to_all.35 = bf16[8,35,512]{2,1,0:T(8,128)(2,1)S(1)} all-to-all(bf16[8,35,512]{2,1,0:T(8,128)(2,1)S(1)} %pad_maximum_fusion.5), channel_id=1, replica_groups=mesh['z'=4,'x'=2,'c'=2,'y'=2] {'x','c','y'}, dimensions={0} | all-to-all | bytes 573440 | tf_op jit(solution)/shard_map/all_to_all | solution.py:215
  33.9 8.6 %all-gather.1 = bf16[1,64,1024]{2,1,0:T(8,128)(2,1)S(1)} all-gather(bf16[1,32,1024]{2,1,0:T(8,128)(2,1)S(1)} %get-tuple-element.191), channel_id=3, replica_groups=mesh['z'=4,'x'=2,'c'=2,'y'=2] {'y'}, dimensions={1}, use_global_device_ids=true | all-gather | bytes 196608 | tf_op jit(solution)/shard_map/all_gather | solution.py:304
  76.4 19.7 %all-gather.17.cloned.1.call-done = bf16[896,1024]{1,0:T(8,128)(2,1)} async-done(((bf16[224,1024]{1,0:T(8,128)(2,1)}), bf16[896,1024]{1,0:T(8,128)(2,1)}) %all-gather.17.cloned.1.call-update) | async-done | bytes 1835024 | tf_op jit(solution)/shard_map/all_gather | solution.py:218
  123.0 11.3 %all-gather.9.cloned.1.call-done = bf16[4,256,768]{2,1,0:T(8,128)(2,1)} async-done(((bf16[1,256,768]{2,1,0:T(8,128)(2,1)}), bf16[4,256,768]{2,1,0:T(8,128)(2,1)}) %all-gather.9.cloned.1.call-update) | async-done | bytes 1572880 | tf_op jit(solution)/shard_map/all_gather | solution.py:218
  180.2 6.2 reshape.867
  282.8 6.2 multiply_reduce_fusion.46
  294.9 4.0 all-to-all-start.2
  318.7 4.8 collective-permute-done.51
  337.1 4.6 collective-permute-done.59
  349.4 12.1 %all-gather.13.cloned.1.call-done = bf16[4,128,1024]{2,1,0:T(8,128)(2,1)} async-done(((bf16[1,128,1024]{2,1,0:T(8,128)(2,1)}), bf16[4,128,1024]{2,1,0:T(8,128)(2,1)}) %all-gather.13.cloned.1.call-update) | async-done | bytes 1048592 | tf_op jit(solution)/shard_map/all_gather | solution.py:218
  399.5 4.3 copy.275
  464.4 5.7 multiply_reduce_fusion.6
  470.1 8.0 %multiply_convert_fusion.1 = (bf16[8,128,128]{2,1,0:T(8,128)(2,1)S(1)}, f32[8,128,128]{2,1,0:T(8,128)S(1)}) fusion(f32[8,128,256]{2,1,0:T(8,128)S(1)} %bitcast.543, f32[8,128]{1,0:T(8,128)S(1)} %get-tuple-element.242, f32[128]{0:T(128)} %mul.1368, pred[8,128]{1,0:T(8,128)(4,1)} %get-tuple-element.254, f32[128]{0:T(128)} %mul.1371, ...), kind=kLoop, calls=%fused_computation.512 | loop fusion | flops 13107200 | bytes 2409984 | tf_op jit(solution)/shard_map/convert_element_type | solution.py:478
  491.5 3.7 collective-permute-done.99
  544.8 3.8 reshape.876
  553.2 3.9 fusion.288
  598.2 3.9 convolution_convert_fusion
  612.8 4.1 collective-permute-done.117
  623.4 4.1 all-to-all-start.4
  689.4 4.0 all-to-all-done.6
  693.5 3.7 concatenate.323
  714.1 3.7 multiply_add_fusion.1
  721.4 4.2 all-to-all-start.3
  732.1 3.8 multiply_add_fusion
  (1398 shorter events, 577.0 us)
Async XLA Ops:
  7.2 48.3 %all-gather.15.cloned.1.call-start = ((), (), s32[]{:S(2)}) async-start(), calls=%async_computation.22 | async-start | bytes 1433600 | tf_op jit(solution)/shard_map/all_gather | solution.py:218
  23.7 24.3 %collective-permute-start.16 = (s32[1,4]{1,0:T(1,128)S(1)}, s32[1,4]{1,0:T(1,128)S(1)}, u32[]{:S(2)}, u32[]{:S(2)}) collective-permute-start(s32[1,4]{1,0:T(1,128)S(1)} %copy-done.227), channel_id=1, source_target_pairs={{0,2},{2,0},{1,3},{3,1},{4,6},{6,4},{5,7},{7,5},{8,10},{10,8},{9,1... | collective-permute-start | bytes 56 | tf_op jit(solution)/shard_map/ppermute | solution.py:35
  30.3 31.4 %all-to-all-start.1 = ((bf16[8,32,768]{2,1,0:T(8,128)(2,1)}), bf16[8,32,768]{2,1,0:T(8,128)(2,1)S(1)}, u32[]{:S(2)}, u32[]{:S(2)}) async-start(bf16[8,32,768]{2,1,0:T(8,128)(2,1)} %constant_dynamic-update-slice_fusion.9), calls=%async_computation.1 | async-start | bytes 786432 | tf_op jit(solution)/shard_map/all_to_all | solution.py:215
  33.8 62.4 %all-gather.17.cloned.1.call-start = ((), (), s32[]{:S(2)}) async-start(), calls=%async_computation.23 | async-start | bytes 2293760 | tf_op jit(solution)/shard_map/all_gather | solution.py:218
  44.1 90.2 %all-gather.9.cloned.1.call-start = ((), (), s32[]{:S(2)}) async-start(), calls=%async_computation.13 | async-start | bytes 1966080 | tf_op jit(solution)/shard_map/all_gather | solution.py:218
  123.0 20.0 %collective-permute-start.19 = (bf16[128,1024]{1,0:T(8,128)(2,1)}, bf16[128,1024]{1,0:T(8,128)(2,1)}, u32[]{:S(2)}, u32[]{:S(2)}) collective-permute-start(bf16[128,1024]{1,0:T(8,128)(2,1)} %get-tuple-element.166), channel_id=1, source_target_pairs={{0,2},{2,0},{1,3},{3,1},{4,6},{6,4},{5,7},{7,5},{8,10},{10,8},{9,1... | collective-permute-start | bytes 786440 | tf_op jit(solution)/shard_map/ppermute | solution.py:35
  221.7 46.3 %collective-permute-start.38 = (bf16[128,1024]{1,0:T(8,128)(2,1)}, bf16[128,1024]{1,0:T(8,128)(2,1)S(1)}, u32[]{:S(2)}, u32[]{:S(2)}) collective-permute-start(bf16[128,1024]{1,0:T(8,128)(2,1)} %get-tuple-element.162), channel_id=1, source_target_pairs={{0,1},{1,0},{2,3},{3,2},{4,5},{5,4},{6,7},{7,6},{8,9},{9,8},{10,11... | collective-permute-start | bytes 786440 | tf_op jit(solution)/shard_map/ppermute | solution.py:35
  223.2 45.4 %collective-permute-start.36 = (bf16[128,1024]{1,0:T(8,128)(2,1)}, bf16[128,1024]{1,0:T(8,128)(2,1)S(1)}, u32[]{:S(2)}, u32[]{:S(2)}) collective-permute-start(bf16[128,1024]{1,0:T(8,128)(2,1)} %get-tuple-element.162), channel_id=1, source_target_pairs={{0,4},{4,0},{1,5},{5,1},{2,6},{6,2},{3,7},{7,3},{8,12},{12,8},{9,1... | collective-permute-start | bytes 786440 | tf_op jit(solution)/shard_map/ppermute | solution.py:35
  224.7 45.1 %collective-permute-start.35 = (bf16[128,1024]{1,0:T(8,128)(2,1)}, bf16[128,1024]{1,0:T(8,128)(2,1)}, u32[]{:S(2)}, u32[]{:S(2)}) collective-permute-start(bf16[128,1024]{1,0:T(8,128)(2,1)} %get-tuple-element.162), channel_id=1, source_target_pairs={{0,2},{2,0},{1,3},{3,1},{4,6},{6,4},{5,7},{7,5},{8,10},{10,8},{9,1... | collective-permute-start | bytes 786440 | tf_op jit(solution)/shard_map/ppermute | solution.py:35
  298.9 47.7 %all-gather.11.cloned.1.call-start = ((), (), s32[]{:S(2)}) async-start(), calls=%async_computation.14 | async-start | bytes 1310720 | tf_op jit(solution)/shard_map/all_gather | solution.py:218
  305.0 56.5 %all-gather.13.cloned.1.call-start = ((), (), s32[]{:S(2)}) async-start(), calls=%async_computation.15 | async-start | bytes 1310720 | tf_op jit(solution)/shard_map/all_gather | solution.py:218
  326.2 297.2 %reduce-scatter.9.cloned.1.call-start = ((), (), s32[]{:S(2)}) async-start(), calls=%async_computation.17 | async-start | bytes 1310720 | tf_op jit(solution)/shard_map/reduce_scatter | solution.py:221
  343.1 21.5 %collective-permute-start.60 = (bf16[64,1024]{1,0:T(8,128)(2,1)}, bf16[64,1024]{1,0:T(8,128)(2,1)}, u32[]{:S(2)}, u32[]{:S(2)}) collective-permute-start(bf16[64,1024]{1,0:T(8,128)(2,1)} %slice.1795), channel_id=1, source_target_pairs={{0,4},{4,0},{1,5},{5,1},{2,6},{6,2},{3,7},{7,3},{8,12},{12,8},{9,1... | collective-permute-start | bytes 393224 | tf_op jit(solution)/shard_map/ppermute | solution.py:35
  345.9 18.7 %collective-permute-start.58 = (bf16[64,1024]{1,0:T(8,128)(2,1)}, bf16[64,1024]{1,0:T(8,128)(2,1)}, u32[]{:S(2)}, u32[]{:S(2)}) collective-permute-start(bf16[64,1024]{1,0:T(8,128)(2,1)} %slice.1794), channel_id=1, source_target_pairs={{0,1},{1,0},{2,3},{3,2},{4,5},{5,4},{6,7},{7,6},{8,9},{9,8},{10,11... | collective-permute-start | bytes 393224 | tf_op jit(solution)/shard_map/ppermute | solution.py:35
  346.6 19.1 %collective-permute-start.56 = (bf16[128,1024]{1,0:T(8,128)(2,1)}, bf16[128,1024]{1,0:T(8,128)(2,1)}, u32[]{:S(2)}, u32[]{:S(2)}) collective-permute-start(bf16[128,1024]{1,0:T(8,128)(2,1)} %collective-permute-done.55), channel_id=1, source_target_pairs={{0,2},{2,0},{1,3},{3,1},{4,6},{6,4},{5,7},{7,5},{8,10},{10,8},{9,1... | collective-permute-start | bytes 786440 | tf_op jit(solution)/shard_map/ppermute | solution.py:35
  364.1 24.2 %collective-permute-start.54 = (bf16[128,1024]{1,0:T(8,128)(2,1)}, bf16[128,1024]{1,0:T(8,128)(2,1)}, u32[]{:S(2)}, u32[]{:S(2)}) collective-permute-start(bf16[128,1024]{1,0:T(8,128)(2,1)} %slice.2843), channel_id=1, source_target_pairs={{0,2},{2,0},{1,3},{3,1},{4,6},{6,4},{5,7},{7,5},{8,10},{10,8},{9,1... | collective-permute-start | bytes 786440 | tf_op jit(solution)/shard_map/ppermute | solution.py:35
  412.1 20.0 %collective-permute-start.70 = (bf16[128,1024]{1,0:T(8,128)(2,1)S(1)}, bf16[128,1024]{1,0:T(8,128)(2,1)S(1)}, u32[]{:S(2)}, u32[]{:S(2)}) collective-permute-start(bf16[128,1024]{1,0:T(8,128)(2,1)S(1)} %slice.2839), channel_id=1, source_target_pairs={{0,2},{2,0},{1,3},{3,1},{4,6},{6,4},{5,7},{7,5},{8,10},{10,8},{9,1... | collective-permute-start | bytes 786440 | tf_op jit(solution)/shard_map/ppermute | solution.py:35
  463.3 211.1 %reduce-scatter.17.cloned.1.call-start = ((), (), s32[]{:S(2)}) async-start(), calls=%async_computation.21 | async-start | bytes 983040 | tf_op jit(solution)/shard_map/reduce_scatter | solution.py:221
  562.2 148.3 %reduce-scatter.15.cloned.1.call-start = ((), (), s32[]{:S(2)}) async-start(), calls=%async_computation.20 | async-start | bytes 1966080 | tf_op jit(solution)/shard_map/reduce_scatter | solution.py:221
  575.6 138.5 %reduce-scatter.13.cloned.1.call-start = ((), (), s32[]{:S(2)}) async-start(), calls=%async_computation.19 | async-start | bytes 1310720 | tf_op jit(solution)/shard_map/reduce_scatter | solution.py:221
  627.5 86.6 %reduce-scatter.11.cloned.1.call-start = ((), (), s32[]{:S(2)}) async-start(), calls=%async_computation.18 | async-start | bytes 1310720 | tf_op jit(solution)/shard_map/reduce_scatter | solution.py:221
  647.7 29.7 %collective-permute-start.120 = (bf16[128,1024]{1,0:T(8,128)(2,1)}, bf16[128,1024]{1,0:T(8,128)(2,1)}, u32[]{:S(2)}, u32[]{:S(2)}) collective-permute-start(bf16[128,1024]{1,0:T(8,128)(2,1)} %slice.2827), channel_id=1, source_target_pairs={{0,2},{2,0},{1,3},{3,1},{4,6},{6,4},{5,7},{7,5},{8,10},{10,8},{9,1... | collective-permute-start | bytes 786440 | tf_op jit(solution)/shard_map/ppermute | solution.py:35
  660.7 57.2 %reduce-scatter.7.cloned.1.call-start = ((), (), s32[]{:S(2)}) async-start(), calls=%async_computation.16 | async-start | bytes 1310720 | tf_op jit(solution)/shard_map/reduce_scatter | solution.py:221
  676.0 54.2 %collective-permute-start.135 = (bf16[64,1024]{1,0:T(8,128)(2,1)}, bf16[64,1024]{1,0:T(8,128)(2,1)}, u32[]{:S(2)}, u32[]{:S(2)}) collective-permute-start(bf16[64,1024]{1,0:T(8,128)(2,1)} %slice_bitcast_fusion.3), channel_id=1, source_target_pairs={{0,1},{1,0},{2,3},{3,2},{4,5},{5,4},{6,7},{7,6},{8,9},{9,8},{10,11... | collective-permute-start | bytes 393224 | tf_op jit(solution)/shard_map/ppermute | solution.py:35
  (385 other events, 2773.6 us)
Sparse Core Ops, SparseCore 0:
  23.8 29.2 all-gather.14
  55.2 40.8 all-gather.16
  98.3 35.9 all-gather.8
  305.1 26.8 all-gather.10
  334.0 27.4 all-gather.12
  463.4 26.0 reduce-scatter.8
  562.4 22.4 reduce-scatter.16
  587.2 34.5 reduce-scatter.14
  624.8 26.1 reduce-scatter.12
  660.8 26.6 reduce-scatter.10
  690.5 26.8 reduce-scatter.6

commit v2 on v1

v2 whole, which is shorter than its diff:
```python
import functools

import jax
import jax.numpy as jnp
from jax import lax
from jax.experimental import pallas as pl
from jax.experimental.pallas import tpu as pltpu
from jax.sharding import Mesh
from jax.sharding import PartitionSpec as P

HEADS = 16
EPSILON = 1e-05
MOMENTUM_DECAY = 0.9
AVERAGE_DECAY = 0.9
RATE_UP = 0.05
RATE_DOWN = 0.026
RATE_SQUARE = 0.05
RATE_CHANNEL = 0.5
MASKED_SCORE = -1e30
BF16 = jnp.bfloat16
F32 = jnp.float32
ALL = ("z", "x", "c", "y")
LANES = 128
PAD = 16
BLOCK = 256
CARRY = 16
ROOM = 6 << 20


def mm(left, right):
    return jnp.dot(left, right, preferred_element_type=F32)


def mm_tn(left, right):
    return lax.dot_general(left, right, (((0,), (0,)), ((), ())), preferred_element_type=F32)


def mm_nt(left, right):
    return lax.dot_general(left, right, (((1,), (1,)), ((), ())), preferred_element_type=F32)


def swap(values, axis, bit=1):
    size = lax.axis_size(axis)
    return lax.ppermute(values, axis, [(i, i ^ bit) for i in range(size)])


def sigmoid(values):
    return 1.0 / (1.0 + jnp.exp(-values))


def swish_grad(values):
    sig = sigmoid(values)
    return sig * (1.0 + values * (1.0 - sig))


def normalize(values):
    centre = values - jnp.mean(values, axis=-1, keepdims=True)
    scale = lax.rsqrt(jnp.mean(centre * centre, axis=-1, keepdims=True) + EPSILON)
    return centre * scale, scale


def shape(dims, dtype):
    return jax.ShapeDtypeStruct(tuple(dims), dtype)


def size_of(item):
    total = 1
    for n in item.shape:
        total *= n
    return total * item.dtype.itemsize


def kernel_call(body, outs, args, scalars=(), flops=0, scratch=()):
    moved = sum(size_of(a) for a in args) + sum(size_of(o) for o in outs)
    return pl.pallas_call(
        body,
        out_shape=tuple(outs),
        in_specs=[pl.BlockSpec(memory_space=pltpu.SMEM)] * len(scalars)
        + [pl.BlockSpec(memory_space=pltpu.VMEM)] * len(args),
        out_specs=tuple(pl.BlockSpec(memory_space=pltpu.VMEM) for _ in outs),
        scratch_shapes=list(scratch),
        compiler_params=pltpu.CompilerParams(vmem_limit_bytes=moved + ROOM),
        cost_estimate=pl.CostEstimate(flops=int(flops), bytes_accessed=moved, transcendentals=0),
    )(*scalars, *args)


def store_partial(mine_refs, mate_ref, i, slots, value):
    mine_refs[i][...] = value[:slots]
    mate_ref[i] = value[slots:].astype(BF16)


def up_product(rows, ref):
    planes = ref.shape[0]
    depth = rows.shape[1] // planes
    total = mm(rows[:, :depth], ref[0, :depth, :])
    for p in range(1, planes):
        total = total + mm(rows[:, p * depth : (p + 1) * depth], ref[p, :depth, :])
    return total


def up_product_back(rows, ref, width):
    planes = ref.shape[0]
    depth = width // planes
    return jnp.concatenate([mm_nt(rows, ref[p, :depth, :]) for p in range(planes)], axis=1)


def down_blocks(ref, width):
    planes, hidden = ref.shape[0], ref.shape[2]
    depth, rows = width // planes, hidden // planes
    return [
        jnp.concatenate(
            [ref[p, depth + b * rows : depth + (b + 1) * rows, :] for p in range(planes)]
        )
        for b in range(width // hidden)
    ]


def down_product(rows, blocks):
    return jnp.concatenate([mm(rows, block) for block in blocks], axis=1)


def down_product_back(rows, blocks):
    size = blocks[0].shape[1]
    total = mm_nt(rows[:, :size], blocks[0])
    for b in range(1, len(blocks)):
        total = total + mm_nt(rows[:, b * size : (b + 1) * size], blocks[b])
    return total


def square_columns(ref, p, depth, first, last):
    parts = []
    while first < last:
        block = first // BLOCK
        stop = min(last, (block + 1) * BLOCK)
        lanes = slice(first - block * BLOCK, stop - block * BLOCK)
        parts.append(ref[p, block * depth : (block + 1) * depth, lanes])
        first = stop
    return jnp.concatenate(parts, axis=1) if len(parts) > 1 else parts[0]


def square_product(rows, ref, first, last):
    planes = ref.shape[0]
    depth = rows.shape[1] // planes
    total = None
    for p in range(planes):
        term = mm(rows[:, p * depth : (p + 1) * depth], square_columns(ref, p, depth, first, last))
        total = term if total is None else total + term
    return total


def square_product_back(rows, ref, width, first, last):
    planes = ref.shape[0]
    depth = width // planes
    return jnp.concatenate(
        [mm_nt(rows, square_columns(ref, p, depth, first, last)) for p in range(planes)], axis=1
    )


def output_rows(ref, p, width, size, mix, conv, want_mix):
    base = (6 * size // BLOCK) * (width // ref.shape[0])
    parts = []
    for b in range(width // BLOCK):
        at = base + b * (mix + conv) + (0 if want_mix else mix)
        rows = ref[pl.ds(p, 1), at : at + (mix if want_mix else conv), :]
        parts.append(rows.reshape(rows.shape[1:]))
    return jnp.concatenate(parts, axis=1)


def forward_kernel(k, with_norm, *refs):
    mine, mate, refs = refs[:k], refs[k : 2 * k], refs[2 * k :]
    if with_norm:
        norm_ref, refs = refs[0], refs[1:]
    pack_ref, refs = refs[0], refs[1:]
    out_mine, out_mate, before_ref, active_ref = refs[:k], refs[k], refs[k + 1], refs[k + 2]
    slots, width = mine[0].shape
    blocks = down_blocks(pack_ref, width)
    for i in range(k):
        rows = jnp.concatenate([mine[i][...], mate[i][...]])
        at = pl.ds(2 * i * slots, 2 * slots)
        if with_norm:
            unit, _ = normalize(rows.astype(F32))
            rows = (unit * norm_ref[0:1, :] + norm_ref[1:2, :]).astype(BF16)
            refs[k + 3][at, :] = rows
        before = up_product(rows, pack_ref)
        before_ref[at, :] = before
        active = (before * sigmoid(before)).astype(BF16)
        active_ref[at, :] = active
        store_partial(out_mine, out_mate, i, slots, down_product(active, blocks))


def forward_call(pieces, pack, norm=None):
    mine, mate = pieces
    k, (slots, width) = len(mine), mine[0].shape
    hidden = pack.shape[2]
    rows = 2 * k * slots
    outs = [shape((slots, width), F32)] * k + [
        shape((k, slots, width), BF16),
        shape((rows, hidden), F32),
        shape((rows, hidden), BF16),
    ]
    args = list(mine) + list(mate)
    if norm is not None:
        outs.append(shape((rows, width), BF16))
        args.append(norm)
    result = kernel_call(
        functools.partial(forward_kernel, k, norm is not None),
        outs,
        args + [pack],
        flops=4 * rows * width * hidden,
    )
    return (result[:k], result[k]), result[k + 1 :]


def backward_kernel(k, *refs):
    mine, mate, refs = refs[:k], refs[k : 2 * k], refs[2 * k :]
    pack_ref, before_ref, refs = refs[0], refs[1], refs[2:]
    out_mine, out_mate, grad_ref = refs[:k], refs[k], refs[k + 1]
    slots, width = mine[0].shape
    blocks = down_blocks(pack_ref, width)
    for i in range(k):
        at = pl.ds(2 * i * slots, 2 * slots)
        rows = jnp.concatenate([mine[i][...], mate[i][...]])
        grad = down_product_back(rows, blocks) * swish_grad(before_ref[at, :])
        grad = grad.astype(BF16)
        grad_ref[at, :] = grad
        store_partial(out_mine, out_mate, i, slots, up_product_back(grad, pack_ref, width))


def backward_call(pieces, pack, before):
    mine, mate = pieces
    k, (slots, width) = len(mine), mine[0].shape
    rows, hidden = before.shape
    outs = [shape((slots, width), F32)] * k + [
        shape((k, slots, width), BF16),
        shape((rows, hidden), BF16),
    ]
    result = kernel_call(
        functools.partial(backward_kernel, k),
        outs,
        list(mine) + list(mate) + [pack, before],
        flops=4 * rows * width * hidden,
    )
    return (result[:k], result[k]), result[k + 1]


def joined(refs):
    return jnp.concatenate([r[...] for r in refs])


def take(refs, counts):
    groups, at = [], 0
    for n in counts:
        groups.append(refs[at : at + n])
        at += n
    return groups + [refs[at:]]


def put(out_refs, plane_ref, planes, write):
    if len(out_refs) == 1 and planes > 1:
        for p in range(planes):
            write(out_refs[0].at[p], p)
    else:
        for d in range(planes):
            write(out_refs[d], plane_ref[0] ^ d)


def rows_at(ref, p, rows, lanes=slice(None)):
    return ref[pl.ds(pl.multiple_of(p * rows, rows), rows), lanes]


def feed_weight_kernel(counts, planes, outs, *refs):
    plane_ref, refs = refs[0], refs[1:]
    normed, grads, active, rows, refs = take(refs, counts)
    out_refs, (up_ref, down_ref) = refs[:outs], refs[outs:]
    width, hidden = up_ref.shape
    depth, below = width // planes, hidden // planes
    down_ref[...] = mm_tn(joined(active), joined(rows))
    up_ref[...] = mm_tn(joined(normed), joined(grads))

    def write(out, p):
        out[:depth, :] = rows_at(up_ref, p, depth).astype(BF16)
        for b in range(width // hidden):
            at = depth + b * below
            lanes = slice(b * hidden, (b + 1) * hidden)
            out[at : at + below, :] = rows_at(down_ref, p, below, lanes).astype(BF16)

    put(out_refs, plane_ref, planes, write)


def feed_weight_call(normed, grads, active, rows, plane, planes, by_plane):
    width, hidden = normed[0].shape[1], grads[0].shape[1]
    lines = width // planes + (hidden // planes) * (width // hidden)
    one = shape((lines, hidden), BF16)
    outs = [shape((planes, lines, hidden), BF16)] if by_plane else [one] * planes
    groups = (normed, grads, active, rows)
    tokens = sum(a.shape[0] for a in grads)
    return kernel_call(
        functools.partial(feed_weight_kernel, [len(g) for g in groups], planes, len(outs)),
        outs,
        [a for g in groups for a in g],
        scalars=(plane,),
        flops=4 * width * hidden * tokens,
        scratch=[pltpu.VMEM((width, hidden), F32), pltpu.VMEM((hidden, width), F32)],
    )


def write_columns(out, total_ref, p, depth):
    for b in range(total_ref.shape[1] // BLOCK):
        lanes = slice(b * BLOCK, (b + 1) * BLOCK)
        out[b * depth : (b + 1) * depth, :] = rows_at(total_ref, p, depth, lanes).astype(BF16)


def write_output_rows(out, base, rows):
    count = rows.shape[0]
    for b in range(rows.shape[1] // BLOCK):
        at = base + b * count
        out[at : at + count, :] = rows[:, b * BLOCK : (b + 1) * BLOCK].astype(BF16)


def conv_weight_kernel(counts, planes, *refs):
    plane_ref, refs = refs[0], refs[1:]
    normed, grads, active, rows, refs = take(refs, counts)
    out_ref, gate_ref, row_ref = refs
    depth = gate_ref.shape[0] // planes
    below = row_ref.shape[0] // planes
    base = (gate_ref.shape[1] // BLOCK) * depth
    gate_ref[...] = mm_tn(joined(normed), joined(grads))
    row_ref[...] = mm_tn(joined(active), joined(rows))

    def write(out, p):
        write_columns(out, gate_ref, p, depth)
        write_output_rows(out, base, rows_at(row_ref, p, below))

    put([out_ref], plane_ref, planes, write)


def conv_weight_call(normed, grads, active, rows, plane, planes):
    width, gates, size = normed[0].shape[1], grads[0].shape[1], active[0].shape[1]
    lines = (gates // BLOCK) * (width // planes) + (width // BLOCK) * (size // planes)
    groups = (normed, grads, active, rows)
    tokens = sum(a.shape[0] for a in grads)
    return kernel_call(
        functools.partial(conv_weight_kernel, [len(g) for g in groups], planes),
        [shape((planes, lines, BLOCK), BF16)],
        [a for g in groups for a in g],
        scalars=(plane,),
        flops=2 * width * (gates + size) * tokens,
        scratch=[pltpu.VMEM((width, gates), F32), pltpu.VMEM((size, width), F32)],
    )[0]


def mix_weight_kernel(counts, planes, per_side, *refs):
    plane_ref, side_ref, refs = refs[0], refs[1], refs[2:]
    normed, grads, mixed, rows, place, refs = take(refs, counts)
    table_ref, near_ref, far_ref = place
    out_ref, total_ref, row_ref = refs
    depth = total_ref.shape[0] // planes
    base = (total_ref.shape[1] // BLOCK) * depth
    right = joined(grads)
    qkv = right.shape[1]
    total_ref[:, :qkv] = mm_tn(joined(normed), right)
    total_ref[:, qkv:] = mm_tn(table_ref[...], (near_ref[...] + far_ref[...]).astype(BF16))
    if per_side:
        row_ref[...] = mm_tn(joined(mixed), joined(rows))

    def write(out, p):
        write_columns(out, total_ref, p, depth)
        if per_side:
            below = row_ref.shape[0] // per_side
            place = p - side_ref[0] * per_side
            held = (place >= 0) & (place < per_side)
            share = held.astype(jnp.int32).astype(F32)
            head = rows_at(row_ref, jnp.where(held, place, 0), below) * share
            write_output_rows(out, base, head)

    put([out_ref], plane_ref, planes, write)


def mix_weight_call(normed, grads, mixed, rows, place, plane, side, planes, per_side):
    width, qkv, size = normed[0].shape[1], grads[0].shape[1], mixed[0].shape[1]
    total = qkv + size
    lines = (total // BLOCK) * (width // planes)
    if per_side:
        lines += (width // BLOCK) * (size // per_side)
    groups = (normed, grads, mixed, rows, place)
    tokens = sum(a.shape[0] for a in grads)
    return kernel_call(
        functools.partial(mix_weight_kernel, [len(g) for g in groups], planes, per_side),
        [shape((planes, lines, BLOCK), BF16)],
        [a for g in groups for a in g],
        scalars=(plane, side),
        flops=2 * width * (total + size) * tokens,
        scratch=[pltpu.VMEM((width, total), F32), pltpu.VMEM((size, width), F32)],
    )[0]


def stack_kernel(planes, *refs):
    plane_ref, ups, downs, out_ref = refs[0], refs[1 : 1 + planes], refs[1 + planes : -1], refs[-1]
    depth = ups[0].shape[0]
    for d in range(planes):
        at = pl.ds(plane_ref[0] ^ d, 1)
        out_ref[at, :depth, :] = ups[d][...].reshape((1,) + ups[d].shape)
        out_ref[at, depth:, :] = downs[d][...].reshape((1,) + downs[d].shape)


def channel_kernel(planes, sides, head_size, *refs):
    at_ref, pieces, refs = refs[0], refs[1 : 1 + planes], refs[1 + planes :]
    norm_refs, (tap_ref, batch_ref, bias_ref, length_ref, wide_ref) = refs[:5], refs[5:]
    plane, member, side, core = at_ref[0], at_ref[1], at_ref[2], at_ref[3]
    team, rows = pieces[0].shape[0], pieces[0].shape[1] - CARRY
    size = tap_ref.shape[1]
    listed = [pieces[0][m, rows : rows + 1, :].astype(F32) for m in range(team)]
    one = jnp.concatenate([listed[4], listed[3]])
    two = jnp.concatenate([listed[1], listed[6]])
    table = [
        listed[0],
        listed[2],
        jnp.where(core == 0, one, two),
        jnp.where(core == 0, two, one),
        listed[5],
        listed[7],
    ]
    length_ref[...] = jnp.concatenate(table).astype(jnp.int32)[:, : length_ref.shape[1]]
    for d in range(planes):
        for m in range(team):
            at = ((plane ^ d) * team + (member ^ m)) * rows
            wide_ref[pl.ds(pl.multiple_of(at, rows), rows), :] = pieces[d][m, :rows, :].astype(F32)
    every = wide_ref[...].T
    taps = tap_ref.shape[0] - 1
    for j in range(5):
        first = every[taps + j : taps + j + 1]
        norm_refs[j][...] = jnp.concatenate([first, every[taps + 5 + j : taps + 6 + j]])
    own = [
        wide_ref[pl.ds(pl.multiple_of((p * team + member) * rows, rows), rows), :]
        for p in range(planes)
    ]
    own = jnp.concatenate(own).T
    tap_ref[...] = own[: taps + 1]
    batch_ref[...] = own[taps + 10 : taps + 12]
    heads = size // head_size
    own = [
        wide_ref[
            pl.ds(
                pl.multiple_of(
                    (side * heads + h) * team * rows + (member // sides) * head_size, head_size
                ),
                head_size,
            ),
            :,
        ]
        for h in range(heads)
    ]
    own = jnp.concatenate(own).T
    bias_ref[...] = own[taps + 12 : taps + 14]


def chunk_order(pieces):
    rows = []
    for mine, mate in zip(*pieces):
        rows += [mine, mate]
    return rows


def item_bounds(length_ref, b=0):
    ends = [length_ref[b, 0]]
    for j in range(1, length_ref.shape[1] - 1):
        ends.append(ends[-1] + length_ref[b, j])
    return ends


def item_index(ends, where_at):
    total = (where_at >= ends[0]).astype(jnp.int32)
    for end in ends[1:]:
        total = total + (where_at >= end).astype(jnp.int32)
    return total


def head_masks(slots, head_size):
    lane = lax.broadcasted_iota(jnp.int32, (slots, LANES), 1)
    return [
        (lane >= h * head_size) & (lane < (h + 1) * head_size) for h in range(LANES // head_size)
    ]


def attention_kernel(k, first, head_size, rows_held, *refs):
    length_ref, side_ref, refs = refs[0], refs[1], refs[2:]
    mine, mate, refs = refs[:k], refs[k : 2 * k], refs[2 * k :]
    column_ref, mix_ref, bias_ref, place_ref, refs = refs[0], refs[1], refs[2], refs[3], refs[4:]
    out_mine, out_mate, saved_ref, probs_ref, mixed_ref = (
        refs[:k],
        refs[k],
        refs[k + 1],
        refs[k + 2],
        refs[k + 3],
    )
    slots, width = mine[0].shape
    size = place_ref.shape[1]
    mix = mix_rows(mix_ref, side_ref, width, size, rows_held)
    scale = head_size ** (-0.5)
    row_at = lax.broadcasted_iota(jnp.int32, (slots, slots), 0)
    column_at = lax.broadcasted_iota(jnp.int32, (slots, slots), 1)
    masks = head_masks(slots, head_size)
    for i in range(k):
        rows = jnp.concatenate([mine[i][...], mate[i][...]])
        qkv = square_product(rows, column_ref, 0, 3 * size)
        query = qkv[:, :size]
        query_c = (query + bias_ref[0:1, :]).astype(BF16)
        query_p = (query + bias_ref[1:2, :]).astype(BF16)
        key = qkv[:, size : 2 * size].astype(BF16)
        value = qkv[:, 2 * size :].astype(BF16)
        at = pl.ds(2 * i * slots, 2 * slots)
        saved_ref[at, 0:size] = query_c
        saved_ref[at, size : 2 * size] = query_p
        saved_ref[at, 2 * size : 3 * size] = key
        saved_ref[at, 3 * size : 4 * size] = value
        halves = []
        for j in range(2):
            b = 2 * i + j
            part = slice(j * slots, (j + 1) * slots)
            ends = item_bounds(length_ref, first + b)
            same = item_index(ends, row_at) == item_index(ends, column_at)
            blocks = []
            for lo in range(0, size, LANES):
                lanes = slice(lo, lo + LANES)
                mixed = jnp.zeros((slots, LANES), F32)
                for h, mask in enumerate(masks):
                    qc = jnp.where(mask, query_c[part, lanes], 0)
                    qp = jnp.where(mask, query_p[part, lanes], 0)
                    wide = mm_nt(qp, place_ref[:, lanes])
                    moved = pltpu.roll(wide, slots + 1, 1, stride=1, stride_axis=0)
                    scores = (mm_nt(qc, key[part, lanes]) + moved[:, :slots]) * scale
                    scores = jnp.where(same, scores, MASKED_SCORE)
                    top = jnp.max(scores, axis=-1, keepdims=True)
                    weights = jnp.exp(scores - top)
                    probs = weights / jnp.sum(weights, axis=-1, keepdims=True)
                    probs_ref[b, (lo // LANES) * len(masks) + h] = probs
                    mixed = jnp.where(mask, mm(probs.astype(BF16), value[part, lanes]), mixed)
                blocks.append(mixed)
            halves.append(jnp.concatenate(blocks, axis=1) if len(blocks) > 1 else blocks[0])
        mixed = jnp.concatenate(halves).astype(BF16)
        mixed_ref[at, :] = mixed
        store_partial(out_mine, out_mate, i, slots, mm(mixed, mix))


def mix_rows(mix_ref, side_ref, width, size, rows_held):
    per_side, mix, conv = rows_held
    if not per_side:
        return mix_ref[...]
    return jnp.concatenate(
        [
            output_rows(mix_ref, side_ref[0] * per_side + h, width, size, mix, conv, True)
            for h in range(per_side)
        ]
    )


def attention_call(pieces, lengths, first, side, columns, mix, rows_held, bias, place, head_size):
    mine, mate = pieces
    k, (slots, width) = len(mine), mine[0].shape
    size = place.shape[1]
    heads = size // head_size
    rows = 2 * k * slots
    outs = [shape((slots, width), F32)] * k + [
        shape((k, slots, width), BF16),
        shape((rows, 4 * size), BF16),
        shape((2 * k, heads, slots, slots), F32),
        shape((rows, size), BF16),
    ]
    result = kernel_call(
        functools.partial(attention_kernel, k, first, head_size, rows_held),
        outs,
        list(mine) + list(mate) + [columns, mix, bias, place],
        scalars=(lengths, side),
        flops=2 * rows * width * size * 4 + 2 * k * heads * 10 * slots * slots * LANES,
    )
    return (result[:k], result[k]), result[k + 1 :]


def attention_back_kernel(k, head_size, rows_held, *refs):
    side_ref, refs = refs[0], refs[1:]
    mine, mate, refs = refs[:k], refs[k : 2 * k], refs[2 * k :]
    column_ref, mix_ref, place_ref, saved_ref, probs_ref, refs = (
        refs[0],
        refs[1],
        refs[2],
        refs[3],
        refs[4],
        refs[5:],
    )
    out_mine, out_mate, grad_ref, place_grad_ref, bias_ref = (
        refs[:k],
        refs[k],
        refs[k + 1],
        refs[k + 2],
        refs[k + 3],
    )
    slots, width = mine[0].shape
    size = place_ref.shape[1]
    mix = mix_rows(mix_ref, side_ref, width, size, rows_held)
    scale = head_size ** (-0.5)
    masks = head_masks(slots, head_size)
    flip = (
        lax.broadcasted_iota(jnp.int32, (slots, slots), 0)
        + lax.broadcasted_iota(jnp.int32, (slots, slots), 1)
        == slots - 1
    ).astype(F32).astype(BF16)
    bias_c = jnp.zeros((1, size), F32)
    bias_p = jnp.zeros((1, size), F32)
    for i in range(k):
        rows = jnp.concatenate([mine[i][...], mate[i][...]])
        grad_mixed_all = mm_nt(rows, mix).astype(BF16)
        at = pl.ds(2 * i * slots, 2 * slots)
        halves = []
        for j in range(2):
            b = 2 * i + j
            part = slice(j * slots, (j + 1) * slots)
            rows_at = pl.ds((2 * i + j) * slots, slots)
            grad_qc, grad_qp, grad_k, grad_v = [], [], [], []
            for lo in range(0, size, LANES):
                lanes = slice(lo, lo + LANES)
                grad_mixed = grad_mixed_all[part, lanes]
                query_c = saved_ref[rows_at, lo : lo + LANES]
                query_p = saved_ref[rows_at, size + lo : size + lo + LANES]
                key = saved_ref[rows_at, 2 * size + lo : 2 * size + lo + LANES]
                value = saved_ref[rows_at, 3 * size + lo : 3 * size + lo + LANES]
                place = place_ref[:, lanes]
                gqc = jnp.zeros((slots, LANES), F32)
                gqp, gk, gv = gqc, gqc, gqc
                place_grad = jnp.zeros(place.shape, F32)
                for h, mask in enumerate(masks):
                    probs = probs_ref[b, (lo // LANES) * len(masks) + h]
                    own = jnp.where(mask, grad_mixed, 0)
                    grad_probs = mm_nt(own, value)
                    gv = gv + mm_tn(probs.astype(BF16), own)
                    inner = jnp.sum(probs * grad_probs, axis=-1, keepdims=True)
                    grad = (probs * (grad_probs - inner)).astype(BF16) * scale
                    grad = grad.astype(BF16)
                    gqc = jnp.where(mask, mm(grad, key), gqc)
                    gk = gk + mm_tn(grad, jnp.where(mask, query_c, 0))
                    turned = mm(flip, grad)
                    wide = jnp.concatenate([turned, jnp.zeros_like(turned)], axis=1)
                    wide = pltpu.roll(wide, 0, 1, stride=1, stride_axis=0).astype(BF16)
                    wide = mm(flip, wide).astype(BF16)
                    gqp = jnp.where(mask, mm(wide, place), gqp)
                    place_grad = place_grad + mm_tn(wide, jnp.where(mask, query_p, 0))
                if i == 0 and j == 0:
                    place_grad_ref[:, lanes] = place_grad
                else:
                    place_grad_ref[:, lanes] = place_grad_ref[:, lanes] + place_grad
                grad_qc.append(gqc)
                grad_qp.append(gqp)
                grad_k.append(gk)
                grad_v.append(gv)

            def side_by_side(blocks):
                return jnp.concatenate(blocks, axis=1) if len(blocks) > 1 else blocks[0]

            gqc, gqp = side_by_side(grad_qc), side_by_side(grad_qp)
            bias_c = bias_c + jnp.sum(gqc, axis=0, keepdims=True)
            bias_p = bias_p + jnp.sum(gqp, axis=0, keepdims=True)
            halves.append(
                jnp.concatenate(
                    [gqc + gqp, side_by_side(grad_k), side_by_side(grad_v)], axis=1
                ).astype(BF16)
            )
        grad = jnp.concatenate(halves)
        grad_ref[at, :] = grad
        store_partial(out_mine, out_mate, i, slots, square_product_back(grad, column_ref, width, 0, 3 * size))
    bias_ref[...] = jnp.concatenate([bias_c, bias_p])


def attention_back_call(pieces, side, columns, mix, rows_held, place, saved, probs, head_size):
    mine, mate = pieces
    k, (slots, width) = len(mine), mine[0].shape
    size = place.shape[1]
    rows = 2 * k * slots
    outs = [shape((slots, width), F32)] * k + [
        shape((k, slots, width), BF16),
        shape((rows, 3 * size), BF16),
        shape(place.shape, F32),
        shape((2, size), F32),
    ]
    result = kernel_call(
        functools.partial(attention_back_kernel, k, head_size, rows_held),
        outs,
        list(mine) + list(mate) + [columns, mix, place, saved, probs],
        scalars=(side,),
        flops=2 * rows * width * size * 4 + 2 * k * 24 * slots * slots * size,
    )
    return (result[:k], result[k]), result[k + 1 :]


def place_kernel(table_ref, column_ref, out_ref):
    size = out_ref.shape[1]
    rows = square_product(table_ref[...], column_ref, 3 * size, 4 * size)
    out_ref[...] = rows.astype(BF16)


def item_reach(ends, row_at, slots):
    start = jnp.zeros_like(row_at)
    end = jnp.full_like(row_at, slots)
    for at in ends:
        start = jnp.where(row_at >= at, at, start)
    for at in reversed(ends):
        end = jnp.where(row_at < at, at, end)
    valid = (row_at < ends[-1]).astype(F32)
    return row_at - start, end - 1 - row_at, valid


def gate_kernel(k, first, tap_count, *refs):
    length_ref, refs = refs[0], refs[1:]
    mine, mate, refs = refs[:k], refs[k : 2 * k], refs[2 * k :]
    column_ref, tap_ref, gate_ref, conv_ref, stat_ref, pad_ref = refs
    slots, _ = mine[0].shape
    size = tap_ref.shape[1]
    reach = tap_count // 2
    row_at = lax.broadcasted_iota(jnp.int32, (slots, size), 0)
    pad_ref[...] = jnp.zeros_like(pad_ref)
    count = jnp.zeros((1, size), F32)
    total = jnp.zeros((1, size), F32)
    for i in range(k):
        rows = jnp.concatenate([mine[i][...], mate[i][...]])
        gates = square_product(rows, column_ref, 4 * size, 6 * size)
        gate_ref[pl.ds(2 * i * slots, 2 * slots), :] = gates
        glu = gates[:, :size] * sigmoid(gates[:, size:])
        for j in range(2):
            b = 2 * i + j
            before, behind, valid = item_reach(item_bounds(length_ref, first + b), row_at, slots)
            pad_ref[PAD : PAD + slots, :] = glu[j * slots : (j + 1) * slots] * valid
            conv = jnp.zeros((slots, size), F32)
            for tap in range(tap_count):
                o = tap - reach
                near = pad_ref[PAD + o : PAD + o + slots, :]
                if o < 0:
                    near = jnp.where(before >= -o, near, 0.0)
                elif o > 0:
                    near = jnp.where(behind >= o, near, 0.0)
                conv = conv + near * tap_ref[tap : tap + 1, :]
            conv_ref[pl.ds(b * slots, slots), :] = conv
            count = count + jnp.sum(valid, axis=0, keepdims=True)
            total = total + jnp.sum(conv * valid, axis=0, keepdims=True)
    mean = total / count
    spread = jnp.zeros((1, size), F32)
    for b in range(2 * k):
        valid = (row_at < item_bounds(length_ref, first + b)[-1]).astype(F32)
        gap = (conv_ref[pl.ds(b * slots, slots), :] - mean) * valid
        spread = spread + jnp.sum(gap * gap, axis=0, keepdims=True)
    stat_ref[...] = jnp.concatenate([count, mean, spread, jnp.zeros((5, size), F32)])


def gate_call(pieces, lengths, first, columns, taps, tap_count):
    mine, mate = pieces
    k, (slots, width) = len(mine), mine[0].shape
    size = taps.shape[1]
    rows = 2 * k * slots
    return kernel_call(
        functools.partial(gate_kernel, k, first, tap_count),
        [shape((rows, 2 * size), F32), shape((rows, size), F32), shape((8, size), F32)],
        list(mine) + list(mate) + [columns, taps],
        scalars=(lengths,),
        flops=4 * rows * width * size + 40 * tap_count * rows * size,
        scratch=[pltpu.VMEM((slots + 2 * PAD, size), F32)],
    )


def merge_kernel(left_ref, right_ref, out_ref):
    n_left, n_right = left_ref[0:1, :], right_ref[0:1, :]
    m_left, m_right = left_ref[1:2, :], right_ref[1:2, :]
    count = n_left + n_right
    gap = m_right - m_left
    mean = (n_left * m_left + n_right * m_right) / count
    spread = left_ref[2:3, :] + right_ref[2:3, :] + gap * gap * (n_left * n_right / count)
    size = left_ref.shape[1]
    out_ref[...] = jnp.concatenate([count, mean, spread, jnp.zeros((5, size), F32)])


def merge(left, right):
    return kernel_call(merge_kernel, [shape(left.shape, F32)], [left, right])[0]


def batch_unit(conv, stat_ref):
    inverse = lax.rsqrt(stat_ref[2:3, :] / stat_ref[0:1, :] + EPSILON)
    return (conv - stat_ref[1:2, :]) * inverse, inverse


def batch_kernel(k, rows_held, *refs):
    conv_ref, stat_ref, batch_ref, out_weight_ref, refs = (
        refs[0],
        refs[1],
        refs[2],
        refs[3],
        refs[4:],
    )
    out_mine, out_mate, active_ref = refs[:k], refs[k], refs[k + 1]
    slots, width = out_mine[0].shape
    weight = conv_rows(out_weight_ref, width, active_ref.shape[1], rows_held)
    for i in range(k):
        at = pl.ds(2 * i * slots, 2 * slots)
        unit, _ = batch_unit(conv_ref[at, :], stat_ref)
        value = unit * batch_ref[0:1, :] + batch_ref[1:2, :]
        active = (value * sigmoid(value)).astype(BF16)
        active_ref[at, :] = active
        store_partial(out_mine, out_mate, i, slots, mm(active, weight))


def conv_rows(ref, width, size, rows_held):
    _, mix, conv = rows_held
    return jnp.concatenate(
        [output_rows(ref, p, width, size, mix, conv, False) for p in range(ref.shape[0])]
    )


def batch_call(k, conv, stats, batch_rows, out_weight, rows_held, slots, width):
    size = conv.shape[1]
    outs = [shape((slots, width), F32)] * k + [
        shape((k, slots, width), BF16),
        shape(conv.shape, BF16),
    ]
    result = kernel_call(
        functools.partial(batch_kernel, k, rows_held),
        outs,
        [conv, stats, batch_rows, out_weight],
        flops=2 * conv.shape[0] * width * size,
    )
    return (result[:k], result[k]), result[k + 1]


def batch_back_kernel(k, first, rows_held, *refs):
    length_ref, refs = refs[0], refs[1:]
    mine, mate, refs = refs[:k], refs[k : 2 * k], refs[2 * k :]
    conv_ref, stat_ref, batch_ref, out_weight_ref, grad_ref, sum_ref = refs
    slots, width = mine[0].shape
    size = conv_ref.shape[1]
    weight = conv_rows(out_weight_ref, width, size, rows_held)
    row_at = lax.broadcasted_iota(jnp.int32, (slots, size), 0)
    sums = [jnp.zeros((1, size), F32)] * 4
    for i in range(k):
        rows = jnp.concatenate([mine[i][...], mate[i][...]])
        grad_active = mm_nt(rows, weight)
        for j in range(2):
            b = 2 * i + j
            at = pl.ds(b * slots, slots)
            unit, _ = batch_unit(conv_ref[at, :], stat_ref)
            value = unit * batch_ref[0:1, :] + batch_ref[1:2, :]
            grad = grad_active[j * slots : (j + 1) * slots] * swish_grad(value)
            valid = (row_at < item_bounds(length_ref, first + b)[-1]).astype(F32)
            grad_unit = grad * batch_ref[0:1, :]
            grad_ref[at, :] = grad_unit
            terms = (grad * unit, grad, grad_unit * valid, grad_unit * unit * valid)
            sums = [s + jnp.sum(t, axis=0, keepdims=True) for s, t in zip(sums, terms)]
    sum_ref[...] = jnp.concatenate(sums + [jnp.zeros((4, size), F32)])


def batch_back_call(pieces, lengths, first, conv, stats, batch_rows, out_weight, rows_held):
    mine, mate = pieces
    k, (slots, width) = len(mine), mine[0].shape
    size = conv.shape[1]
    return kernel_call(
        functools.partial(batch_back_kernel, k, first, rows_held),
        [shape(conv.shape, F32), shape((8, size), F32)],
        list(mine) + list(mate) + [conv, stats, batch_rows, out_weight],
        scalars=(lengths,),
        flops=2 * conv.shape[0] * width * size,
    )


def gate_back_kernel(k, first, tap_count, *refs):
    length_ref, refs = refs[0], refs[1:]
    grad_in_ref, conv_ref, gate_ref, stat_ref, sum_ref, column_ref, tap_ref, refs = (
        refs[0],
        refs[1],
        refs[2],
        refs[3],
        refs[4],
        refs[5],
        refs[6],
        refs[7:],
    )
    out_mine, out_mate, grad_ref, tap_grad_ref, glu_ref, conv_grad_ref = (
        refs[:k],
        refs[k],
        refs[k + 1],
        refs[k + 2],
        refs[k + 3],
        refs[k + 4],
    )
    slots, width = out_mine[0].shape
    size = tap_ref.shape[1]
    reach = tap_count // 2
    row_at = lax.broadcasted_iota(jnp.int32, (slots, size), 0)
    glu_ref[...] = jnp.zeros_like(glu_ref)
    conv_grad_ref[...] = jnp.zeros_like(conv_grad_ref)
    tap_grad_ref[...] = jnp.zeros_like(tap_grad_ref)
    frame_count = stat_ref[0:1, :]
    mean_grad = sum_ref[2:3, :] / frame_count
    mean_cross = sum_ref[3:4, :] / frame_count
    for i in range(k):
        halves = []
        for j in range(2):
            b = 2 * i + j
            at = pl.ds(b * slots, slots)
            before, behind, valid = item_reach(item_bounds(length_ref, first + b), row_at, slots)
            gate_a, gate_sig = gate_ref[at, :size], sigmoid(gate_ref[at, size:])
            glu_ref[PAD : PAD + slots, :] = gate_a * gate_sig * valid
            unit, inverse = batch_unit(conv_ref[at, :], stat_ref)
            conv_grad = valid * inverse * (grad_in_ref[at, :] - mean_grad - unit * mean_cross)
            conv_grad_ref[PAD : PAD + slots, :] = conv_grad
            grad_glu = jnp.zeros((slots, size), F32)
            for tap in range(tap_count):
                o = tap - reach
                near = glu_ref[PAD + o : PAD + o + slots, :]
                back = conv_grad_ref[PAD - o : PAD - o + slots, :]
                if o < 0:
                    near = jnp.where(before >= -o, near, 0.0)
                    back = jnp.where(behind >= -o, back, 0.0)
                elif o > 0:
                    near = jnp.where(behind >= o, near, 0.0)
                    back = jnp.where(before >= o, back, 0.0)
                grad_glu = grad_glu + back * tap_ref[tap : tap + 1, :]
                tap_grad_ref[tap : tap + 1, :] += jnp.sum(near * conv_grad, axis=0, keepdims=True)
            grad_glu = grad_glu * valid
            halves.append(
                jnp.concatenate(
                    [grad_glu * gate_sig, grad_glu * gate_a * gate_sig * (1.0 - gate_sig)], axis=1
                ).astype(BF16)
            )
        grad = jnp.concatenate(halves)
        grad_ref[pl.ds(2 * i * slots, 2 * slots), :] = grad
        store_partial(out_mine, out_mate, i, slots, square_product_back(grad, column_ref, width, 4 * size, 6 * size))


def gate_back_call(k, lengths, first, grad_unit, conv, gates, stats, sums, columns, taps, tap_count, slots, width):
    rows, size = conv.shape
    outs = [shape((slots, width), F32)] * k + [
        shape((k, slots, width), BF16),
        shape((rows, 2 * size), BF16),
        shape(taps.shape, F32),
    ]
    padded = pltpu.VMEM((slots + 2 * PAD, size), F32)
    result = kernel_call(
        functools.partial(gate_back_kernel, k, first, tap_count),
        outs,
        [grad_unit, conv, gates, stats, sums, columns, taps],
        scalars=(lengths,),
        flops=4 * rows * width * size + 80 * tap_count * rows * size,
        scratch=[padded, padded],
    )
    return (result[:k], result[k]), result[k + 1 :]


def join_kernel(count, coefficient, *refs):
    stream_ref, own_ref, mate_ref, refs = refs[0], refs[1], refs[2], refs[3:]
    far, norm_ref, stream_out, normed_ref = refs[:count], refs[count], refs[count + 1], refs[count + 2]
    branch = own_ref[...] + mate_ref[0].astype(F32)
    for ref in far:
        branch = branch + ref[...].astype(F32)
    stream = stream_ref[...].astype(F32) + coefficient * branch
    stream_out[...] = stream
    unit, _ = normalize(stream)
    normed_ref[...] = (unit * norm_ref[0:1, :] + norm_ref[1:2, :]).astype(BF16)


def join_call(stream, parts, coefficient, norm):
    own, mate, far = parts
    return kernel_call(
        functools.partial(join_kernel, len(far), coefficient),
        [shape(own.shape, F32), shape(own.shape, BF16)],
        [stream, own, mate] + list(far) + [norm],
    )


def turn_kernel(count, coefficient, *refs):
    length_ref, refs = refs[0], refs[1:]
    stream_ref, own_ref, mate_ref, refs = refs[0], refs[1], refs[2], refs[3:]
    far, norm_ref, cotangent_ref, refs = refs[:count], refs[count], refs[count + 1], refs[count + 2 :]
    output_ref, grad_out, low_out, norm_grad = refs
    branch = own_ref[...] + mate_ref[0].astype(F32)
    for ref in far:
        branch = branch + ref[...].astype(F32)
    stream = stream_ref[...] + coefficient * branch
    row_at = lax.broadcasted_iota(jnp.int32, (stream.shape[0], 1), 0)
    valid = (row_at < item_bounds(length_ref)[-1]).astype(F32)
    unit, scale = normalize(stream)
    output_ref[...] = ((unit * norm_ref[0:1, :] + norm_ref[1:2, :]) * valid).astype(BF16)
    norm_back(
        unit,
        scale,
        norm_ref,
        cotangent_ref[...].astype(F32) * valid,
        0.0,
        0.5,
        grad_out,
        low_out,
        norm_grad,
    )


def norm_back(unit, scale, norm_ref, grad, base, coefficient, grad_out, low_out, norm_grad):
    norm_grad[...] = jnp.concatenate(
        [jnp.sum(grad * unit, axis=0, keepdims=True), jnp.sum(grad, axis=0, keepdims=True)]
    )
    grad = grad * norm_ref[0:1, :]
    inner = jnp.mean(grad, axis=-1, keepdims=True)
    cross = jnp.mean(grad * unit, axis=-1, keepdims=True)
    grad = base + scale * (grad - inner - unit * cross)
    if grad_out is not None:
        grad_out[...] = grad
    low_out[...] = (coefficient * grad).astype(BF16)


def turn_call(stream, parts, coefficient, norm, cotangent, lengths):
    own, mate, far = parts
    return kernel_call(
        functools.partial(turn_kernel, len(far), coefficient),
        [
            shape(own.shape, BF16),
            shape(own.shape, F32),
            shape(own.shape, BF16),
            shape((2, own.shape[1]), F32),
        ],
        [stream, own, mate] + list(far) + [norm, cotangent],
        scalars=(lengths,),
    )


def join_back_kernel(count, coefficient, keep, *refs):
    stream_ref, grad_ref, own_ref, mate_ref, refs = refs[0], refs[1], refs[2], refs[3], refs[4:]
    far, norm_ref, refs = refs[:count], refs[count], refs[count + 1 :]
    grad_out, (low_out, norm_grad) = (refs[0] if keep else None), refs[-2:]
    grad = own_ref[...] + mate_ref[0].astype(F32)
    for ref in far:
        grad = grad + ref[...].astype(F32)
    unit, scale = normalize(stream_ref[...].astype(F32))
    norm_back(
        unit, scale, norm_ref, grad, grad_ref[...], coefficient, grad_out, low_out, norm_grad
    )


def join_back_call(stream, grad, parts, coefficient, norm, keep=True):
    own, mate, far = parts
    outs = [shape(own.shape, F32)] if keep else []
    return kernel_call(
        functools.partial(join_back_kernel, len(far), coefficient, keep),
        outs + [shape(own.shape, BF16), shape((2, own.shape[1]), F32)],
        [stream, grad, own, mate] + list(far) + [norm],
    )


def offset_table(slot_count, model_width):
    offsets = jnp.arange(2 * slot_count, dtype=F32) - (slot_count - 1)
    freqs = jnp.exp(-jnp.log(10000.0) * jnp.arange(0, model_width, 2, dtype=F32) / model_width)
    angles = offsets[:, None] * freqs[None, :]
    return jnp.concatenate([jnp.sin(angles), jnp.cos(angles)], axis=1)


def nesterov(weight, moment, average, grad_rows, rate, rate_scale):
    moment_new = MOMENTUM_DECAY * moment + grad_rows
    weight_new = weight - rate * rate_scale * (grad_rows + MOMENTUM_DECAY * moment_new)
    average_new = AVERAGE_DECAY * average + (1.0 - AVERAGE_DECAY) * weight_new
    return (moment_new, weight_new, average_new)


def head_lanes(member, i, sides, planes, size):
    side, rest = member % sides, member // sides
    plane = side * (planes // sides) + i
    return (plane * 4 + rest) * size


def split_down_kernel(weight_ref, first_ref, second_ref):
    hidden = first_ref.shape[1]
    rows = weight_ref.shape[1]
    for layer, out in enumerate((first_ref, second_ref)):
        for b in range(weight_ref.shape[2] // hidden):
            part = weight_ref[layer, :, b * hidden : (b + 1) * hidden]
            out[b * rows : (b + 1) * rows, :] = part.astype(BF16)


def split_up_kernel(weight_ref, first_ref, second_ref):
    team, _, hidden = first_ref.shape
    planes = weight_ref.shape[2] // (team * LANES)
    for layer, out in enumerate((first_ref, second_ref)):
        for t in range(team):
            for p in range(planes):
                at = (p * team + t) * LANES
                part = weight_ref[layer, :, at : at + LANES]
                out[t, :, p * LANES : (p + 1) * LANES] = part.astype(BF16)


def split_square_kernel(planes, sides, head_size, weight_ref, column_ref, mix_ref, conv_ref):
    team = column_ref.shape[0]
    width = weight_ref.shape[2]
    size = width // team
    for t in range(team):
        for i, matrix in enumerate((0, 1, 2, 4, 5, 6)):
            if i < 4:
                starts = [
                    head_lanes(t, h, sides, planes, head_size) for h in range(size // head_size)
                ]
                count = head_size
            else:
                count = size // planes
                starts = [(p * team + t) * count for p in range(planes)]
            parts = [weight_ref[matrix, :, at : at + count] for at in starts]
            column_ref[t, :, i * size : (i + 1) * size] = jnp.concatenate(parts, axis=1).astype(BF16)
    mix_ref[...] = weight_ref[3].astype(BF16)
    conv_ref[...] = weight_ref[7].astype(BF16)


def square_pack_kernel(side_ref, column_ref, own_ref, other_ref, conv_ref, out_ref):
    team, rows, lanes = column_ref.shape
    for b in range(lanes // BLOCK):
        for t in range(team):
            at = (b * team + t) * rows
            out_ref[at : at + rows, :] = column_ref[t, :, b * BLOCK : (b + 1) * BLOCK]
    base = (lanes // BLOCK) * team * rows
    low = side_ref[0] == 0
    for b in range(own_ref.shape[1] // BLOCK):
        lane = slice(b * BLOCK, (b + 1) * BLOCK)
        own, other = own_ref[:, lane].astype(F32), other_ref[:, lane].astype(F32)
        at = base + b * 3 * rows
        out_ref[at : at + rows, :] = jnp.where(low, own, other).astype(BF16)
        out_ref[at + rows : at + 2 * rows, :] = jnp.where(low, other, own).astype(BF16)
        out_ref[at + 2 * rows : at + 3 * rows, :] = conv_ref[:, lane]


def feed_pack_kernel(up_ref, down_ref, out_ref):
    team, rows, _ = up_ref.shape
    for t in range(team):
        out_ref[t * rows : (t + 1) * rows, :] = up_ref[t]
    out_ref[team * rows :, :] = down_ref[...]


def column_grad_kernel(mix_ref, conv_ref, out_ref):
    team, rows, lanes = out_ref.shape
    depth = team * rows
    for b in range(lanes // BLOCK):
        ref, at = (mix_ref, b) if b < 2 else (conv_ref, b - 2)
        for t in range(team):
            first = at * depth + t * rows
            out_ref[t, :, b * BLOCK : (b + 1) * BLOCK] = ref[first : first + rows, :]


def update(scale_ref, rate, index, grad, refs):
    weight_ref, moment_ref, average_ref, grad_out, moment_out, weight_out, average_out = refs
    moment = MOMENTUM_DECAY * moment_ref[index] + grad
    weight = weight_ref[index] - rate * scale_ref[0:1, 0:1] * (grad + MOMENTUM_DECAY * moment)
    grad_out[index] = grad
    moment_out[index] = moment
    weight_out[index] = weight
    average_out[index] = AVERAGE_DECAY * average_ref[index] + (1.0 - AVERAGE_DECAY) * weight


def update_up_kernel(scale_ref, first_ref, second_ref, *refs):
    team, _, hidden = first_ref.shape
    for layer, ref in enumerate((first_ref, second_ref)):
        parts = [
            ref[t, :, p * LANES : (p + 1) * LANES] for p in range(hidden // LANES) for t in range(team)
        ]
        update(scale_ref, RATE_UP, layer, jnp.concatenate(parts, axis=1).astype(F32), refs)


def update_down_kernel(scale_ref, first_ref, second_ref, *refs):
    rows, width = refs[0].shape[1:]
    hidden = first_ref.shape[1]
    for layer, ref in enumerate((first_ref, second_ref)):
        base = ref.shape[0] - rows * (width // hidden)
        parts = [
            ref[base + b * rows : base + (b + 1) * rows, :] for b in range(width // hidden)
        ]
        update(scale_ref, RATE_DOWN, layer, jnp.concatenate(parts, axis=1).astype(F32), refs)


def update_square_kernel(planes, sides, head_size, side_ref, *refs):
    scale_ref, column_ref, mix_ref, other_ref, conv_ref, refs = (
        refs[0],
        refs[1],
        refs[2],
        refs[3],
        refs[4],
        refs[5:],
    )
    team, rows, _ = column_ref.shape
    width = refs[0].shape[2]
    size = width // team
    per_side = planes // sides
    for i, matrix in enumerate((0, 1, 2, 4, 5, 6)):
        parts = []
        if i < 4:
            for head in range(width // head_size):
                plane, rest = head // 4, head % 4
                t = rest * sides + plane // per_side
                at = i * size + (plane % per_side) * head_size
                parts.append(column_ref[t, :, at : at + head_size])
        else:
            count = size // planes
            for p in range(planes):
                for t in range(team):
                    at = i * size + p * count
                    parts.append(column_ref[t, :, at : at + count])
        update(scale_ref, RATE_SQUARE, matrix, jnp.concatenate(parts, axis=1).astype(F32), refs)
    blocks = width // BLOCK
    head_rows = sides * rows
    base = mix_ref.shape[0] - blocks * head_rows
    parts = []
    for b in range(blocks):
        at = slice(base + b * head_rows, base + (b + 1) * head_rows)
        parts.append(mix_ref[at, :].astype(F32) + other_ref[at, :].astype(F32))
    whole = jnp.concatenate(parts, axis=1)
    update(scale_ref, RATE_SQUARE, 3, jnp.where(side_ref[0] == 0, whole[:rows], whole[rows:]), refs)
    base = conv_ref.shape[0] - blocks * rows
    parts = [conv_ref[base + b * rows : base + (b + 1) * rows, :] for b in range(blocks)]
    update(scale_ref, RATE_SQUARE, 7, jnp.concatenate(parts, axis=1).astype(F32), refs)


def update_call(body, scale, terms, weight, moment, average, scalars=()):
    return kernel_call(
        body,
        [shape(weight.shape, F32)] * 4,
        [scale] + list(terms) + [weight, moment, average],
        scalars=scalars,
    )


def feature_grad_kernel(planes, sides, *refs):
    member_ref, refs = refs[0], refs[1:]
    norms, near_ref, far_ref, out_ref = refs[:5], refs[5], refs[6], refs[7]
    team, _, size = out_ref.shape
    count = size // planes
    per_side = planes // sides
    head_size = sides * count
    bias = near_ref[...] + far_ref[...]
    rest, side = member_ref[0] // sides, member_ref[0] % sides
    rows = jnp.concatenate([n[0:1, :] for n in norms] + [n[1:2, :] for n in norms])
    for t in range(team):
        parts, own = [], []
        for p in range(planes):
            at = (p * team + t) * count
            parts.append(rows[:, at : at + count])
            at = (p % per_side) * head_size + (t % sides) * count
            held = (rest == t // sides) & (side == p // per_side)
            own.append(bias[:, at : at + count] * held.astype(jnp.int32).astype(F32))
        out_ref[t] = jnp.concatenate(
            [jnp.concatenate(parts, axis=1), jnp.concatenate(own, axis=1)]
        )


def channel_grad_kernel(taps, term_ref, near_ref, far_ref, sum_ref, out_ref):
    features = jnp.sum(term_ref[...], axis=0)
    out_ref[...] = jnp.concatenate(
        [near_ref[:taps] + far_ref[:taps], features[:10], sum_ref[0:2], features[10:12]]
    )


def make_step(planes, sides):
    wide_team = sides == 2
    team_axes = ("x", "c", "y") if wide_team else ("x", "c")
    team = 8 if wide_team else 4
    outer_bits = [("z", 1 << i) for i in range((planes - 1).bit_length())]
    if not wide_team:
        outer_bits += [("y", 1 << i) for i in range((sides - 1).bit_length())]
    head_aligned = wide_team and planes * 4 == HEADS

    def turn(values, first):
        pairs = []
        for x in range(2):
            for c in range(2):
                for y in range(2):
                    along_x = (c == 0) == first
                    to = (1 - x, c, y) if along_x else (x, c, 1 - y)
                    pairs.append((4 * x + 2 * c + y, 4 * to[0] + 2 * to[1] + to[2]))
        return lax.ppermute(values, team_axes, pairs)

    def gather(values):
        mate = swap(values, "c")
        if not wide_team:
            across = swap(values, "x")
            return ([values], [mate]), ([across], [swap(across, "c")])
        first, second = turn(values, True), turn(values, False)
        far = turn(first, False)
        near = ([values, first, second], [mate, swap(first, "c"), swap(second, "c")])
        return near, ([far], [swap(far, "c")])

    def scatter(near, far, fill=()):
        own_near, mate_near = near
        (own_far,), mate_far = far
        got_far = swap(mate_far, "c")
        got_near = swap(mate_near, "c")
        out_far = (own_far + got_far[0].astype(F32)).astype(BF16)
        if not wide_team:
            across, fill = lax.optimization_barrier((swap(out_far, "x"), fill))
            return (own_near[0], got_near, [across]), fill
        relay, fill = lax.optimization_barrier((turn(out_far, False), fill))
        second = (own_near[2] + got_near[2].astype(F32)).astype(BF16)
        from_second = turn(second, False)
        first = own_near[1] + got_near[1].astype(F32) + relay.astype(F32)
        from_first = turn(first.astype(BF16), True)
        return (own_near[0], got_near, [from_first, from_second]), fill

    def side_rows(rows):
        return rows if wide_team else lax.all_gather(rows, "y", axis=0, tiled=True)

    def side_scatter(rows):
        if wide_team:
            return rows
        return lax.psum_scatter(rows, "y", scatter_dimension=0, tiled=True)

    def split_hidden(rows):
        r, f = rows.shape
        return rows.reshape(r, planes, team, f // (planes * team)).transpose(2, 0, 1, 3).reshape(
            team, r, f // team
        )

    def join_hidden(blocks):
        _, r, f = blocks.shape
        return blocks.reshape(team, r, planes, f // planes).transpose(1, 2, 0, 3).reshape(
            r, team * f
        )

    def split_heads(rows):
        r, d = rows.shape
        if not head_aligned:
            return rows.reshape(r, team, d // team).transpose(1, 0, 2)
        size = d // HEADS
        rows = rows.reshape(r, sides, planes // sides, 2, 2, size)
        return rows.transpose(3, 4, 1, 0, 2, 5).reshape(team, r, d // team)

    def join_heads(blocks):
        _, r, f = blocks.shape
        if not head_aligned:
            return blocks.transpose(1, 0, 2).reshape(r, team * f)
        size = team * f // HEADS
        blocks = blocks.reshape(2, 2, sides, r, planes // sides, size)
        return blocks.transpose(3, 2, 4, 0, 1, 5).reshape(r, team * f)

    def team_swap(blocks):
        return lax.all_to_all(blocks, team_axes, split_axis=0, concat_axis=0, tiled=True)

    def plane_pieces(rows):
        return [rows] + [swap(rows, "z", d) for d in range(1, planes)]

    def plane_stack(ups, downs, plane):
        hidden = ups[0].shape[1]
        return kernel_call(
            functools.partial(stack_kernel, planes),
            [shape((planes, ups[0].shape[0] + downs[0].shape[0], hidden), BF16)],
            list(ups) + list(downs),
            scalars=(plane,),
        )[0]

    def plane_gather(rows):
        return lax.all_gather(rows, "z", axis=0, tiled=False)

    def plane_reduce(rows):
        return lax.psum_scatter(rows, "z", scatter_dimension=0, tiled=False)

    def to_blocks(rows, size):
        return jnp.concatenate([rows[:, i : i + size] for i in range(0, rows.shape[1], size)])

    def from_blocks(rows, count):
        return jnp.concatenate(jnp.split(rows, count), axis=1)

    def plane_scatter(pieces):
        total = pieces[0].astype(F32)
        for d in range(1, planes):
            total = total + swap(pieces[d], "z", d).astype(F32)
        return total

    def outer_sum(values):
        for axis, bit in outer_bits:
            values = values + swap(values, axis, bit)
        return values

    def step(
        frames,
        lengths,
        out_grad,
        up_weight,
        down_weight,
        square_weight,
        chan_weight,
        up_moment,
        down_moment,
        square_moment,
        chan_moment,
        up_average,
        down_average,
        square_average,
        chan_average,
    ):
        slots, width = frames.shape
        head_size = width // HEADS
        item_count = lengths.shape[1] - 1
        chan_rows = chan_weight.shape[0]
        tap_count = chan_rows - 14
        hidden = up_weight.shape[2]
        team_hidden = hidden // team
        team_width = width // team
        x_at, c_at, y_at = lax.axis_index("x"), lax.axis_index("c"), lax.axis_index("y")
        team_at = (x_at * 2 + c_at) * 2 + y_at if wide_team else x_at * 2 + c_at
        side = y_at.reshape(1).astype(jnp.int32)
        plane = lax.axis_index("z").reshape(1).astype(jnp.int32)

        chan_low = chan_weight.astype(BF16)
        if head_aligned:
            blocks = [shape((hidden // planes // team * (width // team_hidden), team_hidden), BF16)] * 2
            down_one, down_two = kernel_call(split_down_kernel, blocks, [down_weight])
            rows_in = up_weight.shape[1]
            blocks = [shape((team, rows_in, team_hidden), BF16)] * 2
            up_one, up_two = kernel_call(split_up_kernel, blocks, [up_weight])
            columns, mix, conv_out = kernel_call(
                functools.partial(split_square_kernel, planes, sides, head_size),
                [shape((team, rows_in, 6 * team_width), BF16)] + [shape((rows_in, width), BF16)] * 2,
                [square_weight],
            )
        else:
            up_low = up_weight.astype(BF16)
            down_low = down_weight.astype(BF16)
            square_low = square_weight.astype(BF16)
            down_one, down_two = [to_blocks(side_rows(down_low[i]), team_hidden) for i in (0, 1)]
            up_one, up_two = [split_hidden(side_rows(up_low[i])) for i in (0, 1)]
            columns = jnp.concatenate(
                [split_heads(side_rows(square_low[i])) for i in (0, 1, 2, 4)]
                + [split_hidden(side_rows(square_low[i])) for i in (5, 6)],
                axis=2,
            )
            mix, conv_out = square_low[3], side_rows(square_low[7])
        down_one = plane_pieces(down_one)
        up_one = team_swap(up_one).reshape(-1, team_hidden)
        near, far = gather(frames)

        if wide_team:
            lanes = jnp.pad(chan_low, ((0, LANES - chan_rows), (0, 0))).T
            carried = jnp.pad(
                lengths.astype(BF16), ((0, CARRY - 1), (0, LANES - lengths.shape[1]))
            )
            lanes = jnp.concatenate([lanes, carried])[None]
            for axis in ("y", "c", "x"):
                lanes = jnp.concatenate([lanes, swap(lanes, axis)])
            where_at = jnp.stack([plane[0], team_at, y_at, c_at]).astype(jnp.int32)
            norms = [shape((2, width), F32)] * 5
            params = kernel_call(
                functools.partial(channel_kernel, planes, sides, head_size),
                norms
                + [
                    shape((tap_count + 1, team_width), F32),
                    shape((2, team_width), F32),
                    shape((2, team_width), F32),
                    shape((team, lengths.shape[1]), jnp.int32),
                ],
                plane_pieces(lanes),
                scalars=(where_at,),
                scratch=[pltpu.VMEM((width, LANES), F32)],
            )
            norms, (taps, batch_rows, bias_rows, team_lengths) = params[:5], params[5:]
        else:
            team_lengths = jnp.concatenate(sum([chunk_order(p) for p in gather(lengths)], []))
            chan_float = lax.all_gather(chan_low, ALL, axis=1, tiled=True).astype(F32)

            def own_hidden(rows):
                rows = rows.reshape(rows.shape[0], planes, team, -1)
                rows = lax.dynamic_index_in_dim(rows, team_at, axis=2, keepdims=False)
                return rows.reshape(rows.shape[0], team_width)

            taps = own_hidden(chan_float[: tap_count + 1])
            batch_rows = own_hidden(chan_float[tap_count + 10 : tap_count + 12])
            bias_rows = lax.dynamic_index_in_dim(
                split_heads(chan_float[tap_count + 12 : tap_count + 14]), team_at, 0, False
            )
            norms = [
                jnp.stack([chan_float[tap_count + j], chan_float[tap_count + 5 + j]])
                for j in range(5)
            ]

        columns, up_two = team_swap(columns), team_swap(up_two)
        if head_aligned:
            head_rows = sides * rows_in
            per_side = planes // sides
            rows_held = (per_side, head_rows, rows_in)
            lines = 6 * team_width // BLOCK * team * rows_in + width // BLOCK * 3 * rows_in
            squares = kernel_call(
                square_pack_kernel,
                [shape((lines, BLOCK), BF16)],
                [columns, mix, swap(mix, "y"), conv_out],
                scalars=(side,),
            )[0]
            second = kernel_call(
                feed_pack_kernel,
                [shape((team * rows_in + down_two.shape[0], team_hidden), BF16)],
                [up_two, down_two],
            )[0]
        else:
            per_side = 0
            rows_held = (0, 0, conv_out.shape[0])
            mix = lax.all_gather(mix, ALL, axis=0, tiled=True)
            mix = lax.dynamic_slice_in_dim(mix, team_at * team_width, team_width, axis=0)
            columns = to_blocks(columns.reshape(-1, 6 * team_width), BLOCK)
            squares = jnp.concatenate([columns, to_blocks(conv_out, BLOCK)])
            second = jnp.concatenate([up_two.reshape(-1, team_hidden), down_two])
        table = offset_table(slots, width).astype(BF16)

        early = (near, far, norms, taps, team_lengths, down_one, table)
        up_one, early, squares, second, mix = lax.optimization_barrier(
            (up_one, early, squares, second, mix)
        )
        up_one = plane_pieces(up_one)
        up_one, early, squares, second, mix = lax.optimization_barrier(
            (up_one, early, squares, second, mix)
        )
        near, far, norms, taps, team_lengths, down_one, table = early
        squares = plane_gather(squares)
        if head_aligned:
            mix = squares
        pack_one = plane_stack(up_one, down_one, plane)

        part_near, (before_near, active_near, normed_near) = forward_call(near, pack_one, norms[0])
        part_far, (before_far, active_far, normed_far) = forward_call(far, pack_one, norms[0])
        saved_one = ([normed_near, normed_far], (before_near, before_far), [active_near, active_far])
        parts, _ = scatter(part_near, part_far)
        stream_one, normed = join_call(frames, parts, 0.5, norms[1])
        normed, second = lax.optimization_barrier((normed, second))
        pack_two = plane_gather(second)

        near, far = gather(normed)
        place = kernel_call(
            place_kernel,
            [shape((table.shape[0], team_width), BF16)],
            [table, squares],
            flops=2 * table.shape[0] * width * team_width,
        )[0]
        normed_two = chunk_order(near) + chunk_order(far)
        part_near, saved_near = attention_call(
            near, team_lengths, 0, side, squares, mix, rows_held, bias_rows, place, head_size
        )
        part_far, saved_far = attention_call(
            far, team_lengths, 2 * len(near[0]), side, squares, mix, rows_held, bias_rows, place, head_size
        )
        parts, _ = scatter(part_near, part_far)
        stream_two, normed = join_call(stream_one, parts, 1.0, norms[2])

        near, far = gather(normed)
        normed_three = chunk_order(near) + chunk_order(far)
        k_near, k_far = len(near[0]), len(far[0])
        gates_near, conv_near, stats_near = gate_call(
            near, team_lengths, 0, squares, taps, tap_count
        )
        gates_far, conv_far, stats_far = gate_call(
            far, team_lengths, 2 * k_near, squares, taps, tap_count
        )
        stats = merge(stats_near, stats_far)
        for axis, bit in outer_bits:
            stats = merge(stats, swap(stats, axis, bit))
        part_far, act_far = batch_call(
            k_far, conv_far, stats, batch_rows, squares, rows_held, slots, width
        )
        part_near, act_near = batch_call(
            k_near, conv_near, stats, batch_rows, squares, rows_held, slots, width
        )
        active_conv = [act_near, act_far]
        parts, _ = scatter(part_near, part_far)
        stream_three, normed = join_call(stream_two, parts, 1.0, norms[3])
        normed, pack_two = lax.optimization_barrier((normed, pack_two))

        near, far = gather(normed)
        part_near, (before_near, active_near) = forward_call(near, pack_two)
        part_far, (before_far, active_far) = forward_call(far, pack_two)
        saved_four = (
            chunk_order(near) + chunk_order(far),
            (before_near, before_far),
            [active_near, active_far],
        )
        parts, _ = scatter(part_near, part_far)
        output, grad_four, low, norm_four = turn_call(
            stream_three, parts, 0.5, norms[4], out_grad, lengths
        )

        def feed_backward(low, pack, saved, by_plane):
            normed, (before_near, before_far), active = saved
            near, far = gather(low)
            part_near, grad_near = backward_call(near, pack, before_near)
            part_far, grad_far = backward_call(far, pack, before_far)
            rows = chunk_order(near) + chunk_order(far)
            term = feed_weight_call(
                normed, [grad_near, grad_far], active, rows, plane, planes, by_plane
            )
            return scatter(part_near, part_far, term)

        parts, (second_term,) = feed_backward(low, pack_two, saved_four, True)
        grad_three, low, norm_three = join_back_call(stream_three, grad_four, parts, 1.0, norms[3])
        low, second_term = lax.optimization_barrier((low, second_term))
        second_term = plane_reduce(second_term)

        near, far = gather(low)
        grad_near, sums_near = batch_back_call(
            near, team_lengths, 0, conv_near, stats, batch_rows, squares, rows_held
        )
        grad_far, sums_far = batch_back_call(
            far, team_lengths, 2 * k_near, conv_far, stats, batch_rows, squares, rows_held
        )
        conv_grads = chunk_order(near) + chunk_order(far)
        local_sums = sums_near + sums_far
        sums = outer_sum(local_sums)
        part_far, (gate_grad_far, taps_far) = gate_back_call(
            k_far, team_lengths, 2 * k_near, grad_far, conv_far, gates_far, stats, sums, squares, taps,
            tap_count, slots, width,
        )
        part_near, (gate_grad_near, taps_near) = gate_back_call(
            k_near, team_lengths, 0, grad_near, conv_near, gates_near, stats, sums, squares, taps,
            tap_count, slots, width,
        )
        conv_term = conv_weight_call(
            normed_three, [gate_grad_near, gate_grad_far], active_conv, conv_grads, plane, planes
        )
        parts, conv_term = scatter(part_near, part_far, conv_term)
        grad_two, low, norm_two = join_back_call(stream_two, grad_three, parts, 1.0, norms[2])
        low, conv_term, second_term = lax.optimization_barrier((low, conv_term, second_term))
        conv_term = plane_reduce(conv_term)

        near, far = gather(low)
        part_near, (qkv_near, place_near, bias_near) = attention_back_call(
            near, side, squares, mix, rows_held, place, saved_near[0], saved_near[1], head_size
        )
        part_far, (qkv_far, place_far, bias_far) = attention_back_call(
            far, side, squares, mix, rows_held, place, saved_far[0], saved_far[1], head_size
        )
        mixed, rows = [saved_near[2], saved_far[2]], chunk_order(near) + chunk_order(far)
        mix_term = mix_weight_call(
            normed_two, [qkv_near, qkv_far], mixed, rows, [table, place_near, place_far], plane,
            side, planes, per_side,
        )
        parts, mix_term = scatter(part_near, part_far, mix_term)
        if not head_aligned:
            mix_own = mm_tn(jnp.concatenate(mixed), jnp.concatenate(rows)).astype(BF16)
            mix_own = lax.dynamic_update_slice_in_dim(
                jnp.zeros((width, width), BF16), mix_own, team_at * team_width, axis=0
            )
        grad_one, low, norm_one = join_back_call(stream_one, grad_two, parts, 0.5, norms[1])
        low, mix_term, conv_term = lax.optimization_barrier((low, mix_term, conv_term))
        mix_term = plane_reduce(mix_term)

        parts, first_term = feed_backward(low, pack_one, saved_one, False)
        first_term = plane_scatter(first_term)
        frames_grad, norm_zero = join_back_call(frames, grad_one, parts, 1.0, norms[0], keep=False)

        late = (second_term, conv_term, mix_term)
        frames_grad, late = lax.optimization_barrier((frames_grad, late))
        second_term, conv_term, mix_term = late
        depth = width // planes
        rate_scale = lax.rsqrt(stats[0:1])

        def from_team(rows, columns):
            return team_swap(rows.astype(BF16).reshape(team, -1, columns))

        def finish_channels(chan_term):
            chan_term = outer_sum(chan_term).reshape(chan_rows, planes, -1)
            chan_term = lax.dynamic_index_in_dim(chan_term, lax.axis_index("z"), 1, keepdims=False)
            if not wide_team:
                chan_term = lax.dynamic_index_in_dim(
                    chan_term.reshape(chan_rows, sides, -1), y_at, 1, keepdims=False
                )
            return chan_term

        norm_terms = [norm_zero, norm_one, norm_two, norm_three, norm_four]
        if head_aligned:
            second_up = from_team(second_term[:depth], team_hidden)
            features = kernel_call(
                functools.partial(feature_grad_kernel, planes, sides),
                [shape((team, 12, team_width), F32)],
                norm_terms + [bias_near, bias_far],
                scalars=(team_at.reshape(1).astype(jnp.int32),),
            )[0]
            chan_term = kernel_call(
                functools.partial(channel_grad_kernel, tap_count),
                [shape((chan_rows, team_width), F32)],
                [team_swap(features), taps_near, taps_far, local_sums],
            )[0]
            chan_grad = finish_channels(chan_term)
            blocks = kernel_call(
                column_grad_kernel,
                [shape((team, rows_in, 6 * team_width), BF16)],
                [mix_term, conv_term],
            )[0]
            square_all = update_call(
                functools.partial(update_square_kernel, planes, sides, head_size),
                rate_scale,
                [team_swap(blocks), mix_term, swap(mix_term, "y"), conv_term],
                square_weight,
                square_moment,
                square_average,
                scalars=(side,),
            )
            first_term, square_all, chan_grad, second_up = lax.optimization_barrier(
                (first_term, square_all, chan_grad, second_up)
            )
            first_term = first_term.astype(BF16)
            down_all = update_call(
                update_down_kernel,
                rate_scale,
                [first_term, second_term],
                down_weight,
                down_moment,
                down_average,
            )
            up_all = update_call(
                update_up_kernel,
                rate_scale,
                [from_team(first_term[:depth], team_hidden), second_up],
                up_weight,
                up_moment,
                up_average,
            )
            up_grad, up_new = up_all[0], up_all[1:]
            down_grad, down_new = down_all[0], down_all[1:]
            square_grad, square_new = square_all[0], square_all[1:]
            rate_scale = rate_scale[0, 0]
        else:
            column_blocks = 4 * team_width // BLOCK
            qkv_term = from_blocks(mix_term[: column_blocks * depth], column_blocks)
            gate_blocks = 2 * team_width // BLOCK
            gate_term = from_blocks(conv_term[: gate_blocks * depth], gate_blocks)
            conv_out_term = from_blocks(conv_term[gate_blocks * depth :], width // BLOCK)
            mix_grad = lax.psum_scatter(mix_own, ALL, scatter_dimension=0, tiled=True).astype(F32)
            blocks = from_team(jnp.concatenate([qkv_term, gate_term], axis=1), 6 * team_width)

            def block(i):
                return blocks[:, :, i * team_width : (i + 1) * team_width]

            square_grad = jnp.stack(
                [side_scatter(join_heads(block(i))).astype(F32) for i in range(3)]
                + [mix_grad, side_scatter(join_heads(block(3))).astype(F32)]
                + [side_scatter(join_hidden(block(i))).astype(F32) for i in (4, 5)]
                + [side_scatter(conv_out_term).astype(F32)]
            )
            bias_terms = join_heads(
                lax.dynamic_update_slice_in_dim(
                    jnp.zeros((team, 2, team_width), F32), (bias_near + bias_far)[None], team_at, 0
                )
            )
            features = jnp.concatenate(
                [t[0:1] for t in norm_terms] + [t[1:2] for t in norm_terms] + [bias_terms]
            )
            features = jnp.sum(team_swap(split_hidden(features)), axis=0)
            chan_grad = finish_channels(
                jnp.concatenate(
                    [
                        (taps_near + taps_far)[:tap_count],
                        features[:10],
                        local_sums[:2],
                        features[10:],
                    ]
                )
            )
            feed_terms = (first_term.astype(BF16), second_term)
            up_grad = jnp.stack(
                [
                    side_scatter(join_hidden(from_team(rows[:depth], team_hidden))).astype(F32)
                    for rows in feed_terms
                ]
            )
            down_grad = jnp.stack(
                [
                    side_scatter(from_blocks(rows[depth:], width // team_hidden)).astype(F32)
                    for rows in feed_terms
                ]
            )
            rate_scale = rate_scale[0, 0]
            up_new = nesterov(up_weight, up_moment, up_average, up_grad, RATE_UP, rate_scale)
            down_new = nesterov(
                down_weight, down_moment, down_average, down_grad, RATE_DOWN, rate_scale
            )
            square_new = nesterov(
                square_weight, square_moment, square_average, square_grad, RATE_SQUARE, rate_scale
            )
        chan_new = nesterov(
            chan_weight, chan_moment, chan_average, chan_grad, RATE_CHANNEL, rate_scale
        )
        bias_grad = chan_grad[tap_count + 12 : tap_count + 14]
        return (
            output,
            frames_grad,
            up_grad,
            down_grad,
            square_grad,
            chan_grad,
            up_new[0],
            down_new[0],
            square_new[0],
            chan_new[0],
            up_new[1],
            down_new[1],
            square_new[1],
            chan_new[1],
            up_new[2],
            down_new[2],
            square_new[2],
            chan_new[2],
            bias_grad,
        )

    return step


def solution(mesh):
    wide, narrow = mesh.shape["wide"], mesh.shape["narrow"]
    planes = wide // 4
    inner = Mesh(mesh.devices.reshape(planes, 2, 2, narrow), ALL)
    token = P(ALL, None)
    matrix = P(None, ALL, None)
    vector = P(None, ALL)
    group = (matrix, matrix, matrix, vector)
    return jax.shard_map(
        make_step(planes, narrow),
        mesh=inner,
        in_specs=(token, token, token) + group * 3,
        out_specs=(token, token) + group * 4 + (vector,),
        check_vma=False,
    )
```

time: 757 us -> 567 us (0.75)
  local copies, waits for them, and re-layouts: 236 us -> 53.8 us
  Pallas kernels: 0 us -> 96.8 us
  matrix products: 95.8 us -> 0 us
  other arithmetic: 110 us -> 17.4 us
  waiting for transfers between devices: 140 us -> 230 us
  starting transfers between devices: 126 us -> 140 us
  blocking collectives: 20.9 us -> 7.13 us
    ppermute x0 -> x48, waiting for transfers between devices: none -> 145 us  [turn(): return lax.ppermute(values, team_axes, pairs)]
    pallas_call x0 -> x49, Pallas kernels: none -> 96.8 us  [kernel_call(): pl.pallas_call(body, out_shape=tuple(outs), in_specs=[pl.BlockSpec(memory...]
    dot_general x71 -> x0, matrix products: 95.8 us -> none  [the longest x27 29.3 us: mm(): return jnp.dot(left, right, preferred_element_type=F32)]
    ppermute x0 -> x48, starting transfers between devices: none -> 65.5 us  [turn(): return lax.ppermute(values, team_axes, pairs)]
    ppermute x138 -> x71, starting transfers between devices: 102 us -> 50.3 us  [swap(): return lax.ppermute(values, axis, [(i, i ^ bit) for i in range(size)])]
    mul x38 -> x0, local copies, waits for them, and re-layouts: 45.2 us -> none  [the longest x31 39.6 us: depth_conv(): total = total + jnp.where(match[:, :, None], near, 0.0) * tap]
    all_gather x5 -> x2, waiting for transfers between devices: 43.1 us -> 7.18 us  [plane_gather(): return lax.all_gather(rows, 'z', axis=0, tiled=False)]
    reduce_sum x25 -> x0, other arithmetic: 35.1 us -> none  [the longest x4 12 us: tap_grads(): jnp.sum(jnp.where(match[:, :, None], near, 0.0) * grad, axis=(0, 1))]
  transfers between devices with their start and end apart: 155 -> 130, of which waited for: 55 -> 51; matrix products, arithmetic and copies ran while one was open for 47% -> 3% of each run, Pallas kernels for 0% -> 16%
where the time goes in v2:
time: 567 us; the launch traced here: 561 us
  waiting for transfers between devices  230 us (41%)
  starting transfers between devices  140 us (25%)
  Pallas kernels  96.8 us (17%)
  local copies, waits for them, and re-layouts  53.8 us (9%)
  other arithmetic  17.4 us (3%)
  between operations  15.9 us (3%)
  blocking collectives  7.13 us (1%)
    ppermute x48, waiting for transfers between devices, turn(): return lax.ppermute(values, team_axes, pairs)  145 us
    pallas_call x49, Pallas kernels, kernel_call(): pl.pallas_call(body, out_shape=tuple(outs), in_specs=[pl.BlockSpec(memory...  96.8 us
    ppermute x71, waiting for transfers between devices, swap(): return lax.ppermute(values, axis, [(i, i ^ bit) for i in range(size)])  77.7 us
    ppermute x48, starting transfers between devices, turn(): return lax.ppermute(values, team_axes, pairs)  65.5 us
    unnamed x281, local copies, waits for them, and re-layouts  50.8 us
    ppermute x71, starting transfers between devices, swap(): return lax.ppermute(values, axis, [(i, i ^ bit) for i in range(size)])  50.3 us
    all_to_all x6, starting transfers between devices, team_swap(): lax.all_to_all(blocks, team_axes, split_axis=0, concat_axis=0, tiled=True)  23.4 us
  transfers between devices with their start and end apart: 130, of which 51 were waited for; matrix products, arithmetic and copies ran while one was open for 3% of the time, Pallas kernels for 16%

profile of v2, /device:TPU:0, one launch (start us, length us, event | category | flops | bytes accessed | tf_op | source)
XLA Modules:
  0.0 561.1 jit_solution(9901588965893545914)
XLA Ops:
  76.8 6.8 %collective-permute-done.17.refs_2_ = bf16[256,512]{1,0:T(8,128)(2,1)S(1)} collective-permute-done((bf16[256,512]{1,0:T(8,128)(2,1)S(1)}, bf16[256,512]{1,0:T(8,128)(2,1)S(1)}, u32[]{:S(2)}, u32[]{:S(2)}) %collective-permute-start.17) | collective-permute-done | bytes 262176 | tf_op jit(solution)/shard_map/ppermute | solution.py:44
  83.6 11.7 %collective-permute-done.18.refs_3_ = bf16[256,512]{1,0:T(8,128)(2,1)S(1)} collective-permute-done((bf16[256,512]{1,0:T(8,128)(2,1)S(1)}, bf16[256,512]{1,0:T(8,128)(2,1)S(1)}, u32[]{:S(2)}, u32[]{:S(2)}) %collective-permute-start.18) | collective-permute-done | bytes 262176 | tf_op jit(solution)/shard_map/ppermute | solution.py:44
  109.6 6.4 %collective-permute-done.22 = bf16[128,1024]{1,0:T(8,128)(2,1)S(1)} collective-permute-done((bf16[128,1024]{1,0:T(8,128)(2,1)S(1)}, bf16[128,1024]{1,0:T(8,128)(2,1)S(1)}, u32[]{:S(2)}, u32[]{:S(2)}) %collective-permute-start.22) | collective-permute-done | bytes 262176 | tf_op jit(solution)/shard_map/ppermute | solution.py:1271
  118.6 5.8 %collective-permute-done.23.refs_3_ = bf16[128,1024]{1,0:T(8,128)(2,1)S(1)} collective-permute-done((bf16[128,1024]{1,0:T(8,128)(2,1)S(1)}, bf16[128,1024]{1,0:T(8,128)(2,1)S(1)}, u32[]{:S(2)}, u32[]{:S(2)}) %collective-permute-start.23) | collective-permute-done | bytes 262176 | tf_op jit(solution)/shard_map/ppermute | solution.py:1271
  128.7 6.0 %collective-permute-done.25.refs_3_.refs_4_ = bf16[128,1024]{1,0:T(8,128)(2,1)} collective-permute-done((bf16[128,1024]{1,0:T(8,128)(2,1)}, bf16[128,1024]{1,0:T(8,128)(2,1)}, u32[]{:S(2)}, u32[]{:S(2)}) %collective-permute-start.25) | collective-permute-done | bytes 262176 | tf_op jit(solution)/shard_map/ppermute | solution.py:1271
  141.3 7.2 %all-gather.5.cloned.1.call-done = bf16[4608,256]{1,0:T(8,128)(2,1)} async-done(((bf16[1152,256]{1,0:T(8,128)(2,1)}), bf16[4608,256]{1,0:T(8,128)(2,1)}) %all-gather.5.cloned.1.call-update) | async-done | bytes 2359312 | tf_op jit(solution)/shard_map/all_gather | solution.py:1351
  151.9 8.1 %shard_map.305 = (f32[128,1024]{1,0:T(8,128)S(1)}, f32[128,1024]{1,0:T(8,128)S(1)}, f32[128,1024]{1,0:T(8,128)S(1)}, bf16[3,128,1024]{2,1,0:T(8,128)(2,1)}, bf16...) custom-call(s32[8,4]{1,0:T(8,128)S(1)} %get-tuple-element.307.refs_0_, ...), custom_call_target="tpu_custom_call" | custom-call | flops 1056964608 | bytes 10486784 | tf_op jit(solution)/shard_map/pallas_call | solution.py:75
  181.2 6.0 %collective-permute-done.35.refs_3_ = bf16[128,1024]{1,0:T(8,128)(2,1)S(1)} collective-permute-done((bf16[128,1024]{1,0:T(8,128)(2,1)S(1)}, bf16[128,1024]{1,0:T(8,128)(2,1)S(1)}, u32[]{:S(2)}, u32[]{:S(2)}) %collective-permute-start.35) | collective-permute-done | bytes 262176 | tf_op jit(solution)/shard_map/ppermute | solution.py:1271
  190.8 6.2 %collective-permute-done.37.refs_2_.refs_3_ = bf16[128,1024]{1,0:T(8,128)(2,1)S(1)} collective-permute-done((bf16[128,1024]{1,0:T(8,128)(2,1)S(1)}, bf16[128,1024]{1,0:T(8,128)(2,1)S(1)}, u32[]{:S(2)}, u32[]{:S(2)}) %collective-permute-start.37) | collective-permute-done | bytes 262176 | tf_op jit(solution)/shard_map/ppermute | solution.py:1271
  230.8 5.9 %collective-permute-done.49.refs_3_ = bf16[128,1024]{1,0:T(8,128)(2,1)S(1)} collective-permute-done((bf16[128,1024]{1,0:T(8,128)(2,1)S(1)}, bf16[128,1024]{1,0:T(8,128)(2,1)S(1)}, u32[]{:S(2)}, u32[]{:S(2)}) %collective-permute-start.49) | collective-permute-done | bytes 262176 | tf_op jit(solution)/shard_map/ppermute | solution.py:1271
  240.8 5.9 %collective-permute-done.51.refs_1_.refs_3_ = bf16[128,1024]{1,0:T(8,128)(2,1)S(1)} collective-permute-done((bf16[128,1024]{1,0:T(8,128)(2,1)}, bf16[128,1024]{1,0:T(8,128)(2,1)S(1)}, u32[]{:S(2)}, u32[]{:S(2)}) %collective-permute-start.51) | collective-permute-done | bytes 262176 | tf_op jit(solution)/shard_map/ppermute | solution.py:1271
  271.2 5.6 %collective-permute-done.61.refs_4_ = bf16[128,1024]{1,0:T(8,128)(2,1)S(1)} collective-permute-done((bf16[128,1024]{1,0:T(8,128)(2,1)S(1)}, bf16[128,1024]{1,0:T(8,128)(2,1)S(1)}, u32[]{:S(2)}, u32[]{:S(2)}) %collective-permute-start.61) | collective-permute-done | bytes 262176 | tf_op jit(solution)/shard_map/ppermute | solution.py:1271
  281.3 6.4 %collective-permute-done.63.refs_1_.refs_15_ = bf16[128,1024]{1,0:T(8,128)(2,1)S(1)} collective-permute-done((bf16[128,1024]{1,0:T(8,128)(2,1)S(1)}, bf16[128,1024]{1,0:T(8,128)(2,1)S(1)}, u32[]{:S(2)}, u32[]{:S(2)}) %collective-permute-start.63) | collective-permute-done | bytes 262176 | tf_op jit(solution)/shard_map/ppermute | solution.py:1271
  312.1 6.2 %collective-permute-done.73.refs_4_ = bf16[128,1024]{1,0:T(8,128)(2,1)S(1)} collective-permute-done((bf16[128,1024]{1,0:T(8,128)(2,1)S(1)}, bf16[128,1024]{1,0:T(8,128)(2,1)S(1)}, u32[]{:S(2)}, u32[]{:S(2)}) %collective-permute-start.73) | collective-permute-done | bytes 262176 | tf_op jit(solution)/shard_map/ppermute | solution.py:1271
  323.7 6.1 %collective-permute-done.75.refs_2_.refs_15_ = bf16[128,1024]{1,0:T(8,128)(2,1)S(1)} collective-permute-done((bf16[128,1024]{1,0:T(8,128)(2,1)}, bf16[128,1024]{1,0:T(8,128)(2,1)S(1)}, u32[]{:S(2)}, u32[]{:S(2)}) %collective-permute-start.75) | collective-permute-done | bytes 262176 | tf_op jit(solution)/shard_map/ppermute | solution.py:1271
  348.7 5.7 %shard_map.325 = (f32[128,1024]{1,0:T(8,128)S(1)}, f32[128,1024]{1,0:T(8,128)S(1)}, f32[128,1024]{1,0:T(8,128)S(1)}, bf16[3,128,1024]{2,1,0:T(8,128)(2,1)}, bf16...) custom-call(s32[8,4]{1,0:T(8,128)S(1)} %get-tuple-element.307.refs_0_, f32[768,128]{1,0:T(8,128)S(1)} %get-tuple-element.368.refs_1_, ...), custom_call_target="tpu_custom_call" | custom-call | flops 646447104 | bytes 6725632 | tf_op jit(solution)/shard_map/pallas_call | solution.py:75
  372.2 5.9 %collective-permute-done.87.refs_4_ = bf16[128,1024]{1,0:T(8,128)(2,1)S(1)} collective-permute-done((bf16[128,1024]{1,0:T(8,128)(2,1)S(1)}, bf16[128,1024]{1,0:T(8,128)(2,1)S(1)}, u32[]{:S(2)}, u32[]{:S(2)}) %collective-permute-start.87) | collective-permute-done | bytes 262176 | tf_op jit(solution)/shard_map/ppermute | solution.py:1271
  383.3 6.1 %collective-permute-done.89.refs_2_.refs_16_ = bf16[128,1024]{1,0:T(8,128)(2,1)S(1)} collective-permute-done((bf16[128,1024]{1,0:T(8,128)(2,1)}, bf16[128,1024]{1,0:T(8,128)(2,1)S(1)}, u32[]{:S(2)}, u32[]{:S(2)}) %collective-permute-start.89) | collective-permute-done | bytes 262176 | tf_op jit(solution)/shard_map/ppermute | solution.py:1271
  399.5 10.8 %shard_map.329 = (f32[128,1024]{1,0:T(8,128)S(1)}, f32[128,1024]{1,0:T(8,128)S(1)}, f32[128,1024]{1,0:T(8,128)S(1)}, bf16[3,128,1024]{2,1,0:T(8,128)(2,1)}, bf16...) custom-call(s32[1]{0:T(128)} %bitcast.3.side_ref.refs_1_.refs_0_, ...), custom_call_target="tpu_custom_call" | custom-call | flops 1107296256 | bytes 11011072 | tf_op jit(solution)/shard_map/pallas_call | solution.py:75
  427.9 6.5 %collective-permute-done.99.refs_4_ = bf16[128,1024]{1,0:T(8,128)(2,1)S(1)} collective-permute-done((bf16[128,1024]{1,0:T(8,128)(2,1)S(1)}, bf16[128,1024]{1,0:T(8,128)(2,1)S(1)}, u32[]{:S(2)}, u32[]{:S(2)}) %collective-permute-start.99) | collective-permute-done | bytes 262176 | tf_op jit(solution)/shard_map/ppermute | solution.py:1271
  440.0 6.8 %collective-permute-done.101.refs_1_.refs_9_ = bf16[128,1024]{1,0:T(8,128)(2,1)S(1)} collective-permute-done((bf16[128,1024]{1,0:T(8,128)(2,1)S(1)}, bf16[128,1024]{1,0:T(8,128)(2,1)S(1)}, u32[]{:S(2)}, u32[]{:S(2)}) %collective-permute-start.101) | collective-permute-done | bytes 262176 | tf_op jit(solution)/shard_map/ppermute | solution.py:1271
  477.4 7.1 %all_to_all.35.term_ref = f32[8,12,128]{2,1,0:T(8,128)S(1)} all-to-all(f32[8,12,128]{2,1,0:T(8,128)S(1)} %shard_map.339), channel_id=1, replica_groups=mesh['z'=4,'x'=2,'c'=2,'y'=2] {'x','c','y'}, dimensions={0} | all-to-all | bytes 98304 | tf_op jit(solution)/shard_map/all_to_all | solution.py:1336
  489.9 14.6 %collective-permute-done.117 = f32[45,128]{1,0:T(8,128)S(1)} collective-permute-done((f32[45,128]{1,0:T(8,128)S(1)}, f32[45,128]{1,0:T(8,128)S(1)}, u32[]{:S(2)}, u32[]{:S(2)}) %collective-permute-start.117) | collective-permute-done | bytes 23072 | tf_op jit(solution)/shard_map/ppermute | solution.py:44
  507.7 9.2 %collective-permute-done.118 = f32[45,128]{1,0:T(8,128)S(1)} collective-permute-done((f32[45,128]{1,0:T(8,128)S(1)}, f32[45,128]{1,0:T(8,128)S(1)}, u32[]{:S(2)}, u32[]{:S(2)}) %collective-permute-start.118) | collective-permute-done | bytes 23072 | tf_op jit(solution)/shard_map/ppermute | solution.py:44
  (614 shorter events, 372.1 us)
Async XLA Ops:
  13.3 18.0 %collective-permute-start = (bf16[128,1024]{1,0:T(8,128)(2,1)}, bf16[128,1024]{1,0:T(8,128)(2,1)}, u32[]{:S(2)}, u32[]{:S(2)}) collective-permute-start(bf16[128,1024]{1,0:T(8,128)(2,1)} %refs_0_.8), channel_id=1, source_target_pairs={{0,4},{1,5},{2,3},{3,2},{4,0},{5,1},{6,7},{7,6},{8,12},{9,13},{10,... | collective-permute-start | bytes 786440 | tf_op jit(solution)/shard_map/ppermute | solution.py:1271
  28.1 22.4 %collective-permute-start.1 = (bf16[128,1024]{1,0:T(8,128)(2,1)}, bf16[128,1024]{1,0:T(8,128)(2,1)}, u32[]{:S(2)}, u32[]{:S(2)}) collective-permute-start(bf16[128,1024]{1,0:T(8,128)(2,1)} %refs_0_.8), channel_id=1, source_target_pairs={{0,1},{1,0},{2,6},{3,7},{4,5},{5,4},{6,2},{7,3},{8,9},{9,8},{10,14... | collective-permute-start | bytes 786440 | tf_op jit(solution)/shard_map/ppermute | solution.py:1271
  30.0 21.8 %collective-permute-start.2 = (bf16[128,1024]{1,0:T(8,128)(2,1)}, bf16[128,1024]{1,0:T(8,128)(2,1)S(1)}, u32[]{:S(2)}, u32[]{:S(2)}) collective-permute-start(bf16[128,1024]{1,0:T(8,128)(2,1)} %refs_0_.8), channel_id=1, source_target_pairs={{0,2},{2,0},{1,3},{3,1},{4,6},{6,4},{5,7},{7,5},{8,10},{10,8},{9,1... | collective-permute-start | bytes 786440 | tf_op jit(solution)/shard_map/ppermute | solution.py:44
  30.8 20.9 %collective-permute-start.13 = (bf16[256,512]{1,0:T(8,128)(2,1)S(1)}, bf16[256,512]{1,0:T(8,128)(2,1)S(1)}, u32[]{:S(2)}, u32[]{:S(2)}) collective-permute-start(bf16[256,512]{1,0:T(8,128)(2,1)S(1)} %get-tuple-element.293.refs_5_), channel_id=1, source_target_pairs={{0,8},{8,0},{16,24},{24,16},{1,9},{9,1},{17,25},{25,17},{2,10},{10... | collective-permute-start | bytes 786440 | tf_op jit(solution)/shard_map/ppermute | solution.py:44
  31.3 21.0 %collective-permute-start.5 = (bf16[128,1024]{1,0:T(8,128)(2,1)}, bf16[128,1024]{1,0:T(8,128)(2,1)S(1)}, u32[]{:S(2)}, u32[]{:S(2)}) collective-permute-start(bf16[128,1024]{1,0:T(8,128)(2,1)} %collective-permute-done.refs_1_), channel_id=1, source_target_pairs={{0,1},{1,0},{2,6},{3,7},{4,5},{5,4},{6,2},{7,3},{8,9},{9,8},{10,14... | collective-permute-start | bytes 786440 | tf_op jit(solution)/shard_map/ppermute | solution.py:1271
  35.0 20.1 %all-to-all-start.1 = ((bf16[8,32,768]{2,1,0:T(8,128)(2,1)}), bf16[8,32,768]{2,1,0:T(8,128)(2,1)S(1)}, u32[]{:S(2)}, u32[]{:S(2)}) async-start(bf16[8,32,768]{2,1,0:T(8,128)(2,1)} %get-tuple-element.254), calls=%async_computation.1 | async-start | bytes 786432 | tf_op jit(solution)/shard_map/all_to_all | solution.py:1336
  46.8 22.0 %collective-permute-start.14 = (bf16[256,512]{1,0:T(8,128)(2,1)S(1)}, bf16[256,512]{1,0:T(8,128)(2,1)S(1)}, u32[]{:S(2)}, u32[]{:S(2)}) collective-permute-start(bf16[256,512]{1,0:T(8,128)(2,1)S(1)} %get-tuple-element.293.refs_5_), channel_id=1, source_target_pairs={{0,16},{8,24},{16,0},{24,8},{1,17},{9,25},{17,1},{25,9},{2,18},{10... | collective-permute-start | bytes 786440 | tf_op jit(solution)/shard_map/ppermute | solution.py:44
  50.5 18.3 %collective-permute-start.15 = (bf16[256,512]{1,0:T(8,128)(2,1)S(1)}, bf16[256,512]{1,0:T(8,128)(2,1)S(1)}, u32[]{:S(2)}, u32[]{:S(2)}) collective-permute-start(bf16[256,512]{1,0:T(8,128)(2,1)S(1)} %get-tuple-element.293.refs_5_), channel_id=1, source_target_pairs={{0,24},{8,16},{16,8},{24,0},{1,25},{9,17},{17,9},{25,1},{2,26},{10... | collective-permute-start | bytes 786440 | tf_op jit(solution)/shard_map/ppermute | solution.py:44
  51.8 17.1 %collective-permute-start.3 = (bf16[128,1024]{1,0:T(8,128)(2,1)}, bf16[128,1024]{1,0:T(8,128)(2,1)}, u32[]{:S(2)}, u32[]{:S(2)}) collective-permute-start(bf16[128,1024]{1,0:T(8,128)(2,1)} %collective-permute-done.refs_1_), channel_id=1, source_target_pairs={{0,2},{2,0},{1,3},{3,1},{4,6},{6,4},{5,7},{7,5},{8,10},{10,8},{9,1... | collective-permute-start | bytes 786440 | tf_op jit(solution)/shard_map/ppermute | solution.py:44
  51.8 17.0 %collective-permute-start.4 = (bf16[128,1024]{1,0:T(8,128)(2,1)}, bf16[128,1024]{1,0:T(8,128)(2,1)}, u32[]{:S(2)}, u32[]{:S(2)}) collective-permute-start(bf16[128,1024]{1,0:T(8,128)(2,1)} %collective-permute-done.1.refs_2_), channel_id=1, source_target_pairs={{0,2},{2,0},{1,3},{3,1},{4,6},{6,4},{5,7},{7,5},{8,10},{10,8},{9,1... | collective-permute-start | bytes 786440 | tf_op jit(solution)/shard_map/ppermute | solution.py:44
  58.5 90.0 %all-gather.5.cloned.1.call-start = ((), (), s32[]{:S(2)}) async-start(), calls=%async_computation.13 | async-start | bytes 2949120 | tf_op jit(solution)/shard_map/all_gather | solution.py:1351
  74.3 21.0 %collective-permute-start.18 = (bf16[256,512]{1,0:T(8,128)(2,1)S(1)}, bf16[256,512]{1,0:T(8,128)(2,1)S(1)}, u32[]{:S(2)}, u32[]{:S(2)}) collective-permute-start(bf16[256,512]{1,0:T(8,128)(2,1)S(1)} %bitcast.147), channel_id=1, source_target_pairs={{0,16},{8,24},{16,0},{24,8},{1,17},{9,25},{17,1},{25,9},{2,18},{10... | collective-permute-start | bytes 786440 | tf_op jit(solution)/shard_map/ppermute | solution.py:44
  74.3 21.7 %collective-permute-start.19 = (bf16[256,512]{1,0:T(8,128)(2,1)S(1)}, bf16[256,512]{1,0:T(8,128)(2,1)S(1)}, u32[]{:S(2)}, u32[]{:S(2)}) collective-permute-start(bf16[256,512]{1,0:T(8,128)(2,1)S(1)} %bitcast.148), channel_id=1, source_target_pairs={{0,24},{8,16},{16,8},{24,0},{1,25},{9,17},{17,9},{25,1},{2,26},{10... | collective-permute-start | bytes 786440 | tf_op jit(solution)/shard_map/ppermute | solution.py:44
  96.8 141.8 %all-gather.7.cloned.1.call-start = ((), (), s32[]{:S(2)}) async-start(), calls=%async_computation.14 | async-start | bytes 2621440 | tf_op jit(solution)/shard_map/all_gather | solution.py:1351
  141.3 18.7 %collective-permute-start.32 = (bf16[128,1024]{1,0:T(8,128)(2,1)}, bf16[128,1024]{1,0:T(8,128)(2,1)}, u32[]{:S(2)}, u32[]{:S(2)}) collective-permute-start(bf16[128,1024]{1,0:T(8,128)(2,1)} %collective-permute-done.31.refs_2_.refs_8_), channel_id=1, source_target_pairs={{0,2},{2,0},{1,3},{3,1},{4,6},{6,4},{5,7},{7,5},{8,10},{10,8},{9,1... | collective-permute-start | bytes 786440 | tf_op jit(solution)/shard_map/ppermute | solution.py:44
  160.0 16.7 %collective-permute-start.30 = (bf16[3,128,1024]{2,1,0:T(8,128)(2,1)}, bf16[3,128,1024]{2,1,0:T(8,128)(2,1)}, u32[]{:S(2)}, u32[]{:S(2)}) collective-permute-start(bf16[3,128,1024]{2,1,0:T(8,128)(2,1)} %get-tuple-element.315), channel_id=1, source_target_pairs={{0,2},{2,0},{1,3},{3,1},{4,6},{6,4},{5,7},{7,5},{8,10},{10,8},{9,1... | collective-permute-start | bytes 2359304 | tf_op jit(solution)/shard_map/ppermute | solution.py:44
  167.6 213.7 %reduce-scatter.4.cloned.1.call-start = ((), (), s32[]{:S(2)}) async-start(), calls=%async_computation.10 | async-start | bytes 2621440 | tf_op jit(solution)/shard_map/reduce_scatter | solution.py:1354
  321.5 116.8 %reduce-scatter.6.cloned.1.call-start = ((), (), s32[]{:S(2)}) async-start(), calls=%async_computation.11 | async-start | bytes 983040 | tf_op jit(solution)/shard_map/reduce_scatter | solution.py:1354
  396.0 88.6 %reduce-scatter.8.cloned.1.call-start = ((), (), s32[]{:S(2)}) async-start(), calls=%async_computation.12 | async-start | bytes 1966080 | tf_op jit(solution)/shard_map/reduce_scatter | solution.py:1354
  469.4 54.7 %collective-permute-start.115 = (bf16[512,512]{1,0:T(8,128)(2,1)}, bf16[512,512]{1,0:T(8,128)(2,1)}, u32[]{:S(2)}, u32[]{:S(2)}) collective-permute-start(bf16[512,512]{1,0:T(8,128)(2,1)} %get-tuple-element.439), channel_id=1, source_target_pairs={{0,24},{8,16},{16,8},{24,0},{1,25},{9,17},{17,9},{25,1},{2,26},{10... | collective-permute-start | bytes 1572872 | tf_op jit(solution)/shard_map/ppermute | solution.py:44
  471.0 53.1 %collective-permute-start.114 = (bf16[512,512]{1,0:T(8,128)(2,1)}, bf16[512,512]{1,0:T(8,128)(2,1)}, u32[]{:S(2)}, u32[]{:S(2)}) collective-permute-start(bf16[512,512]{1,0:T(8,128)(2,1)} %get-tuple-element.438), channel_id=1, source_target_pairs={{0,16},{8,24},{16,0},{24,8},{1,17},{9,25},{17,1},{25,9},{2,18},{10... | collective-permute-start | bytes 1572872 | tf_op jit(solution)/shard_map/ppermute | solution.py:44
  471.0 53.1 %collective-permute-start.113 = (bf16[512,512]{1,0:T(8,128)(2,1)S(1)}, bf16[512,512]{1,0:T(8,128)(2,1)}, u32[]{:S(2)}, u32[]{:S(2)}) collective-permute-start(bf16[512,512]{1,0:T(8,128)(2,1)S(1)} %get-tuple-element.437), channel_id=1, source_target_pairs={{0,8},{8,0},{16,24},{24,16},{1,9},{9,1},{17,25},{25,17},{2,10},{10... | collective-permute-start | bytes 1572872 | tf_op jit(solution)/shard_map/ppermute | solution.py:44
  484.5 19.9 %collective-permute-start.117 = (f32[45,128]{1,0:T(8,128)S(1)}, f32[45,128]{1,0:T(8,128)S(1)}, u32[]{:S(2)}, u32[]{:S(2)}) collective-permute-start(f32[45,128]{1,0:T(8,128)S(1)} %shard_map.340), channel_id=1, source_target_pairs={{0,8},{8,0},{16,24},{24,16},{1,9},{9,1},{17,25},{25,17},{2,10},{10... | collective-permute-start | bytes 69128 | tf_op jit(solution)/shard_map/ppermute | solution.py:44
  486.4 33.6 %all-to-all-start.3 = ((bf16[8,32,768]{2,1,0:T(8,128)(2,1)}), bf16[8,32,768]{2,1,0:T(8,128)(2,1)S(1)}, u32[]{:S(2)}, u32[]{:S(2)}) async-start(bf16[8,32,768]{2,1,0:T(8,128)(2,1)} %shard_map.337), calls=%async_computation.6 | async-start | bytes 786432 | tf_op jit(solution)/shard_map/all_to_all | solution.py:1336
  (246 other events, 1786.4 us)
Sparse Core Ops, SparseCore 0:
  96.9 51.5 all-gather.4
  167.7 44.7 all-gather.6
  321.6 42.2 reduce-scatter.3
  396.1 23.1 reduce-scatter.5
  438.5 33.4 reduce-scatter.7

commit v3 on v2

--- a/solution.py
+++ b/solution.py
@@ -255,23 +255,18 @@
     return groups + [refs[at:]]
 
 
-def put(out_refs, plane_ref, planes, write):
-    if len(out_refs) == 1 and planes > 1:
-        for p in range(planes):
-            write(out_refs[0].at[p], p)
-    else:
-        for d in range(planes):
-            write(out_refs[d], plane_ref[0] ^ d)
+def put(out_ref, planes, write):
+    for p in range(planes):
+        write(out_ref.at[p], p)
 
 
 def rows_at(ref, p, rows, lanes=slice(None)):
     return ref[pl.ds(pl.multiple_of(p * rows, rows), rows), lanes]
 
 
-def feed_weight_kernel(counts, planes, outs, *refs):
-    plane_ref, refs = refs[0], refs[1:]
+def feed_weight_kernel(counts, planes, *refs):
     normed, grads, active, rows, refs = take(refs, counts)
-    out_refs, (up_ref, down_ref) = refs[:outs], refs[outs:]
+    out_ref, up_ref, down_ref = refs
     width, hidden = up_ref.shape
     depth, below = width // planes, hidden // planes
     down_ref[...] = mm_tn(joined(active), joined(rows))
@@ -284,24 +279,21 @@
             lanes = slice(b * hidden, (b + 1) * hidden)
             out[at : at + below, :] = rows_at(down_ref, p, below, lanes).astype(BF16)
 
-    put(out_refs, plane_ref, planes, write)
-
-
-def feed_weight_call(normed, grads, active, rows, plane, planes, by_plane):
+    put(out_ref, planes, write)
+
+
+def feed_weight_call(normed, grads, active, rows, planes):
     width, hidden = normed[0].shape[1], grads[0].shape[1]
     lines = width // planes + (hidden // planes) * (width // hidden)
-    one = shape((lines, hidden), BF16)
-    outs = [shape((planes, lines, hidden), BF16)] if by_plane else [one] * planes
     groups = (normed, grads, active, rows)
     tokens = sum(a.shape[0] for a in grads)
     return kernel_call(
-        functools.partial(feed_weight_kernel, [len(g) for g in groups], planes, len(outs)),
-        outs,
+        functools.partial(feed_weight_kernel, [len(g) for g in groups], planes),
+        [shape((planes, lines, hidden), BF16)],
         [a for g in groups for a in g],
-        scalars=(plane,),
         flops=4 * width * hidden * tokens,
         scratch=[pltpu.VMEM((width, hidden), F32), pltpu.VMEM((hidden, width), F32)],
-    )
+    )[0]
 
 
 def write_columns(out, total_ref, p, depth):
@@ -318,7 +310,6 @@
 
 
 def conv_weight_kernel(counts, planes, *refs):
-    plane_ref, refs = refs[0], refs[1:]
     normed, grads, active, rows, refs = take(refs, counts)
     out_ref, gate_ref, row_ref = refs
     depth = gate_ref.shape[0] // planes
@@ -331,10 +322,10 @@
         write_columns(out, gate_ref, p, depth)
         write_output_rows(out, base, rows_at(row_ref, p, below))
 
-    put([out_ref], plane_ref, planes, write)
-
-
-def conv_weight_call(normed, grads, active, rows, plane, planes):
+    put(out_ref, planes, write)
+
+
+def conv_weight_call(normed, grads, active, rows, planes):
     width, gates, size = normed[0].shape[1], grads[0].shape[1], active[0].shape[1]
     lines = (gates // BLOCK) * (width // planes) + (width // BLOCK) * (size // planes)
     groups = (normed, grads, active, rows)
@@ -343,23 +334,23 @@
         functools.partial(conv_weight_kernel, [len(g) for g in groups], planes),
         [shape((planes, lines, BLOCK), BF16)],
         [a for g in groups for a in g],
-        scalars=(plane,),
         flops=2 * width * (gates + size) * tokens,
         scratch=[pltpu.VMEM((width, gates), F32), pltpu.VMEM((size, width), F32)],
     )[0]
 
 
 def mix_weight_kernel(counts, planes, per_side, *refs):
-    plane_ref, side_ref, refs = refs[0], refs[1], refs[2:]
+    side_ref, refs = refs[0], refs[1:]
     normed, grads, mixed, rows, place, refs = take(refs, counts)
-    table_ref, near_ref, far_ref = place
+    table_ref, place = place[0], place[1:]
     out_ref, total_ref, row_ref = refs
     depth = total_ref.shape[0] // planes
     base = (total_ref.shape[1] // BLOCK) * depth
     right = joined(grads)
     qkv = right.shape[1]
     total_ref[:, :qkv] = mm_tn(joined(normed), right)
-    total_ref[:, qkv:] = mm_tn(table_ref[...], (near_ref[...] + far_ref[...]).astype(BF16))
+    position = sum(ref[...] for ref in place)
+    total_ref[:, qkv:] = mm_tn(table_ref[...], position.astype(BF16))
     if per_side:
         row_ref[...] = mm_tn(joined(mixed), joined(rows))
 
@@ -373,10 +364,10 @@
             head = rows_at(row_ref, jnp.where(held, place, 0), below) * share
             write_output_rows(out, base, head)
 
-    put([out_ref], plane_ref, planes, write)
-
-
-def mix_weight_call(normed, grads, mixed, rows, place, plane, side, planes, per_side):
+    put(out_ref, planes, write)
+
+
+def mix_weight_call(normed, grads, mixed, rows, place, side, planes, per_side):
     width, qkv, size = normed[0].shape[1], grads[0].shape[1], mixed[0].shape[1]
     total = qkv + size
     lines = (total // BLOCK) * (width // planes)
@@ -388,19 +379,10 @@
         functools.partial(mix_weight_kernel, [len(g) for g in groups], planes, per_side),
         [shape((planes, lines, BLOCK), BF16)],
         [a for g in groups for a in g],
-        scalars=(plane, side),
+        scalars=(side,),
         flops=2 * width * (total + size) * tokens,
         scratch=[pltpu.VMEM((width, total), F32), pltpu.VMEM((size, width), F32)],
     )[0]
-
-
-def stack_kernel(planes, *refs):
-    plane_ref, ups, downs, out_ref = refs[0], refs[1 : 1 + planes], refs[1 + planes : -1], refs[-1]
-    depth = ups[0].shape[0]
-    for d in range(planes):
-        at = pl.ds(plane_ref[0] ^ d, 1)
-        out_ref[at, :depth, :] = ups[d][...].reshape((1,) + ups[d].shape)
-        out_ref[at, depth:, :] = downs[d][...].reshape((1,) + downs[d].shape)
 
 
 def channel_kernel(planes, sides, head_size, *refs):
@@ -454,11 +436,22 @@
     bias_ref[...] = own[taps + 12 : taps + 14]
 
 
-def chunk_order(pieces):
-    rows = []
-    for mine, mate in zip(*pieces):
-        rows += [mine, mate]
-    return rows
+def chunk_order(groups):
+    return [chunk for group in groups for pair in zip(*group) for chunk in pair]
+
+
+def add_kernel(count, *refs):
+    own_ref, mate_ref, out_ref = refs[0], refs[1], refs[-1]
+    total = own_ref[...] + mate_ref[count].astype(F32)
+    for ref in refs[2:-1]:
+        total = total + ref[...].astype(F32)
+    out_ref[...] = total.astype(BF16)
+
+
+def add_call(own, mate, index, *more):
+    return kernel_call(
+        functools.partial(add_kernel, index), [shape(own.shape, BF16)], [own, mate] + list(more)
+    )[0]
 
 
 def item_bounds(length_ref, b=0):
@@ -1223,12 +1216,12 @@
 
 def feature_grad_kernel(planes, sides, *refs):
     member_ref, refs = refs[0], refs[1:]
-    norms, near_ref, far_ref, out_ref = refs[:5], refs[5], refs[6], refs[7]
+    norms, biases, out_ref = refs[:5], refs[5:-1], refs[-1]
     team, _, size = out_ref.shape
     count = size // planes
     per_side = planes // sides
     head_size = sides * count
-    bias = near_ref[...] + far_ref[...]
+    bias = sum(ref[...] for ref in biases)
     rest, side = member_ref[0] // sides, member_ref[0] % sides
     rows = jnp.concatenate([n[0:1, :] for n in norms] + [n[1:2, :] for n in norms])
     for t in range(team):
@@ -1244,10 +1237,16 @@
         )
 
 
-def channel_grad_kernel(taps, term_ref, near_ref, far_ref, sum_ref, out_ref):
+def channel_grad_kernel(taps, term_ref, sum_ref, *refs):
+    tap_refs, out_ref = refs[:-1], refs[-1]
     features = jnp.sum(term_ref[...], axis=0)
     out_ref[...] = jnp.concatenate(
-        [near_ref[:taps] + far_ref[:taps], features[:10], sum_ref[0:2], features[10:12]]
+        [
+            sum(ref[:taps] for ref in tap_refs),
+            features[:10],
+            sum_ref[0:2],
+            features[10:12],
+        ]
     )
 
 
@@ -1271,30 +1270,45 @@
         return lax.ppermute(values, team_axes, pairs)
 
     def gather(values):
-        mate = swap(values, "c")
+        return spread(values, None)[0]
+
+    def spread(values, run):
+        groups, results = [([values], [swap(values, "c")])], []
+
+        def work(*travelling):
+            if run is not None:
+                result = run(len(results), groups[-1])
+                travelling, result = lax.optimization_barrier((travelling, result))
+                results.append(result)
+            return travelling
+
         if not wide_team:
-            across = swap(values, "x")
-            return ([values], [mate]), ([across], [swap(across, "c")])
-        first, second = turn(values, True), turn(values, False)
-        far = turn(first, False)
-        near = ([values, first, second], [mate, swap(first, "c"), swap(second, "c")])
-        return near, ([far], [swap(far, "c")])
-
-    def scatter(near, far, fill=()):
-        own_near, mate_near = near
-        (own_far,), mate_far = far
-        got_far = swap(mate_far, "c")
-        got_near = swap(mate_near, "c")
-        out_far = (own_far + got_far[0].astype(F32)).astype(BF16)
+            (far,) = work(swap(values, "x"))
+        else:
+            first, second = work(turn(values, True), turn(values, False))
+            far = turn(first, False)
+            groups.append(([first, second], [swap(first, "c"), swap(second, "c")]))
+            (far,) = work(far)
+        groups.append(([far], [swap(far, "c")]))
+        if run is not None:
+            results.append(run(len(results), groups[-1]))
+        return groups, results
+
+    def scatter(parts, fill=()):
+        (own,), own_mate = parts[0]
+        (far,), far_mate = parts[-1]
+        out_far = add_call(far, swap(far_mate, "c"), 0)
+        got_own = swap(own_mate, "c")
         if not wide_team:
             across, fill = lax.optimization_barrier((swap(out_far, "x"), fill))
-            return (own_near[0], got_near, [across]), fill
-        relay, fill = lax.optimization_barrier((turn(out_far, False), fill))
-        second = (own_near[2] + got_near[2].astype(F32)).astype(BF16)
-        from_second = turn(second, False)
-        first = own_near[1] + got_near[1].astype(F32) + relay.astype(F32)
-        from_first = turn(first.astype(BF16), True)
-        return (own_near[0], got_near, [from_first, from_second]), fill
+            return (own, got_own, [across]), fill
+        (first, second), side_mate = parts[1]
+        got_side = swap(side_mate, "c")
+        relay = turn(out_far, False)
+        from_second = turn(add_call(second, got_side, 1), False)
+        relay, fill = lax.optimization_barrier((relay, fill))
+        from_first = turn(add_call(first, got_side, 0, relay), True)
+        return (own, got_own, [from_first, from_second]), fill
 
     def side_rows(rows):
         return rows if wide_team else lax.all_gather(rows, "y", axis=0, tiled=True)
@@ -1338,15 +1352,6 @@
     def plane_pieces(rows):
         return [rows] + [swap(rows, "z", d) for d in range(1, planes)]
 
-    def plane_stack(ups, downs, plane):
-        hidden = ups[0].shape[1]
-        return kernel_call(
-            functools.partial(stack_kernel, planes),
-            [shape((planes, ups[0].shape[0] + downs[0].shape[0], hidden), BF16)],
-            list(ups) + list(downs),
-            scalars=(plane,),
-        )[0]
-
     def plane_gather(rows):
         return lax.all_gather(rows, "z", axis=0, tiled=False)
 
@@ -1358,12 +1363,6 @@
 
     def from_blocks(rows, count):
         return jnp.concatenate(jnp.split(rows, count), axis=1)
-
-    def plane_scatter(pieces):
-        total = pieces[0].astype(F32)
-        for d in range(1, planes):
-            total = total + swap(pieces[d], "z", d).astype(F32)
-        return total
 
     def outer_sum(values):
         for axis, bit in outer_bits:
@@ -1424,9 +1423,20 @@
                 axis=2,
             )
             mix, conv_out = square_low[3], side_rows(square_low[7])
-        down_one = plane_pieces(down_one)
-        up_one = team_swap(up_one).reshape(-1, team_hidden)
-        near, far = gather(frames)
+        up_one = team_swap(up_one)
+        up_one, frames, chan_low, lengths, columns, up_two, mix = lax.optimization_barrier(
+            (up_one, frames, chan_low, lengths, columns, up_two, mix)
+        )
+        if head_aligned:
+            first = kernel_call(
+                feed_pack_kernel,
+                [shape((team * rows_in + down_one.shape[0], team_hidden), BF16)],
+                [up_one, down_one],
+            )[0]
+        else:
+            first = jnp.concatenate([up_one.reshape(-1, team_hidden), down_one])
+        pack_one = plane_gather(first)
+        groups = gather(frames)
 
         if wide_team:
             lanes = jnp.pad(chan_low, ((0, LANES - chan_rows), (0, 0))).T
@@ -1453,7 +1463,7 @@
             )
             norms, (taps, batch_rows, bias_rows, team_lengths) = params[:5], params[5:]
         else:
-            team_lengths = jnp.concatenate(sum([chunk_order(p) for p in gather(lengths)], []))
+            team_lengths = jnp.concatenate(chunk_order(gather(lengths)))
             chan_float = lax.all_gather(chan_low, ALL, axis=1, tiled=True).astype(F32)
 
             def own_hidden(rows):
@@ -1498,136 +1508,128 @@
             second = jnp.concatenate([up_two.reshape(-1, team_hidden), down_two])
         table = offset_table(slots, width).astype(BF16)
 
-        early = (near, far, norms, taps, team_lengths, down_one, table)
-        up_one, early, squares, second, mix = lax.optimization_barrier(
-            (up_one, early, squares, second, mix)
-        )
-        up_one = plane_pieces(up_one)
-        up_one, early, squares, second, mix = lax.optimization_barrier(
-            (up_one, early, squares, second, mix)
-        )
-        near, far, norms, taps, team_lengths, down_one, table = early
+        ready = (pack_one, groups, norms, taps, team_lengths, table)
+        ready, squares, second, mix = lax.optimization_barrier((ready, squares, second, mix))
+        pack_one, groups, norms, taps, team_lengths, table = ready
         squares = plane_gather(squares)
         if head_aligned:
             mix = squares
-        pack_one = plane_stack(up_one, down_one, plane)
-
-        part_near, (before_near, active_near, normed_near) = forward_call(near, pack_one, norms[0])
-        part_far, (before_far, active_far, normed_far) = forward_call(far, pack_one, norms[0])
-        saved_one = ([normed_near, normed_far], (before_near, before_far), [active_near, active_far])
-        parts, _ = scatter(part_near, part_far)
+
+        def columns_of(results, i):
+            return [result[i] for result in results]
+
+        at = [0]
+        for group in groups:
+            at.append(at[-1] + 2 * len(group[0]))
+
+        results = [forward_call(group, pack_one, norms[0]) for group in groups]
+        saved_one = [columns_of(columns_of(results, 1), i) for i in (2, 0, 1)]
+        parts, _ = scatter(columns_of(results, 0))
         stream_one, normed = join_call(frames, parts, 0.5, norms[1])
         normed, second = lax.optimization_barrier((normed, second))
         pack_two = plane_gather(second)
 
-        near, far = gather(normed)
         place = kernel_call(
             place_kernel,
             [shape((table.shape[0], team_width), BF16)],
             [table, squares],
             flops=2 * table.shape[0] * width * team_width,
         )[0]
-        normed_two = chunk_order(near) + chunk_order(far)
-        part_near, saved_near = attention_call(
-            near, team_lengths, 0, side, squares, mix, rows_held, bias_rows, place, head_size
-        )
-        part_far, saved_far = attention_call(
-            far, team_lengths, 2 * len(near[0]), side, squares, mix, rows_held, bias_rows, place, head_size
-        )
-        parts, _ = scatter(part_near, part_far)
+
+        def attention(i, group):
+            return attention_call(
+                group, team_lengths, at[i], side, squares, mix, rows_held, bias_rows, place, head_size
+            )
+
+        groups, results = spread(normed, attention)
+        normed_two = chunk_order(groups)
+        saved_two = columns_of(results, 1)
+        parts, _ = scatter(columns_of(results, 0))
         stream_two, normed = join_call(stream_one, parts, 1.0, norms[2])
 
-        near, far = gather(normed)
-        normed_three = chunk_order(near) + chunk_order(far)
-        k_near, k_far = len(near[0]), len(far[0])
-        gates_near, conv_near, stats_near = gate_call(
-            near, team_lengths, 0, squares, taps, tap_count
-        )
-        gates_far, conv_far, stats_far = gate_call(
-            far, team_lengths, 2 * k_near, squares, taps, tap_count
-        )
-        stats = merge(stats_near, stats_far)
+        def gates(i, group):
+            return gate_call(group, team_lengths, at[i], squares, taps, tap_count)
+
+        groups, saved_three = spread(normed, gates)
+        normed_three = chunk_order(groups)
+        stats = saved_three[0][2]
+        for saved in saved_three[1:]:
+            stats = merge(stats, saved[2])
         for axis, bit in outer_bits:
             stats = merge(stats, swap(stats, axis, bit))
-        part_far, act_far = batch_call(
-            k_far, conv_far, stats, batch_rows, squares, rows_held, slots, width
-        )
-        part_near, act_near = batch_call(
-            k_near, conv_near, stats, batch_rows, squares, rows_held, slots, width
-        )
-        active_conv = [act_near, act_far]
-        parts, _ = scatter(part_near, part_far)
+        results = [
+            batch_call(
+                len(group[0]), saved[1], stats, batch_rows, squares, rows_held, slots, width
+            )
+            for group, saved in reversed(list(zip(groups, saved_three)))
+        ][::-1]
+        active_conv = columns_of(results, 1)
+        parts, _ = scatter(columns_of(results, 0))
         stream_three, normed = join_call(stream_two, parts, 1.0, norms[3])
         normed, pack_two = lax.optimization_barrier((normed, pack_two))
 
-        near, far = gather(normed)
-        part_near, (before_near, active_near) = forward_call(near, pack_two)
-        part_far, (before_far, active_far) = forward_call(far, pack_two)
-        saved_four = (
-            chunk_order(near) + chunk_order(far),
-            (before_near, before_far),
-            [active_near, active_far],
-        )
-        parts, _ = scatter(part_near, part_far)
+        groups, results = spread(normed, lambda i, group: forward_call(group, pack_two))
+        saved_four = [chunk_order(groups)] + [columns_of(columns_of(results, 1), i) for i in (0, 1)]
+        parts, _ = scatter(columns_of(results, 0))
         output, grad_four, low, norm_four = turn_call(
             stream_three, parts, 0.5, norms[4], out_grad, lengths
         )
 
-        def feed_backward(low, pack, saved, by_plane):
-            normed, (before_near, before_far), active = saved
-            near, far = gather(low)
-            part_near, grad_near = backward_call(near, pack, before_near)
-            part_far, grad_far = backward_call(far, pack, before_far)
-            rows = chunk_order(near) + chunk_order(far)
+        def feed_backward(low, pack, saved):
+            normed, before, active = saved
+            groups, results = spread(
+                low, lambda i, group: backward_call(group, pack, before[i])
+            )
             term = feed_weight_call(
-                normed, [grad_near, grad_far], active, rows, plane, planes, by_plane
-            )
-            return scatter(part_near, part_far, term)
-
-        parts, (second_term,) = feed_backward(low, pack_two, saved_four, True)
+                normed, columns_of(results, 1), active, chunk_order(groups), planes
+            )
+            return scatter(columns_of(results, 0), term)
+
+        parts, second_term = feed_backward(low, pack_two, saved_four)
         grad_three, low, norm_three = join_back_call(stream_three, grad_four, parts, 1.0, norms[3])
         low, second_term = lax.optimization_barrier((low, second_term))
         second_term = plane_reduce(second_term)
 
-        near, far = gather(low)
-        grad_near, sums_near = batch_back_call(
-            near, team_lengths, 0, conv_near, stats, batch_rows, squares, rows_held
+        def batch_back(i, group):
+            return batch_back_call(
+                group, team_lengths, at[i], saved_three[i][1], stats, batch_rows, squares, rows_held
+            )
+
+        groups, grads = spread(low, batch_back)
+        local_sums = sum(columns_of(grads, 1))
+        sums = outer_sum(local_sums)
+        results = [
+            gate_back_call(
+                len(groups[i][0]), team_lengths, at[i], grads[i][0], saved_three[i][1],
+                saved_three[i][0], stats, sums, squares, taps, tap_count, slots, width,
+            )
+            for i in reversed(range(len(groups)))
+        ][::-1]
+        tap_terms = columns_of(columns_of(results, 1), 1)
+        conv_term = conv_weight_call(
+            normed_three, columns_of(columns_of(results, 1), 0), active_conv, chunk_order(groups),
+            planes,
         )
-        grad_far, sums_far = batch_back_call(
-            far, team_lengths, 2 * k_near, conv_far, stats, batch_rows, squares, rows_held
-        )
-        conv_grads = chunk_order(near) + chunk_order(far)
-        local_sums = sums_near + sums_far
-        sums = outer_sum(local_sums)
-        part_far, (gate_grad_far, taps_far) = gate_back_call(
-            k_far, team_lengths, 2 * k_near, grad_far, conv_far, gates_far, stats, sums, squares, taps,
-            tap_count, slots, width,
-        )
-        part_near, (gate_grad_near, taps_near) = gate_back_call(
-            k_near, team_lengths, 0, grad_near, conv_near, gates_near, stats, sums, squares, taps,
-            tap_count, slots, width,
-        )
-        conv_term = conv_weight_call(
-            normed_three, [gate_grad_near, gate_grad_far], active_conv, conv_grads, plane, planes
-        )
-        parts, conv_term = scatter(part_near, part_far, conv_term)
+        parts, conv_term = scatter(columns_of(results, 0), conv_term)
         grad_two, low, norm_two = join_back_call(stream_two, grad_three, parts, 1.0, norms[2])
         low, conv_term, second_term = lax.optimization_barrier((low, conv_term, second_term))
         conv_term = plane_reduce(conv_term)
 
-        near, far = gather(low)
-        part_near, (qkv_near, place_near, bias_near) = attention_back_call(
-            near, side, squares, mix, rows_held, place, saved_near[0], saved_near[1], head_size
+        def attention_back(i, group):
+            return attention_back_call(
+                group, side, squares, mix, rows_held, place, saved_two[i][0], saved_two[i][1],
+                head_size,
+            )
+
+        groups, results = spread(low, attention_back)
+        mixed, rows = columns_of(saved_two, 2), chunk_order(groups)
+        grads = columns_of(results, 1)
+        bias_terms = columns_of(grads, 2)
+        mix_term = mix_weight_call(
+            normed_two, columns_of(grads, 0), mixed, rows, [table] + columns_of(grads, 1), side,
+            planes, per_side,
         )
-        part_far, (qkv_far, place_far, bias_far) = attention_back_call(
-            far, side, squares, mix, rows_held, place, saved_far[0], saved_far[1], head_size
-        )
-        mixed, rows = [saved_near[2], saved_far[2]], chunk_order(near) + chunk_order(far)
-        mix_term = mix_weight_call(
-            normed_two, [qkv_near, qkv_far], mixed, rows, [table, place_near, place_far], plane,
-            side, planes, per_side,
-        )
-        parts, mix_term = scatter(part_near, part_far, mix_term)
+        parts, mix_term = scatter(columns_of(results, 0), mix_term)
         if not head_aligned:
             mix_own = mm_tn(jnp.concatenate(mixed), jnp.concatenate(rows)).astype(BF16)
             mix_own = lax.dynamic_update_slice_in_dim(
@@ -1637,8 +1639,8 @@
         low, mix_term, conv_term = lax.optimization_barrier((low, mix_term, conv_term))
         mix_term = plane_reduce(mix_term)
 
-        parts, first_term = feed_backward(low, pack_one, saved_one, False)
-        first_term = plane_scatter(first_term)
+        parts, first_term = feed_backward(low, pack_one, saved_one)
+        first_term = plane_reduce(first_term)
         frames_grad, norm_zero = join_back_call(frames, grad_one, parts, 1.0, norms[0], keep=False)
 
         late = (second_term, conv_term, mix_term)
@@ -1665,13 +1667,13 @@
             features = kernel_call(
                 functools.partial(feature_grad_kernel, planes, sides),
                 [shape((team, 12, team_width), F32)],
-                norm_terms + [bias_near, bias_far],
+                norm_terms + bias_terms,
                 scalars=(team_at.reshape(1).astype(jnp.int32),),
             )[0]
             chan_term = kernel_call(
                 functools.partial(channel_grad_kernel, tap_count),
                 [shape((chan_rows, team_width), F32)],
-                [team_swap(features), taps_near, taps_far, local_sums],
+                [team_swap(features), local_sums] + tap_terms,
             )[0]
             chan_grad = finish_channels(chan_term)
             blocks = kernel_call(
@@ -1688,10 +1690,9 @@
                 square_average,
                 scalars=(side,),
             )
-            first_term, square_all, chan_grad, second_up = lax.optimization_barrier(
-                (first_term, square_all, chan_grad, second_up)
-            )
-            first_term = first_term.astype(BF16)
+            first_term, square_all, second_up = lax.optimization_barrier(
+                (first_term, square_all, second_up)
+            )
             down_all = update_call(
                 update_down_kernel,
                 rate_scale,
@@ -1730,26 +1731,26 @@
                 + [side_scatter(join_hidden(block(i))).astype(F32) for i in (4, 5)]
                 + [side_scatter(conv_out_term).astype(F32)]
             )
-            bias_terms = join_heads(
+            bias_rows = join_heads(
                 lax.dynamic_update_slice_in_dim(
-                    jnp.zeros((team, 2, team_width), F32), (bias_near + bias_far)[None], team_at, 0
+                    jnp.zeros((team, 2, team_width), F32), sum(bias_terms)[None], team_at, 0
                 )
             )
             features = jnp.concatenate(
-                [t[0:1] for t in norm_terms] + [t[1:2] for t in norm_terms] + [bias_terms]
+                [t[0:1] for t in norm_terms] + [t[1:2] for t in norm_terms] + [bias_rows]
             )
             features = jnp.sum(team_swap(split_hidden(features)), axis=0)
             chan_grad = finish_channels(
                 jnp.concatenate(
                     [
-                        (taps_near + taps_far)[:tap_count],
+                        sum(tap_terms)[:tap_count],
                         features[:10],
                         local_sums[:2],
                         features[10:],
                     ]
                 )
             )
-            feed_terms = (first_term.astype(BF16), second_term)
+            feed_terms = (first_term, second_term)
             up_grad = jnp.stack(
                 [
                     side_scatter(join_hidden(from_team(rows[:depth], team_hidden))).astype(F32)

time: 567 us -> 510 us (0.90)
  waiting for transfers between devices: 230 us -> 194 us
  starting transfers between devices: 140 us -> 116 us
  other arithmetic: 17.4 us -> 5.32 us
  Pallas kernels: 96.8 us -> 108 us
  local copies, waits for them, and re-layouts: 53.8 us -> 61.4 us
  blocking collectives: 7.13 us -> 0 us
    ppermute x48, waiting for transfers between devices: 145 us -> 83.9 us  [turn(): return lax.ppermute(values, team_axes, pairs)]
    all_gather x2 -> x3, waiting for transfers between devices: 7.18 us -> 32.3 us  [plane_gather(): return lax.all_gather(rows, 'z', axis=0, tiled=False)]
    ppermute x71 -> x70, starting transfers between devices: 50.3 us -> 27.6 us  [swap(): return lax.ppermute(values, axis, [(i, i ^ bit) for i in range(size)])]
    pallas_call x49 -> x84, Pallas kernels: 96.8 us -> 108 us  [kernel_call(): pl.pallas_call(body, out_shape=tuple(outs), in_specs=[pl.BlockSpec(memory...]
    ppermute x71 -> x70, waiting for transfers between devices: 77.7 us -> 67.7 us  [swap(): return lax.ppermute(values, axis, [(i, i ^ bit) for i in range(size)])]
    convert_element_type x16 -> x0, other arithmetic: 9.81 us -> none  [the longest x8 6.81 us: scatter(): second = (own_near[2] + got_near[2].astype(F32)).astype(BF16)]
    all_to_all x6 -> x7, waiting for transfers between devices: 0.02 us -> 7.82 us  [team_swap(): lax.all_to_all(blocks, team_axes, split_axis=0, concat_axis=0, tiled=True)]
    all_to_all x1 -> x0, blocking collectives: 7.13 us -> none  [team_swap(): lax.all_to_all(blocks, team_axes, split_axis=0, concat_axis=0, tiled=True)]
  transfers between devices with their start and end apart: 130 -> 132, of which waited for: 51 -> 73; matrix products, arithmetic and copies ran while one was open for 3% -> 1% of each run, Pallas kernels for 16% -> 20%
where the time goes in v3:
time: 510 us; the launch traced here: 501 us
  waiting for transfers between devices  194 us (38%)
  starting transfers between devices  116 us (23%)
  Pallas kernels  108 us (21%)
  local copies, waits for them, and re-layouts  61.4 us (12%)
  between operations  16.5 us (3%)
  other arithmetic  5.32 us (1%)
    pallas_call x84, Pallas kernels, kernel_call(): pl.pallas_call(body, out_shape=tuple(outs), in_specs=[pl.BlockSpec(memory...  108 us
    ppermute x48, waiting for transfers between devices, turn(): return lax.ppermute(values, team_axes, pairs)  83.9 us
    ppermute x70, waiting for transfers between devices, swap(): return lax.ppermute(values, axis, [(i, i ^ bit) for i in range(size)])  67.7 us
    ppermute x48, starting transfers between devices, turn(): return lax.ppermute(values, team_axes, pairs)  61 us
    unnamed x350, local copies, waits for them, and re-layouts  57.6 us
    all_gather x3, waiting for transfers between devices, plane_gather(): return lax.all_gather(rows, 'z', axis=0, tiled=False)  32.3 us
    ppermute x70, starting transfers between devices, swap(): return lax.ppermute(values, axis, [(i, i ^ bit) for i in range(size)])  27.6 us
    all_to_all x7, starting transfers between devices, team_swap(): lax.all_to_all(blocks, team_axes, split_axis=0, concat_axis=0, tiled=True)  26 us
  transfers between devices with their start and end apart: 132, of which 73 were waited for; matrix products, arithmetic and copies ran while one was open for 1% of the time, Pallas kernels for 20%

profile of v3, /device:TPU:0, one launch (start us, length us, event | category | flops | bytes accessed | tf_op | source)
XLA Modules:
  0.0 501.4 jit_solution(14260345653178919501)
XLA Ops:
  9.4 5.3 %all-to-all-start = ((bf16[8,32,512]{2,1,0:T(8,128)(2,1)}), bf16[8,32,512]{2,1,0:T(8,128)(2,1)S(1)}, u32[]{:S(2)}, u32[]{:S(2)}) async-start(bf16[8,32,512]{2,1,0:T(8,128)(2,1)} %get-tuple-element.319), calls=%async_computation | async-start | bytes 524288 | tf_op jit(solution)/shard_map/all_to_all | solution.py:1350
  15.9 4.9 all-to-all-done.up_ref
  34.1 4.0 collective-permute-done.9
  45.8 4.2 collective-permute-done.10.refs_2_
  57.7 5.1 %collective-permute-done.12.refs_4_ = bf16[8,48,128]{2,1,0:T(8,128)(2,1)S(1)} collective-permute-done((bf16[8,48,128]{2,1,0:T(8,128)(2,1)S(1)}, bf16[8,48,128]{2,1,0:T(8,128)(2,1)S(1)}, u32[]{:S(2)}, u32[]{:S(2)}) %collective-permute-start.12) | collective-permute-done | bytes 98336 | tf_op jit(solution)/shard_map/ppermute | solution.py:44
  67.9 8.4 %all-gather.7.cloned.1.call-done = bf16[2048,512]{1,0:T(8,128)(2,1)} async-done(((bf16[512,512]{1,0:T(8,128)(2,1)}), bf16[2048,512]{1,0:T(8,128)(2,1)}) %all-gather.7.cloned.1.call-update) | async-done | bytes 2097168 | tf_op jit(solution)/shard_map/all_gather | solution.py:1356
  103.8 23.9 %all-gather.9.cloned.1.call-done = bf16[4608,256]{1,0:T(8,128)(2,1)} async-done(((bf16[1152,256]{1,0:T(8,128)(2,1)}), bf16[4608,256]{1,0:T(8,128)(2,1)}) %all-gather.9.cloned.1.call-update) | async-done | bytes 2359312 | tf_op jit(solution)/shard_map/all_gather | solution.py:1356
  138.4 5.0 shard_map.310
  182.1 3.6 collective-permute-done.40.right_ref
  278.2 3.6 collective-permute-done.72.refs_4_
  291.3 4.3 collective-permute-done.74.refs_1_.refs_16_
  298.6 3.8 collective-permute-done.77.refs_1_.refs_20_
  305.0 4.8 collective-permute-done.81
  309.9 5.7 %collective-permute-done.82 = f32[8,128]{1,0:T(8,128)S(1)} collective-permute-done((f32[8,128]{1,0:T(8,128)S(1)}, f32[8,128]{1,0:T(8,128)S(1)}, u32[]{:S(2)}, u32[]{:S(2)}) %collective-permute-start.82) | collective-permute-done | bytes 4128 | tf_op jit(solution)/shard_map/ppermute | solution.py:44
  315.6 4.2 shard_map.349
  342.0 3.9 collective-permute-done.87.refs_4_
  353.6 4.9 shard_map.356
  361.5 7.8 %shard_map.357 = (f32[128,1024]{1,0:T(8,128)S(1)}, f32[128,1024]{1,0:T(8,128)S(1)}, bf16[2,128,1024]{2,1,0:T(8,128)(2,1)}, bf16[512,384]{1,0:T(8,128)(2,1)S(1)},...) custom-call(s32[1]{0:T(128)} %bitcast.3.side_ref.refs_1_.refs_0_, ...), custom_call_target="tpu_custom_call" | custom-call | flops 738197504 | bytes 8979456 | tf_op jit(solution)/shard_map/pallas_call | solution.py:75
  418.4 3.7 shard_map.368
  429.0 4.6 collective-permute-done.114.refs_5_
  450.4 4.6 collective-permute-done.116
  462.1 4.1 collective-permute-done.115.refs_3_
  469.6 3.7 shard_map.373
  477.4 3.6 all-to-all-start.5
  (706 shorter events, 353.2 us)
Async XLA Ops:
  14.8 61.5 %all-gather.7.cloned.1.call-start = ((), (), s32[]{:S(2)}) async-start(), calls=%async_computation.15 | async-start | bytes 2621440 | tf_op jit(solution)/shard_map/all_gather | solution.py:1356
  25.6 24.4 %collective-permute-start.2 = (bf16[128,1024]{1,0:T(8,128)(2,1)S(1)}, bf16[128,1024]{1,0:T(8,128)(2,1)}, u32[]{:S(2)}, u32[]{:S(2)}) collective-permute-start(bf16[128,1024]{1,0:T(8,128)(2,1)S(1)} %copy-done.16), channel_id=1, source_target_pairs={{0,1},{1,0},{2,6},{3,7},{4,5},{5,4},{6,2},{7,3},{8,9},{9,8},{10,14... | collective-permute-start | bytes 786440 | tf_op jit(solution)/shard_map/ppermute | solution.py:1270
  27.1 15.2 %all-to-all-start.2 = ((bf16[8,32,512]{2,1,0:T(8,128)(2,1)}), bf16[8,32,512]{2,1,0:T(8,128)(2,1)S(1)}, u32[]{:S(2)}, u32[]{:S(2)}) async-start(bf16[8,32,512]{2,1,0:T(8,128)(2,1)} %get-tuple-element.338), calls=%async_computation.2 | async-start | bytes 524288 | tf_op jit(solution)/shard_map/all_to_all | solution.py:1350
  32.6 18.0 %collective-permute-start.5 = (bf16[128,1024]{1,0:T(8,128)(2,1)S(1)}, bf16[128,1024]{1,0:T(8,128)(2,1)S(1)}, u32[]{:S(2)}, u32[]{:S(2)}) collective-permute-start(bf16[128,1024]{1,0:T(8,128)(2,1)S(1)} %collective-permute-done.1.refs_0_), channel_id=1, source_target_pairs={{0,1},{1,0},{2,6},{3,7},{4,5},{5,4},{6,2},{7,3},{8,9},{9,8},{10,14... | collective-permute-start | bytes 786440 | tf_op jit(solution)/shard_map/ppermute | solution.py:1270
  38.0 12.0 %collective-permute-start.10 = (bf16[8,48,128]{2,1,0:T(8,128)(2,1)S(1)}, bf16[8,48,128]{2,1,0:T(8,128)(2,1)S(1)}, u32[]{:S(2)}, u32[]{:S(2)}) collective-permute-start(bf16[8,48,128]{2,1,0:T(8,128)(2,1)S(1)} %pad_maximum_fusion.1.refs_1_), channel_id=1, source_target_pairs={{0,8},{8,0},{16,24},{24,16},{1,9},{9,1},{17,25},{25,17},{2,10},{10... | collective-permute-start | bytes 294920 | tf_op jit(solution)/shard_map/ppermute | solution.py:44
  39.7 28.2 %collective-permute-start = (bf16[128,1024]{1,0:T(8,128)(2,1)S(1)}, bf16[128,1024]{1,0:T(8,128)(2,1)S(1)}, u32[]{:S(2)}, u32[]{:S(2)}) collective-permute-start(bf16[128,1024]{1,0:T(8,128)(2,1)S(1)} %copy-done.16), channel_id=1, source_target_pairs={{0,2},{2,0},{1,3},{3,1},{4,6},{6,4},{5,7},{7,5},{8,10},{10,8},{9,1... | collective-permute-start | bytes 786440 | tf_op jit(solution)/shard_map/ppermute | solution.py:44
  39.7 13.7 %collective-permute-start.11 = (bf16[8,48,128]{2,1,0:T(8,128)(2,1)S(1)}, bf16[8,48,128]{2,1,0:T(8,128)(2,1)S(1)}, u32[]{:S(2)}, u32[]{:S(2)}) collective-permute-start(bf16[8,48,128]{2,1,0:T(8,128)(2,1)S(1)} %pad_maximum_fusion.1.refs_1_), channel_id=1, source_target_pairs={{0,16},{8,24},{16,0},{24,8},{1,17},{9,25},{17,1},{25,9},{2,18},{10... | collective-permute-start | bytes 294920 | tf_op jit(solution)/shard_map/ppermute | solution.py:44
  42.3 24.6 %all-to-all-start.1 = ((bf16[8,32,768]{2,1,0:T(8,128)(2,1)}), bf16[8,32,768]{2,1,0:T(8,128)(2,1)S(1)}, u32[]{:S(2)}, u32[]{:S(2)}) async-start(bf16[8,32,768]{2,1,0:T(8,128)(2,1)} %get-tuple-element.335), calls=%async_computation.1 | async-start | bytes 786432 | tf_op jit(solution)/shard_map/all_to_all | solution.py:1350
  45.8 81.9 %all-gather.9.cloned.1.call-start = ((), (), s32[]{:S(2)}) async-start(), calls=%async_computation.16 | async-start | bytes 2949120 | tf_op jit(solution)/shard_map/all_gather | solution.py:1356
  50.0 17.8 %collective-permute-start.3 = (bf16[128,1024]{1,0:T(8,128)(2,1)S(1)}, bf16[128,1024]{1,0:T(8,128)(2,1)}, u32[]{:S(2)}, u32[]{:S(2)}) collective-permute-start(bf16[128,1024]{1,0:T(8,128)(2,1)S(1)} %collective-permute-done.1.refs_0_), channel_id=1, source_target_pairs={{0,2},{2,0},{1,3},{3,1},{4,6},{6,4},{5,7},{7,5},{8,10},{10,8},{9,1... | collective-permute-start | bytes 786440 | tf_op jit(solution)/shard_map/ppermute | solution.py:44
  50.0 17.8 %collective-permute-start.4 = (bf16[128,1024]{1,0:T(8,128)(2,1)}, bf16[128,1024]{1,0:T(8,128)(2,1)}, u32[]{:S(2)}, u32[]{:S(2)}) collective-permute-start(bf16[128,1024]{1,0:T(8,128)(2,1)} %collective-permute-done.2.refs_1_), channel_id=1, source_target_pairs={{0,2},{2,0},{1,3},{3,1},{4,6},{6,4},{5,7},{7,5},{8,10},{10,8},{9,1... | collective-permute-start | bytes 786440 | tf_op jit(solution)/shard_map/ppermute | solution.py:44
  50.5 17.3 %collective-permute-start.6 = (bf16[128,1024]{1,0:T(8,128)(2,1)S(1)}, bf16[128,1024]{1,0:T(8,128)(2,1)S(1)}, u32[]{:S(2)}, u32[]{:S(2)}) collective-permute-start(bf16[128,1024]{1,0:T(8,128)(2,1)S(1)} %collective-permute-done.5.refs_0_), channel_id=1, source_target_pairs={{0,2},{2,0},{1,3},{3,1},{4,6},{6,4},{5,7},{7,5},{8,10},{10,8},{9,1... | collective-permute-start | bytes 786440 | tf_op jit(solution)/shard_map/ppermute | solution.py:44
  76.3 131.7 %all-gather.11.cloned.1.call-start = ((), (), s32[]{:S(2)}) async-start(), calls=%async_computation.17 | async-start | bytes 2621440 | tf_op jit(solution)/shard_map/all_gather | solution.py:1356
  100.6 29.1 %collective-permute-start.22 = (bf16[128,1024]{1,0:T(8,128)(2,1)}, bf16[128,1024]{1,0:T(8,128)(2,1)}, u32[]{:S(2)}, u32[]{:S(2)}) collective-permute-start(bf16[128,1024]{1,0:T(8,128)(2,1)} %get-tuple-element.361.refs_2_.refs_1_), channel_id=1, source_target_pairs={{0,2},{2,0},{1,3},{3,1},{4,6},{6,4},{5,7},{7,5},{8,10},{10,8},{9,1... | collective-permute-start | bytes 786440 | tf_op jit(solution)/shard_map/ppermute | solution.py:44
  100.6 35.6 %collective-permute-start.20 = (bf16[128,1024]{1,0:T(8,128)(2,1)}, bf16[128,1024]{1,0:T(8,128)(2,1)S(1)}, u32[]{:S(2)}, u32[]{:S(2)}) collective-permute-start(bf16[128,1024]{1,0:T(8,128)(2,1)} %get-tuple-element.361.refs_2_.refs_1_), channel_id=1, source_target_pairs={{0,4},{1,5},{2,3},{3,2},{4,0},{5,1},{6,7},{7,6},{8,12},{9,13},{10,... | collective-permute-start | bytes 786440 | tf_op jit(solution)/shard_map/ppermute | solution.py:1270
  102.1 34.1 %collective-permute-start.21 = (bf16[128,1024]{1,0:T(8,128)(2,1)}, bf16[128,1024]{1,0:T(8,128)(2,1)}, u32[]{:S(2)}, u32[]{:S(2)}) collective-permute-start(bf16[128,1024]{1,0:T(8,128)(2,1)} %get-tuple-element.361.refs_2_.refs_1_), channel_id=1, source_target_pairs={{0,1},{1,0},{2,6},{3,7},{4,5},{5,4},{6,2},{7,3},{8,9},{9,8},{10,14... | collective-permute-start | bytes 786440 | tf_op jit(solution)/shard_map/ppermute | solution.py:1270
  103.6 245.7 %reduce-scatter.5.cloned.1.call-start = ((), (), s32[]{:S(2)}) async-start(), calls=%async_computation.11 | async-start | bytes 2621440 | tf_op jit(solution)/shard_map/reduce_scatter | solution.py:1359
  285.9 109.9 %reduce-scatter.7.cloned.1.call-start = ((), (), s32[]{:S(2)}) async-start(), calls=%async_computation.12 | async-start | bytes 983040 | tf_op jit(solution)/shard_map/reduce_scatter | solution.py:1359
  321.3 12.0 %collective-permute-start.84 = (bf16[2,128,1024]{2,1,0:T(8,128)(2,1)}, bf16[2,128,1024]{2,1,0:T(8,128)(2,1)}, u32[]{:S(2)}, u32[]{:S(2)}) collective-permute-start(bf16[2,128,1024]{2,1,0:T(8,128)(2,1)} %get-tuple-element.491), channel_id=1, source_target_pairs={{0,2},{2,0},{1,3},{3,1},{4,6},{6,4},{5,7},{7,5},{8,10},{10,8},{9,1... | collective-permute-start | bytes 1572872 | tf_op jit(solution)/shard_map/ppermute | solution.py:44
  351.4 88.9 %reduce-scatter.9.cloned.1.call-start = ((), (), s32[]{:S(2)}) async-start(), calls=%async_computation.13 | async-start | bytes 1966080 | tf_op jit(solution)/shard_map/reduce_scatter | solution.py:1359
  395.8 79.9 %reduce-scatter.11.cloned.1.call-start = ((), (), s32[]{:S(2)}) async-start(), calls=%async_computation.14 | async-start | bytes 2621440 | tf_op jit(solution)/shard_map/reduce_scatter | solution.py:1359
  448.4 17.7 %collective-permute-start.115 = (bf16[768,256]{1,0:T(8,128)(2,1)}, bf16[768,256]{1,0:T(8,128)(2,1)}, u32[]{:S(2)}, u32[]{:S(2)}) collective-permute-start(bf16[768,256]{1,0:T(8,128)(2,1)} %bitcast.11.mix_ref.refs_2_), channel_id=1, source_target_pairs={{0,1},{1,0},{2,3},{3,2},{4,5},{5,4},{6,7},{7,6},{8,9},{9,8},{10,11... | collective-permute-start | bytes 1179656 | tf_op jit(solution)/shard_map/ppermute | solution.py:44
  455.8 17.5 %all-to-all-start.4 = ((bf16[8,32,512]{2,1,0:T(8,128)(2,1)}), bf16[8,32,512]{2,1,0:T(8,128)(2,1)S(1)}, u32[]{:S(2)}, u32[]{:S(2)}) async-start(bf16[8,32,512]{2,1,0:T(8,128)(2,1)} %bitcast.13), calls=%async_computation.8 | async-start | bytes 524288 | tf_op jit(solution)/shard_map/all_to_all | solution.py:1350
  477.4 12.1 %all-to-all-start.5 = ((bf16[8,32,512]{2,1,0:T(8,128)(2,1)}), bf16[8,32,512]{2,1,0:T(8,128)(2,1)S(1)}, u32[]{:S(2)}, u32[]{:S(2)}) async-start(bf16[8,32,512]{2,1,0:T(8,128)(2,1)} %bitcast.14), calls=%async_computation.9 | async-start | bytes 524288 | tf_op jit(solution)/shard_map/all_to_all | solution.py:1350
  (283 other events, 1763.4 us)
Sparse Core Ops, SparseCore 0:
  21.8 54.4 all-gather.6
  78.4 49.2 all-gather.8
  129.9 44.7 all-gather.10
  286.0 41.9 reduce-scatter.4
  351.5 21.5 reduce-scatter.6
  395.9 33.5 reduce-scatter.8
  431.8 43.8 reduce-scatter.10

commit v4 on v3

--- a/solution.py
+++ b/solution.py
@@ -106,7 +106,8 @@
 
 def down_blocks(ref, width):
     planes, hidden = ref.shape[0], ref.shape[2]
-    depth, rows = width // planes, hidden // planes
+    rows = hidden // planes
+    depth = ref.shape[1] - rows * (width // hidden)
     return [
         jnp.concatenate(
             [ref[p, depth + b * rows : depth + (b + 1) * rows, :] for p in range(planes)]
@@ -156,95 +157,98 @@
     )
 
 
-def output_rows(ref, p, width, size, mix, conv, want_mix):
-    base = (6 * size // BLOCK) * (width // ref.shape[0])
+def output_rows(ref, p, width, base):
+    blocks = width // BLOCK
+    rows = (ref.shape[1] - base) // blocks
     parts = []
-    for b in range(width // BLOCK):
-        at = base + b * (mix + conv) + (0 if want_mix else mix)
-        rows = ref[pl.ds(p, 1), at : at + (mix if want_mix else conv), :]
-        parts.append(rows.reshape(rows.shape[1:]))
+    for b in range(blocks):
+        at = base + b * rows
+        part = ref[pl.ds(p, 1), at : at + rows, :]
+        parts.append(part.reshape(part.shape[1:]))
     return jnp.concatenate(parts, axis=1)
 
 
-def forward_kernel(k, with_norm, *refs):
+def forward_kernel(k, packs, with_norm, *refs):
     mine, mate, refs = refs[:k], refs[k : 2 * k], refs[2 * k :]
     if with_norm:
         norm_ref, refs = refs[0], refs[1:]
-    pack_ref, refs = refs[0], refs[1:]
-    out_mine, out_mate, before_ref, active_ref = refs[:k], refs[k], refs[k + 1], refs[k + 2]
+    up_ref, down_ref, refs = refs[0], refs[packs - 1], refs[packs:]
+    out_mine, out_mate, before_ref = refs[:k], refs[k], refs[k + 1]
     slots, width = mine[0].shape
-    blocks = down_blocks(pack_ref, width)
+    blocks = down_blocks(down_ref, width)
     for i in range(k):
         rows = jnp.concatenate([mine[i][...], mate[i][...]])
         at = pl.ds(2 * i * slots, 2 * slots)
         if with_norm:
             unit, _ = normalize(rows.astype(F32))
             rows = (unit * norm_ref[0:1, :] + norm_ref[1:2, :]).astype(BF16)
-            refs[k + 3][at, :] = rows
-        before = up_product(rows, pack_ref)
+            refs[k + 2][at, :] = rows
+        before = up_product(rows, up_ref)
         before_ref[at, :] = before
         active = (before * sigmoid(before)).astype(BF16)
-        active_ref[at, :] = active
         store_partial(out_mine, out_mate, i, slots, down_product(active, blocks))
 
 
-def forward_call(pieces, pack, norm=None):
-    mine, mate = pieces
+def forward_call(group, packs, norm=None):
+    mine, mate = group
     k, (slots, width) = len(mine), mine[0].shape
-    hidden = pack.shape[2]
+    hidden = packs[0].shape[2]
     rows = 2 * k * slots
     outs = [shape((slots, width), F32)] * k + [
         shape((k, slots, width), BF16),
         shape((rows, hidden), F32),
-        shape((rows, hidden), BF16),
     ]
     args = list(mine) + list(mate)
     if norm is not None:
         outs.append(shape((rows, width), BF16))
         args.append(norm)
     result = kernel_call(
-        functools.partial(forward_kernel, k, norm is not None),
+        functools.partial(forward_kernel, k, len(packs), norm is not None),
         outs,
-        args + [pack],
+        args + list(packs),
         flops=4 * rows * width * hidden,
     )
     return (result[:k], result[k]), result[k + 1 :]
 
 
-def backward_kernel(k, *refs):
+def backward_kernel(k, packs, *refs):
     mine, mate, refs = refs[:k], refs[k : 2 * k], refs[2 * k :]
-    pack_ref, before_ref, refs = refs[0], refs[1], refs[2:]
-    out_mine, out_mate, grad_ref = refs[:k], refs[k], refs[k + 1]
+    up_ref, down_ref, before_ref, refs = refs[0], refs[packs - 1], refs[packs], refs[packs + 1 :]
+    out_mine, out_mate, grad_ref, active_ref = refs[:k], refs[k], refs[k + 1], refs[k + 2]
     slots, width = mine[0].shape
-    blocks = down_blocks(pack_ref, width)
+    blocks = down_blocks(down_ref, width)
     for i in range(k):
         at = pl.ds(2 * i * slots, 2 * slots)
         rows = jnp.concatenate([mine[i][...], mate[i][...]])
-        grad = down_product_back(rows, blocks) * swish_grad(before_ref[at, :])
+        before = before_ref[at, :]
+        sig = sigmoid(before)
+        active_ref[at, :] = (before * sig).astype(BF16)
+        grad = down_product_back(rows, blocks) * (sig * (1.0 + before * (1.0 - sig)))
         grad = grad.astype(BF16)
         grad_ref[at, :] = grad
-        store_partial(out_mine, out_mate, i, slots, up_product_back(grad, pack_ref, width))
-
-
-def backward_call(pieces, pack, before):
-    mine, mate = pieces
+        store_partial(out_mine, out_mate, i, slots, up_product_back(grad, up_ref, width))
+
+
+def backward_call(group, packs, before):
+    mine, mate = group
     k, (slots, width) = len(mine), mine[0].shape
     rows, hidden = before.shape
     outs = [shape((slots, width), F32)] * k + [
         shape((k, slots, width), BF16),
         shape((rows, hidden), BF16),
+        shape((rows, hidden), BF16),
     ]
     result = kernel_call(
-        functools.partial(backward_kernel, k),
+        functools.partial(backward_kernel, k, len(packs)),
         outs,
-        list(mine) + list(mate) + [pack, before],
+        list(mine) + list(mate) + list(packs) + [before],
         flops=4 * rows * width * hidden,
     )
-    return (result[:k], result[k]), result[k + 1]
-
-
-def joined(refs):
-    return jnp.concatenate([r[...] for r in refs])
+    return (result[:k], result[k]), result[k + 1 :]
+
+
+def joined(refs, first=0, last=None):
+    return jnp.concatenate([r[:, first:last] for r in refs])
 
 
 def take(refs, counts):
@@ -341,18 +345,20 @@
 
 def mix_weight_kernel(counts, planes, per_side, *refs):
     side_ref, refs = refs[0], refs[1:]
-    normed, grads, mixed, rows, place, refs = take(refs, counts)
+    saved, grads, rows, place, refs = take(refs, counts)
     table_ref, place = place[0], place[1:]
     out_ref, total_ref, row_ref = refs
+    size = row_ref.shape[0]
     depth = total_ref.shape[0] // planes
     base = (total_ref.shape[1] // BLOCK) * depth
     right = joined(grads)
     qkv = right.shape[1]
-    total_ref[:, :qkv] = mm_tn(joined(normed), right)
+    total_ref[:, :qkv] = mm_tn(joined(saved, 0, total_ref.shape[0]), right)
     position = sum(ref[...] for ref in place)
     total_ref[:, qkv:] = mm_tn(table_ref[...], position.astype(BF16))
     if per_side:
-        row_ref[...] = mm_tn(joined(mixed), joined(rows))
+        last = saved[0].shape[1]
+        row_ref[...] = mm_tn(joined(saved, last - size, last), joined(rows))
 
     def write(out, p):
         write_columns(out, total_ref, p, depth)
@@ -367,13 +373,13 @@
     put(out_ref, planes, write)
 
 
-def mix_weight_call(normed, grads, mixed, rows, place, side, planes, per_side):
-    width, qkv, size = normed[0].shape[1], grads[0].shape[1], mixed[0].shape[1]
+def mix_weight_call(saved, grads, rows, place, side, planes, per_side):
+    width, qkv, size = rows[0].shape[1], grads[0].shape[1], grads[0].shape[1] // 3
     total = qkv + size
     lines = (total // BLOCK) * (width // planes)
     if per_side:
         lines += (width // BLOCK) * (size // per_side)
-    groups = (normed, grads, mixed, rows, place)
+    groups = (saved, grads, rows, place)
     tokens = sum(a.shape[0] for a in grads)
     return kernel_call(
         functools.partial(mix_weight_kernel, [len(g) for g in groups], planes, per_side),
@@ -475,43 +481,46 @@
     ]
 
 
-def attention_kernel(k, first, head_size, rows_held, *refs):
+def saved_lanes(width, size, heads, slots):
+    ends = [width]
+    for lanes in [size] * 4 + [slots] * heads + [size]:
+        ends.append(ends[-1] + lanes)
+    return ends
+
+
+def attention_kernel(k, first, head_size, per_side, *refs):
     length_ref, side_ref, refs = refs[0], refs[1], refs[2:]
     mine, mate, refs = refs[:k], refs[k : 2 * k], refs[2 * k :]
-    column_ref, mix_ref, bias_ref, place_ref, refs = refs[0], refs[1], refs[2], refs[3], refs[4:]
-    out_mine, out_mate, saved_ref, probs_ref, mixed_ref = (
-        refs[:k],
-        refs[k],
-        refs[k + 1],
-        refs[k + 2],
-        refs[k + 3],
-    )
+    bias_ref, place_ref, pack_ref = refs[:3]
+    mix_ref, refs = (None, refs[3:]) if per_side else (refs[3], refs[4:])
+    out_mine, out_mate, saved_ref = refs[:k], refs[k], refs[k + 1]
     slots, width = mine[0].shape
     size = place_ref.shape[1]
-    mix = mix_rows(mix_ref, side_ref, width, size, rows_held)
+    ends = saved_lanes(width, size, size // head_size, slots)
+    mix = mix_rows(pack_ref, mix_ref, side_ref, width, size, per_side)
     scale = head_size ** (-0.5)
     row_at = lax.broadcasted_iota(jnp.int32, (slots, slots), 0)
     column_at = lax.broadcasted_iota(jnp.int32, (slots, slots), 1)
     masks = head_masks(slots, head_size)
     for i in range(k):
         rows = jnp.concatenate([mine[i][...], mate[i][...]])
-        qkv = square_product(rows, column_ref, 0, 3 * size)
+        qkv = square_product(rows, pack_ref, 0, 3 * size)
         query = qkv[:, :size]
         query_c = (query + bias_ref[0:1, :]).astype(BF16)
         query_p = (query + bias_ref[1:2, :]).astype(BF16)
         key = qkv[:, size : 2 * size].astype(BF16)
         value = qkv[:, 2 * size :].astype(BF16)
         at = pl.ds(2 * i * slots, 2 * slots)
-        saved_ref[at, 0:size] = query_c
-        saved_ref[at, size : 2 * size] = query_p
-        saved_ref[at, 2 * size : 3 * size] = key
-        saved_ref[at, 3 * size : 4 * size] = value
+        saved_ref[at, : ends[0]] = rows
+        for n, part in enumerate((query_c, query_p, key, value)):
+            saved_ref[at, ends[n] : ends[n + 1]] = part
         halves = []
         for j in range(2):
             b = 2 * i + j
             part = slice(j * slots, (j + 1) * slots)
-            ends = item_bounds(length_ref, first + b)
-            same = item_index(ends, row_at) == item_index(ends, column_at)
+            rows_of = pl.ds(b * slots, slots)
+            edges = item_bounds(length_ref, first + b)
+            same = item_index(edges, row_at) == item_index(edges, column_at)
             blocks = []
             for lo in range(0, size, LANES):
                 lanes = slice(lo, lo + LANES)
@@ -526,60 +535,51 @@
                     top = jnp.max(scores, axis=-1, keepdims=True)
                     weights = jnp.exp(scores - top)
                     probs = weights / jnp.sum(weights, axis=-1, keepdims=True)
-                    probs_ref[b, (lo // LANES) * len(masks) + h] = probs
-                    mixed = jnp.where(mask, mm(probs.astype(BF16), value[part, lanes]), mixed)
+                    probs = probs.astype(BF16)
+                    n = 4 + (lo // LANES) * len(masks) + h
+                    saved_ref[rows_of, ends[n] : ends[n + 1]] = probs
+                    mixed = jnp.where(mask, mm(probs, value[part, lanes]), mixed)
                 blocks.append(mixed)
             halves.append(jnp.concatenate(blocks, axis=1) if len(blocks) > 1 else blocks[0])
         mixed = jnp.concatenate(halves).astype(BF16)
-        mixed_ref[at, :] = mixed
+        saved_ref[at, ends[-2] : ends[-1]] = mixed
         store_partial(out_mine, out_mate, i, slots, mm(mixed, mix))
 
 
-def mix_rows(mix_ref, side_ref, width, size, rows_held):
-    per_side, mix, conv = rows_held
+def mix_rows(pack_ref, mix_ref, side_ref, width, size, per_side):
     if not per_side:
         return mix_ref[...]
+    base = (4 * size // BLOCK) * (width // pack_ref.shape[0])
     return jnp.concatenate(
-        [
-            output_rows(mix_ref, side_ref[0] * per_side + h, width, size, mix, conv, True)
-            for h in range(per_side)
-        ]
-    )
-
-
-def attention_call(pieces, lengths, first, side, columns, mix, rows_held, bias, place, head_size):
-    mine, mate = pieces
+        [output_rows(pack_ref, side_ref[0] * per_side + h, width, base) for h in range(per_side)]
+    )
+
+
+def attention_call(group, lengths, first, side, packs, per_side, bias, place, head_size):
+    mine, mate = group
     k, (slots, width) = len(mine), mine[0].shape
     size = place.shape[1]
     heads = size // head_size
     rows = 2 * k * slots
     outs = [shape((slots, width), F32)] * k + [
         shape((k, slots, width), BF16),
-        shape((rows, 4 * size), BF16),
-        shape((2 * k, heads, slots, slots), F32),
-        shape((rows, size), BF16),
+        shape((rows, saved_lanes(width, size, heads, slots)[-1]), BF16),
     ]
     result = kernel_call(
-        functools.partial(attention_kernel, k, first, head_size, rows_held),
+        functools.partial(attention_kernel, k, first, head_size, per_side),
         outs,
-        list(mine) + list(mate) + [columns, mix, bias, place],
+        list(mine) + list(mate) + [bias, place] + list(packs),
         scalars=(lengths, side),
         flops=2 * rows * width * size * 4 + 2 * k * heads * 10 * slots * slots * LANES,
     )
-    return (result[:k], result[k]), result[k + 1 :]
-
-
-def attention_back_kernel(k, head_size, rows_held, *refs):
+    return (result[:k], result[k]), result[k + 1]
+
+
+def attention_back_kernel(k, head_size, per_side, *refs):
     side_ref, refs = refs[0], refs[1:]
     mine, mate, refs = refs[:k], refs[k : 2 * k], refs[2 * k :]
-    column_ref, mix_ref, place_ref, saved_ref, probs_ref, refs = (
-        refs[0],
-        refs[1],
-        refs[2],
-        refs[3],
-        refs[4],
-        refs[5:],
-    )
+    place_ref, saved_ref, pack_ref = refs[:3]
+    mix_ref, refs = (None, refs[3:]) if per_side else (refs[3], refs[4:])
     out_mine, out_mate, grad_ref, place_grad_ref, bias_ref = (
         refs[:k],
         refs[k],
@@ -589,7 +589,8 @@
     )
     slots, width = mine[0].shape
     size = place_ref.shape[1]
-    mix = mix_rows(mix_ref, side_ref, width, size, rows_held)
+    mix = mix_rows(pack_ref, mix_ref, side_ref, width, size, per_side)
+    ends = saved_lanes(width, size, size // head_size, slots)
     scale = head_size ** (-0.5)
     masks = head_masks(slots, head_size)
     flip = (
@@ -612,19 +613,20 @@
             for lo in range(0, size, LANES):
                 lanes = slice(lo, lo + LANES)
                 grad_mixed = grad_mixed_all[part, lanes]
-                query_c = saved_ref[rows_at, lo : lo + LANES]
-                query_p = saved_ref[rows_at, size + lo : size + lo + LANES]
-                key = saved_ref[rows_at, 2 * size + lo : 2 * size + lo + LANES]
-                value = saved_ref[rows_at, 3 * size + lo : 3 * size + lo + LANES]
+                query_c, query_p, key, value = [
+                    saved_ref[rows_at, ends[n] + lo : ends[n] + lo + LANES] for n in range(4)
+                ]
                 place = place_ref[:, lanes]
                 gqc = jnp.zeros((slots, LANES), F32)
                 gqp, gk, gv = gqc, gqc, gqc
                 place_grad = jnp.zeros(place.shape, F32)
                 for h, mask in enumerate(masks):
-                    probs = probs_ref[b, (lo // LANES) * len(masks) + h]
+                    n = 4 + (lo // LANES) * len(masks) + h
+                    probs = saved_ref[rows_at, ends[n] : ends[n + 1]]
                     own = jnp.where(mask, grad_mixed, 0)
                     grad_probs = mm_nt(own, value)
-                    gv = gv + mm_tn(probs.astype(BF16), own)
+                    gv = gv + mm_tn(probs, own)
+                    probs = probs.astype(F32)
                     inner = jnp.sum(probs * grad_probs, axis=-1, keepdims=True)
                     grad = (probs * (grad_probs - inner)).astype(BF16) * scale
                     grad = grad.astype(BF16)
@@ -658,12 +660,12 @@
             )
         grad = jnp.concatenate(halves)
         grad_ref[at, :] = grad
-        store_partial(out_mine, out_mate, i, slots, square_product_back(grad, column_ref, width, 0, 3 * size))
+        store_partial(out_mine, out_mate, i, slots, square_product_back(grad, pack_ref, width, 0, 3 * size))
     bias_ref[...] = jnp.concatenate([bias_c, bias_p])
 
 
-def attention_back_call(pieces, side, columns, mix, rows_held, place, saved, probs, head_size):
-    mine, mate = pieces
+def attention_back_call(group, side, packs, per_side, place, saved, head_size):
+    mine, mate = group
     k, (slots, width) = len(mine), mine[0].shape
     size = place.shape[1]
     rows = 2 * k * slots
@@ -674,9 +676,9 @@
         shape((2, size), F32),
     ]
     result = kernel_call(
-        functools.partial(attention_back_kernel, k, head_size, rows_held),
+        functools.partial(attention_back_kernel, k, head_size, per_side),
         outs,
-        list(mine) + list(mate) + [columns, mix, place, saved, probs],
+        list(mine) + list(mate) + [place, saved] + list(packs),
         scalars=(side,),
         flops=2 * rows * width * size * 4 + 2 * k * 24 * slots * slots * size,
     )
@@ -703,7 +705,7 @@
 def gate_kernel(k, first, tap_count, *refs):
     length_ref, refs = refs[0], refs[1:]
     mine, mate, refs = refs[:k], refs[k : 2 * k], refs[2 * k :]
-    column_ref, tap_ref, gate_ref, conv_ref, stat_ref, pad_ref = refs
+    pack_ref, tap_ref, gate_ref, normed_ref, stat_ref, pad_ref = refs
     slots, _ = mine[0].shape
     size = tap_ref.shape[1]
     reach = tap_count // 2
@@ -713,8 +715,9 @@
     total = jnp.zeros((1, size), F32)
     for i in range(k):
         rows = jnp.concatenate([mine[i][...], mate[i][...]])
-        gates = square_product(rows, column_ref, 4 * size, 6 * size)
-        gate_ref[pl.ds(2 * i * slots, 2 * slots), :] = gates
+        gates = square_product(rows, pack_ref, 0, 2 * size)
+        gate_ref[pl.ds(2 * i * slots, 2 * slots), : 2 * size] = gates
+        normed_ref[pl.ds(2 * i * slots, 2 * slots), :] = rows
         glu = gates[:, :size] * sigmoid(gates[:, size:])
         for j in range(2):
             b = 2 * i + j
@@ -729,46 +732,56 @@
                 elif o > 0:
                     near = jnp.where(behind >= o, near, 0.0)
                 conv = conv + near * tap_ref[tap : tap + 1, :]
-            conv_ref[pl.ds(b * slots, slots), :] = conv
+            gate_ref[pl.ds(b * slots, slots), 2 * size :] = conv
             count = count + jnp.sum(valid, axis=0, keepdims=True)
             total = total + jnp.sum(conv * valid, axis=0, keepdims=True)
     mean = total / count
     spread = jnp.zeros((1, size), F32)
     for b in range(2 * k):
         valid = (row_at < item_bounds(length_ref, first + b)[-1]).astype(F32)
-        gap = (conv_ref[pl.ds(b * slots, slots), :] - mean) * valid
+        gap = (gate_ref[pl.ds(b * slots, slots), 2 * size :] - mean) * valid
         spread = spread + jnp.sum(gap * gap, axis=0, keepdims=True)
     stat_ref[...] = jnp.concatenate([count, mean, spread, jnp.zeros((5, size), F32)])
 
 
-def gate_call(pieces, lengths, first, columns, taps, tap_count):
-    mine, mate = pieces
+def gate_call(group, lengths, first, pack, taps, tap_count):
+    mine, mate = group
     k, (slots, width) = len(mine), mine[0].shape
     size = taps.shape[1]
     rows = 2 * k * slots
     return kernel_call(
         functools.partial(gate_kernel, k, first, tap_count),
-        [shape((rows, 2 * size), F32), shape((rows, size), F32), shape((8, size), F32)],
-        list(mine) + list(mate) + [columns, taps],
+        [shape((rows, 3 * size), F32), shape((rows, width), BF16), shape((8, size), F32)],
+        list(mine) + list(mate) + [pack, taps],
         scalars=(lengths,),
         flops=4 * rows * width * size + 40 * tap_count * rows * size,
         scratch=[pltpu.VMEM((slots + 2 * PAD, size), F32)],
     )
 
 
-def merge_kernel(left_ref, right_ref, out_ref):
-    n_left, n_right = left_ref[0:1, :], right_ref[0:1, :]
-    m_left, m_right = left_ref[1:2, :], right_ref[1:2, :]
-    count = n_left + n_right
-    gap = m_right - m_left
-    mean = (n_left * m_left + n_right * m_right) / count
-    spread = left_ref[2:3, :] + right_ref[2:3, :] + gap * gap * (n_left * n_right / count)
-    size = left_ref.shape[1]
-    out_ref[...] = jnp.concatenate([count, mean, spread, jnp.zeros((5, size), F32)])
-
-
-def merge(left, right):
-    return kernel_call(merge_kernel, [shape(left.shape, F32)], [left, right])[0]
+def merge_kernel(*refs):
+    out_ref = refs[-1]
+    count, mean, spread = refs[0][0:1, :], refs[0][1:2, :], refs[0][2:3, :]
+    for ref in refs[1:-1]:
+        more = ref[0:1, :]
+        total = count + more
+        gap = ref[1:2, :] - mean
+        spread = spread + ref[2:3, :] + gap * gap * (count * more / total)
+        mean = (count * mean + more * ref[1:2, :]) / total
+        count = total
+    out_ref[...] = jnp.concatenate([count, mean, spread, jnp.zeros((5, mean.shape[1]), F32)])
+
+
+def merge(parts):
+    return kernel_call(merge_kernel, [shape(parts[0].shape, F32)], parts)[0]
+
+
+def sum_kernel(*refs):
+    refs[-1][...] = sum(ref[...] for ref in refs[:-1])
+
+
+def sum_call(parts):
+    return kernel_call(sum_kernel, [shape(parts[0].shape, F32)], parts)[0]
 
 
 def batch_unit(conv, stat_ref):
@@ -776,55 +789,52 @@
     return (conv - stat_ref[1:2, :]) * inverse, inverse
 
 
-def batch_kernel(k, rows_held, *refs):
-    conv_ref, stat_ref, batch_ref, out_weight_ref, refs = (
-        refs[0],
-        refs[1],
-        refs[2],
-        refs[3],
-        refs[4:],
-    )
-    out_mine, out_mate, active_ref = refs[:k], refs[k], refs[k + 1]
+def batch_kernel(k, *refs):
+    gate_ref, stat_ref, batch_ref, pack_ref, refs = refs[0], refs[1], refs[2], refs[3], refs[4:]
+    out_mine, out_mate = refs[:k], refs[k]
     slots, width = out_mine[0].shape
-    weight = conv_rows(out_weight_ref, width, active_ref.shape[1], rows_held)
+    size = batch_ref.shape[1]
+    weight = conv_rows(pack_ref, width, size)
     for i in range(k):
         at = pl.ds(2 * i * slots, 2 * slots)
-        unit, _ = batch_unit(conv_ref[at, :], stat_ref)
+        unit, _ = batch_unit(gate_ref[at, 2 * size :], stat_ref)
         value = unit * batch_ref[0:1, :] + batch_ref[1:2, :]
         active = (value * sigmoid(value)).astype(BF16)
-        active_ref[at, :] = active
         store_partial(out_mine, out_mate, i, slots, mm(active, weight))
 
 
-def conv_rows(ref, width, size, rows_held):
-    _, mix, conv = rows_held
-    return jnp.concatenate(
-        [output_rows(ref, p, width, size, mix, conv, False) for p in range(ref.shape[0])]
-    )
-
-
-def batch_call(k, conv, stats, batch_rows, out_weight, rows_held, slots, width):
-    size = conv.shape[1]
-    outs = [shape((slots, width), F32)] * k + [
-        shape((k, slots, width), BF16),
-        shape(conv.shape, BF16),
-    ]
+def conv_rows(pack_ref, width, size):
+    planes = pack_ref.shape[0]
+    base = (2 * size // BLOCK) * (width // planes)
+    rows = size // planes
+    parts = []
+    for p in range(planes):
+        blocks = [
+            pack_ref[p, base + b * rows : base + (b + 1) * rows, :] for b in range(width // BLOCK)
+        ]
+        parts.append(jnp.concatenate(blocks, axis=1))
+    return jnp.concatenate(parts)
+
+
+def batch_call(k, gates, stats, batch_rows, pack, slots, width):
+    rows, size = gates.shape[0], batch_rows.shape[1]
+    outs = [shape((slots, width), F32)] * k + [shape((k, slots, width), BF16)]
     result = kernel_call(
-        functools.partial(batch_kernel, k, rows_held),
+        functools.partial(batch_kernel, k),
         outs,
-        [conv, stats, batch_rows, out_weight],
-        flops=2 * conv.shape[0] * width * size,
-    )
-    return (result[:k], result[k]), result[k + 1]
-
-
-def batch_back_kernel(k, first, rows_held, *refs):
+        [gates, stats, batch_rows, pack],
+        flops=2 * rows * width * size,
+    )
+    return result[:k], result[k]
+
+
+def batch_back_kernel(k, first, *refs):
     length_ref, refs = refs[0], refs[1:]
     mine, mate, refs = refs[:k], refs[k : 2 * k], refs[2 * k :]
-    conv_ref, stat_ref, batch_ref, out_weight_ref, grad_ref, sum_ref = refs
+    gate_ref, stat_ref, batch_ref, pack_ref, grad_ref, active_ref, sum_ref = refs
     slots, width = mine[0].shape
-    size = conv_ref.shape[1]
-    weight = conv_rows(out_weight_ref, width, size, rows_held)
+    size = batch_ref.shape[1]
+    weight = conv_rows(pack_ref, width, size)
     row_at = lax.broadcasted_iota(jnp.int32, (slots, size), 0)
     sums = [jnp.zeros((1, size), F32)] * 4
     for i in range(k):
@@ -833,9 +843,11 @@
         for j in range(2):
             b = 2 * i + j
             at = pl.ds(b * slots, slots)
-            unit, _ = batch_unit(conv_ref[at, :], stat_ref)
+            unit, _ = batch_unit(gate_ref[at, 2 * size :], stat_ref)
             value = unit * batch_ref[0:1, :] + batch_ref[1:2, :]
-            grad = grad_active[j * slots : (j + 1) * slots] * swish_grad(value)
+            sig = sigmoid(value)
+            active_ref[at, :] = (value * sig).astype(BF16)
+            grad = grad_active[j * slots : (j + 1) * slots] * (sig * (1.0 + value * (1.0 - sig)))
             valid = (row_at < item_bounds(length_ref, first + b)[-1]).astype(F32)
             grad_unit = grad * batch_ref[0:1, :]
             grad_ref[at, :] = grad_unit
@@ -844,30 +856,29 @@
     sum_ref[...] = jnp.concatenate(sums + [jnp.zeros((4, size), F32)])
 
 
-def batch_back_call(pieces, lengths, first, conv, stats, batch_rows, out_weight, rows_held):
-    mine, mate = pieces
+def batch_back_call(group, lengths, first, gates, stats, batch_rows, pack):
+    mine, mate = group
     k, (slots, width) = len(mine), mine[0].shape
-    size = conv.shape[1]
+    rows, size = gates.shape[0], batch_rows.shape[1]
     return kernel_call(
-        functools.partial(batch_back_kernel, k, first, rows_held),
-        [shape(conv.shape, F32), shape((8, size), F32)],
-        list(mine) + list(mate) + [conv, stats, batch_rows, out_weight],
+        functools.partial(batch_back_kernel, k, first),
+        [shape((rows, size), F32), shape((rows, size), BF16), shape((8, size), F32)],
+        list(mine) + list(mate) + [gates, stats, batch_rows, pack],
         scalars=(lengths,),
-        flops=2 * conv.shape[0] * width * size,
+        flops=2 * rows * width * size,
     )
 
 
 def gate_back_kernel(k, first, tap_count, *refs):
     length_ref, refs = refs[0], refs[1:]
-    grad_in_ref, conv_ref, gate_ref, stat_ref, sum_ref, column_ref, tap_ref, refs = (
+    grad_in_ref, gate_ref, stat_ref, sum_ref, pack_ref, tap_ref, refs = (
         refs[0],
         refs[1],
         refs[2],
         refs[3],
         refs[4],
         refs[5],
-        refs[6],
-        refs[7:],
+        refs[6:],
     )
     out_mine, out_mate, grad_ref, tap_grad_ref, glu_ref, conv_grad_ref = (
         refs[:k],
@@ -893,9 +904,9 @@
             b = 2 * i + j
             at = pl.ds(b * slots, slots)
             before, behind, valid = item_reach(item_bounds(length_ref, first + b), row_at, slots)
-            gate_a, gate_sig = gate_ref[at, :size], sigmoid(gate_ref[at, size:])
+            gate_a, gate_sig = gate_ref[at, :size], sigmoid(gate_ref[at, size : 2 * size])
             glu_ref[PAD : PAD + slots, :] = gate_a * gate_sig * valid
-            unit, inverse = batch_unit(conv_ref[at, :], stat_ref)
+            unit, inverse = batch_unit(gate_ref[at, 2 * size :], stat_ref)
             conv_grad = valid * inverse * (grad_in_ref[at, :] - mean_grad - unit * mean_cross)
             conv_grad_ref[PAD : PAD + slots, :] = conv_grad
             grad_glu = jnp.zeros((slots, size), F32)
@@ -919,11 +930,11 @@
             )
         grad = jnp.concatenate(halves)
         grad_ref[pl.ds(2 * i * slots, 2 * slots), :] = grad
-        store_partial(out_mine, out_mate, i, slots, square_product_back(grad, column_ref, width, 4 * size, 6 * size))
-
-
-def gate_back_call(k, lengths, first, grad_unit, conv, gates, stats, sums, columns, taps, tap_count, slots, width):
-    rows, size = conv.shape
+        store_partial(out_mine, out_mate, i, slots, square_product_back(grad, pack_ref, width, 0, 2 * size))
+
+
+def gate_back_call(k, lengths, first, grads, gates, stats, sums, pack, taps, tap_count, slots, width):
+    rows, size = grads.shape
     outs = [shape((slots, width), F32)] * k + [
         shape((k, slots, width), BF16),
         shape((rows, 2 * size), BF16),
@@ -933,7 +944,7 @@
     result = kernel_call(
         functools.partial(gate_back_kernel, k, first, tap_count),
         outs,
-        [grad_unit, conv, gates, stats, sums, columns, taps],
+        [grads, gates, stats, sums, pack, taps],
         scalars=(lengths,),
         flops=4 * rows * width * size + 80 * tap_count * rows * size,
         scratch=[padded, padded],
@@ -1099,21 +1110,25 @@
     conv_ref[...] = weight_ref[7].astype(BF16)
 
 
-def square_pack_kernel(side_ref, column_ref, own_ref, other_ref, conv_ref, out_ref):
+def square_pack_kernel(side_ref, column_ref, own_ref, other_ref, conv_ref, mix_out, conv_out):
     team, rows, lanes = column_ref.shape
+    depth = team * rows
     for b in range(lanes // BLOCK):
+        out, at = (mix_out, b * depth) if b < 2 else (conv_out, (b - 2) * depth)
         for t in range(team):
-            at = (b * team + t) * rows
-            out_ref[at : at + rows, :] = column_ref[t, :, b * BLOCK : (b + 1) * BLOCK]
-    base = (lanes // BLOCK) * team * rows
+            first = at + t * rows
+            out[first : first + rows, :] = column_ref[t, :, b * BLOCK : (b + 1) * BLOCK]
     low = side_ref[0] == 0
     for b in range(own_ref.shape[1] // BLOCK):
         lane = slice(b * BLOCK, (b + 1) * BLOCK)
         own, other = own_ref[:, lane].astype(F32), other_ref[:, lane].astype(F32)
-        at = base + b * 3 * rows
-        out_ref[at : at + rows, :] = jnp.where(low, own, other).astype(BF16)
-        out_ref[at + rows : at + 2 * rows, :] = jnp.where(low, other, own).astype(BF16)
-        out_ref[at + 2 * rows : at + 3 * rows, :] = conv_ref[:, lane]
+        at = 2 * depth + b * 2 * rows
+        mix_out[at : at + rows, :] = jnp.where(low, own, other).astype(BF16)
+        mix_out[at + rows : at + 2 * rows, :] = jnp.where(low, other, own).astype(BF16)
+        at = depth + b * rows
+        conv_out[at : at + rows, :] = conv_ref[:, lane]
+    at = depth + (own_ref.shape[1] // BLOCK) * rows
+    conv_out[at:, :] = jnp.zeros((conv_out.shape[0] - at, BLOCK), BF16)
 
 
 def feed_pack_kernel(up_ref, down_ref, out_ref):
@@ -1364,9 +1379,11 @@
     def from_blocks(rows, count):
         return jnp.concatenate(jnp.split(rows, count), axis=1)
 
-    def outer_sum(values):
+    def outer_merge(values, combine):
+        if wide_team:
+            return combine([values] + [swap(values, "z", d) for d in range(1, planes)])
         for axis, bit in outer_bits:
-            values = values + swap(values, axis, bit)
+            values = combine([values, swap(values, axis, bit)])
         return values
 
     def step(
@@ -1423,19 +1440,12 @@
                 axis=2,
             )
             mix, conv_out = square_low[3], side_rows(square_low[7])
+        down_one = plane_gather(down_one)
         up_one = team_swap(up_one)
         up_one, frames, chan_low, lengths, columns, up_two, mix = lax.optimization_barrier(
             (up_one, frames, chan_low, lengths, columns, up_two, mix)
         )
-        if head_aligned:
-            first = kernel_call(
-                feed_pack_kernel,
-                [shape((team * rows_in + down_one.shape[0], team_hidden), BF16)],
-                [up_one, down_one],
-            )[0]
-        else:
-            first = jnp.concatenate([up_one.reshape(-1, team_hidden), down_one])
-        pack_one = plane_gather(first)
+        packs_one = (plane_gather(up_one.reshape(-1, team_hidden)), down_one)
         groups = gather(frames)
 
         if wide_team:
@@ -1485,35 +1495,38 @@
         if head_aligned:
             head_rows = sides * rows_in
             per_side = planes // sides
-            rows_held = (per_side, head_rows, rows_in)
-            lines = 6 * team_width // BLOCK * team * rows_in + width // BLOCK * 3 * rows_in
-            squares = kernel_call(
+            depth = team * rows_in
+            lines = [2 * depth + width // BLOCK * head_rows, 2 * depth]
+            mix_pack, conv_pack = kernel_call(
                 square_pack_kernel,
-                [shape((lines, BLOCK), BF16)],
+                [shape((n, BLOCK), BF16) for n in lines],
                 [columns, mix, swap(mix, "y"), conv_out],
                 scalars=(side,),
-            )[0]
+            )
             second = kernel_call(
                 feed_pack_kernel,
-                [shape((team * rows_in + down_two.shape[0], team_hidden), BF16)],
+                [shape((depth + down_two.shape[0], team_hidden), BF16)],
                 [up_two, down_two],
             )[0]
         else:
             per_side = 0
-            rows_held = (0, 0, conv_out.shape[0])
             mix = lax.all_gather(mix, ALL, axis=0, tiled=True)
             mix = lax.dynamic_slice_in_dim(mix, team_at * team_width, team_width, axis=0)
-            columns = to_blocks(columns.reshape(-1, 6 * team_width), BLOCK)
-            squares = jnp.concatenate([columns, to_blocks(conv_out, BLOCK)])
+            columns = columns.reshape(-1, 6 * team_width)
+            mix_pack = to_blocks(columns[:, : 4 * team_width], BLOCK)
+            conv_pack = jnp.concatenate(
+                [to_blocks(columns[:, 4 * team_width :], BLOCK), to_blocks(conv_out, BLOCK)]
+            )
             second = jnp.concatenate([up_two.reshape(-1, team_hidden), down_two])
         table = offset_table(slots, width).astype(BF16)
 
-        ready = (pack_one, groups, norms, taps, team_lengths, table)
-        ready, squares, second, mix = lax.optimization_barrier((ready, squares, second, mix))
-        pack_one, groups, norms, taps, team_lengths, table = ready
-        squares = plane_gather(squares)
-        if head_aligned:
-            mix = squares
+        ready = (packs_one, groups, norms, taps, team_lengths, table)
+        ready, mix_pack, conv_pack, second, mix = lax.optimization_barrier(
+            (ready, mix_pack, conv_pack, second, mix)
+        )
+        packs_one, groups, norms, taps, team_lengths, table = ready
+        mix_pack = plane_gather(mix_pack)
+        mix_packs = (mix_pack,) if head_aligned else (mix_pack, mix)
 
         def columns_of(results, i):
             return [result[i] for result in results]
@@ -1522,93 +1535,84 @@
         for group in groups:
             at.append(at[-1] + 2 * len(group[0]))
 
-        results = [forward_call(group, pack_one, norms[0]) for group in groups]
-        saved_one = [columns_of(columns_of(results, 1), i) for i in (2, 0, 1)]
+        results = [forward_call(group, packs_one, norms[0]) for group in groups]
+        saved_one = [columns_of(columns_of(results, 1), i) for i in (1, 0)]
         parts, _ = scatter(columns_of(results, 0))
         stream_one, normed = join_call(frames, parts, 0.5, norms[1])
-        normed, second = lax.optimization_barrier((normed, second))
+        normed, conv_pack, second = lax.optimization_barrier((normed, conv_pack, second))
+        conv_pack = plane_gather(conv_pack)
         pack_two = plane_gather(second)
 
         place = kernel_call(
             place_kernel,
             [shape((table.shape[0], team_width), BF16)],
-            [table, squares],
+            [table, mix_pack],
             flops=2 * table.shape[0] * width * team_width,
         )[0]
 
         def attention(i, group):
             return attention_call(
-                group, team_lengths, at[i], side, squares, mix, rows_held, bias_rows, place, head_size
+                group, team_lengths, at[i], side, mix_packs, per_side, bias_rows, place, head_size
             )
 
         groups, results = spread(normed, attention)
-        normed_two = chunk_order(groups)
         saved_two = columns_of(results, 1)
         parts, _ = scatter(columns_of(results, 0))
         stream_two, normed = join_call(stream_one, parts, 1.0, norms[2])
 
         def gates(i, group):
-            return gate_call(group, team_lengths, at[i], squares, taps, tap_count)
+            return gate_call(group, team_lengths, at[i], conv_pack, taps, tap_count)
 
         groups, saved_three = spread(normed, gates)
-        normed_three = chunk_order(groups)
-        stats = saved_three[0][2]
-        for saved in saved_three[1:]:
-            stats = merge(stats, saved[2])
-        for axis, bit in outer_bits:
-            stats = merge(stats, swap(stats, axis, bit))
+        stats = outer_merge(merge(columns_of(saved_three, 2)), merge)
         results = [
-            batch_call(
-                len(group[0]), saved[1], stats, batch_rows, squares, rows_held, slots, width
-            )
+            batch_call(len(group[0]), saved[0], stats, batch_rows, conv_pack, slots, width)
             for group, saved in reversed(list(zip(groups, saved_three)))
         ][::-1]
-        active_conv = columns_of(results, 1)
-        parts, _ = scatter(columns_of(results, 0))
+        parts, _ = scatter(results)
         stream_three, normed = join_call(stream_two, parts, 1.0, norms[3])
         normed, pack_two = lax.optimization_barrier((normed, pack_two))
 
-        groups, results = spread(normed, lambda i, group: forward_call(group, pack_two))
-        saved_four = [chunk_order(groups)] + [columns_of(columns_of(results, 1), i) for i in (0, 1)]
+        groups, results = spread(normed, lambda i, group: forward_call(group, (pack_two,)))
+        saved_four = [chunk_order(groups), columns_of(columns_of(results, 1), 0)]
         parts, _ = scatter(columns_of(results, 0))
         output, grad_four, low, norm_four = turn_call(
             stream_three, parts, 0.5, norms[4], out_grad, lengths
         )
 
-        def feed_backward(low, pack, saved):
-            normed, before, active = saved
+        def feed_backward(low, packs, saved):
+            normed, before = saved
             groups, results = spread(
-                low, lambda i, group: backward_call(group, pack, before[i])
-            )
-            term = feed_weight_call(
-                normed, columns_of(results, 1), active, chunk_order(groups), planes
-            )
+                low, lambda i, group: backward_call(group, packs, before[i])
+            )
+            grads, active = [columns_of(columns_of(results, 1), i) for i in (0, 1)]
+            term = feed_weight_call(normed, grads, active, chunk_order(groups), planes)
             return scatter(columns_of(results, 0), term)
 
-        parts, second_term = feed_backward(low, pack_two, saved_four)
+        parts, second_term = feed_backward(low, (pack_two,), saved_four)
         grad_three, low, norm_three = join_back_call(stream_three, grad_four, parts, 1.0, norms[3])
         low, second_term = lax.optimization_barrier((low, second_term))
         second_term = plane_reduce(second_term)
 
         def batch_back(i, group):
             return batch_back_call(
-                group, team_lengths, at[i], saved_three[i][1], stats, batch_rows, squares, rows_held
+                group, team_lengths, at[i], saved_three[i][0], stats, batch_rows, conv_pack
             )
 
         groups, grads = spread(low, batch_back)
-        local_sums = sum(columns_of(grads, 1))
-        sums = outer_sum(local_sums)
+        local_sums = sum_call(columns_of(grads, 2))
+        sums = outer_merge(local_sums, sum_call)
         results = [
             gate_back_call(
-                len(groups[i][0]), team_lengths, at[i], grads[i][0], saved_three[i][1],
-                saved_three[i][0], stats, sums, squares, taps, tap_count, slots, width,
+                len(groups[i][0]), team_lengths, at[i], grads[i][0], saved_three[i][0], stats, sums,
+                conv_pack, taps, tap_count, slots, width,
             )
             for i in reversed(range(len(groups)))
         ][::-1]
         tap_terms = columns_of(columns_of(results, 1), 1)
         conv_term = conv_weight_call(
-            normed_three, columns_of(columns_of(results, 1), 0), active_conv, chunk_order(groups),
-            planes,
+            columns_of(saved_three, 1), columns_of(columns_of(results, 1), 0), columns_of(grads, 1),
+            chunk_order(groups), planes,
         )
         parts, conv_term = scatter(columns_of(results, 0), conv_term)
         grad_two, low, norm_two = join_back_call(stream_two, grad_three, parts, 1.0, norms[2])
@@ -1617,29 +1621,29 @@
 
         def attention_back(i, group):
             return attention_back_call(
-                group, side, squares, mix, rows_held, place, saved_two[i][0], saved_two[i][1],
-                head_size,
+                group, side, mix_packs, per_side, place, saved_two[i], head_size
             )
 
         groups, results = spread(low, attention_back)
-        mixed, rows = columns_of(saved_two, 2), chunk_order(groups)
+        rows = chunk_order(groups)
         grads = columns_of(results, 1)
         bias_terms = columns_of(grads, 2)
         mix_term = mix_weight_call(
-            normed_two, columns_of(grads, 0), mixed, rows, [table] + columns_of(grads, 1), side,
-            planes, per_side,
+            saved_two, columns_of(grads, 0), rows, [table] + columns_of(grads, 1), side, planes,
+            per_side,
         )
         parts, mix_term = scatter(columns_of(results, 0), mix_term)
         if not head_aligned:
-            mix_own = mm_tn(jnp.concatenate(mixed), jnp.concatenate(rows)).astype(BF16)
+            mixed = jnp.concatenate([saved[:, -team_width:] for saved in saved_two])
+            mix_own = mm_tn(mixed, jnp.concatenate(rows)).astype(BF16)
             mix_own = lax.dynamic_update_slice_in_dim(
                 jnp.zeros((width, width), BF16), mix_own, team_at * team_width, axis=0
             )
         grad_one, low, norm_one = join_back_call(stream_one, grad_two, parts, 0.5, norms[1])
-        low, mix_term, conv_term = lax.optimization_barrier((low, mix_term, conv_term))
+        low, conv_term = lax.optimization_barrier((low, conv_term))
         mix_term = plane_reduce(mix_term)
 
-        parts, first_term = feed_backward(low, pack_one, saved_one)
+        parts, first_term = feed_backward(low, packs_one, saved_one)
         first_term = plane_reduce(first_term)
         frames_grad, norm_zero = join_back_call(frames, grad_one, parts, 1.0, norms[0], keep=False)
 
@@ -1653,7 +1657,7 @@
             return team_swap(rows.astype(BF16).reshape(team, -1, columns))
 
         def finish_channels(chan_term):
-            chan_term = outer_sum(chan_term).reshape(chan_rows, planes, -1)
+            chan_term = outer_merge(chan_term, sum_call).reshape(chan_rows, planes, -1)
             chan_term = lax.dynamic_index_in_dim(chan_term, lax.axis_index("z"), 1, keepdims=False)
             if not wide_team:
                 chan_term = lax.dynamic_index_in_dim(

time: 510 us -> 490 us (0.961)
  waiting for transfers between devices: 194 us -> 165 us
  starting transfers between devices: 116 us -> 126 us
  Pallas kernels: 108 us -> 100 us
  local copies, waits for them, and re-layouts: 61.4 us -> 68 us
    ppermute x70 -> x73, waiting for transfers between devices: 67.7 us -> 51.1 us  [swap(): return lax.ppermute(values, axis, [(i, i ^ bit) for i in range(size)])]
    all_gather x3 -> x5, waiting for transfers between devices: 32.3 us -> 17.2 us  [plane_gather(): return lax.all_gather(rows, 'z', axis=0, tiled=False)]
    ppermute x70 -> x73, starting transfers between devices: 27.6 us -> 37.1 us  [swap(): return lax.ppermute(values, axis, [(i, i ^ bit) for i in range(size)])]
    pallas_call x84, Pallas kernels: 108 us -> 100 us  [kernel_call(): pl.pallas_call(body, out_shape=tuple(outs), in_specs=[pl.BlockSpec(memory...]
    unnamed x350 -> x308, local copies, waits for them, and re-layouts: 57.6 us -> 64.8 us
  transfers between devices with their start and end apart: 132 -> 137, of which waited for: 73 -> 68; matrix products, arithmetic and copies ran while one was open for 1% -> 1% of each run, Pallas kernels for 20% -> 19%
where the time goes in v4:
time: 490 us; the launch traced here: 481 us
  waiting for transfers between devices  165 us (34%)
  starting transfers between devices  126 us (26%)
  Pallas kernels  100 us (20%)
  local copies, waits for them, and re-layouts  68 us (14%)
  between operations  15.9 us (3%)
  other arithmetic  5.31 us (1%)
    pallas_call x84, Pallas kernels, kernel_call(): pl.pallas_call(body, out_shape=tuple(outs), in_specs=[pl.BlockSpec(memory...  100 us
    ppermute x48, waiting for transfers between devices, turn(): return lax.ppermute(values, team_axes, pairs)  88.7 us
    unnamed x308, local copies, waits for them, and re-layouts  64.8 us
    ppermute x48, starting transfers between devices, turn(): return lax.ppermute(values, team_axes, pairs)  61 us
    ppermute x73, waiting for transfers between devices, swap(): return lax.ppermute(values, axis, [(i, i ^ bit) for i in range(size)])  51.1 us
    ppermute x73, starting transfers between devices, swap(): return lax.ppermute(values, axis, [(i, i ^ bit) for i in range(size)])  37.1 us
    all_to_all x7, starting transfers between devices, team_swap(): lax.all_to_all(blocks, team_axes, split_axis=0, concat_axis=0, tiled=True)  26.9 us
    all_gather x5, waiting for transfers between devices, plane_gather(): return lax.all_gather(rows, 'z', axis=0, tiled=False)  17.2 us
  transfers between devices with their start and end apart: 137, of which 68 were waited for; matrix products, arithmetic and copies ran while one was open for 1% of the time, Pallas kernels for 19%

profile of v4, /device:TPU:0, one launch (start us, length us, event | category | flops | bytes accessed | tf_op | source)
XLA Modules:
  0.0 480.8 jit_solution(10191963866134108261)
XLA Ops:
  11.4 5.2 %all-to-all-start = ((bf16[8,32,512]{2,1,0:T(8,128)(2,1)}), bf16[8,32,512]{2,1,0:T(8,128)(2,1)S(1)}, u32[]{:S(2)}, u32[]{:S(2)}) async-start(bf16[8,32,512]{2,1,0:T(8,128)(2,1)} %get-tuple-element.317), calls=%async_computation | async-start | bytes 524288 | tf_op jit(solution)/shard_map/all_to_all | solution.py:1365
  17.6 5.0 %all-to-all-done = bf16[8,32,512]{2,1,0:T(8,128)(2,1)S(1)} async-done(((bf16[8,32,512]{2,1,0:T(8,128)(2,1)}), bf16[8,32,512]{2,1,0:T(8,128)(2,1)S(1)}, u32[]{:S(2)}, u32[]{:S(2)}) %all-to-all-start) | async-done | bytes 262176 | tf_op jit(solution)/shard_map/all_to_all | solution.py:1365
  35.8 4.0 collective-permute-done.9
  44.0 3.5 all-to-all-start.1
  53.2 7.1 %collective-permute-done.12.refs_4_ = bf16[8,48,128]{2,1,0:T(8,128)(2,1)S(1)} collective-permute-done((bf16[8,48,128]{2,1,0:T(8,128)(2,1)S(1)}, bf16[8,48,128]{2,1,0:T(8,128)(2,1)S(1)}, u32[]{:S(2)}, u32[]{:S(2)}) %collective-permute-start.12) | collective-permute-done | bytes 98336 | tf_op jit(solution)/shard_map/ppermute | solution.py:44
  66.2 9.1 %all-gather.10.cloned.1.call-done.refs_3_.refs_5_.refs_2_.refs_4_ = bf16[4,256,512]{2,1,0:T(8,128)(2,1)} async-done(((bf16[1,256,512]{2,1,0:T(8,128)(2,1)}), bf16[4,256,512]{2,1,0:T(8,128)(2,1)}) %all-gather.10.cloned.1.call-update) | async-done | bytes 1048592 | tf_op jit(solution)/shard_map/all_gather | solution.py:1371
  89.2 3.7 collective-permute-done.17.refs_2_
  96.1 5.9 %collective-permute-done.19.refs_4_ = bf16[128,1024]{1,0:T(8,128)(2,1)S(1)} collective-permute-done((bf16[128,1024]{1,0:T(8,128)(2,1)S(1)}, bf16[128,1024]{1,0:T(8,128)(2,1)S(1)}, u32[]{:S(2)}, u32[]{:S(2)}) %collective-permute-start.19) | collective-permute-done | bytes 262176 | tf_op jit(solution)/shard_map/ppermute | solution.py:1285
  105.0 8.1 %all-gather.14.cloned.1.call-done = bf16[3072,256]{1,0:T(8,128)(2,1)} async-done(((bf16[768,256]{1,0:T(8,128)(2,1)}), bf16[3072,256]{1,0:T(8,128)(2,1)}) %all-gather.14.cloned.1.call-update) | async-done | bytes 1572880 | tf_op jit(solution)/shard_map/all_gather | solution.py:1371
  122.7 5.0 %shard_map.309 = (f32[128,1024]{1,0:T(8,128)S(1)}, f32[128,1024]{1,0:T(8,128)S(1)}, bf16[2,128,1024]{2,1,0:T(8,128)(2,1)S(1)}, bf16[512,1920]{1,0:T(8,128)(2,1)S(1)}) custom-call(s32[8,4]{1,0:T(8,128)S(1)} %get-tuple-element.364.refs_0_, s32[1]{0:T(128)} %bitcast.4.side_ref.refs_1_.refs_0_, bf16[128,1024]{1,0:T(8,128)(2,1)} %collective-permute-done.20.refs_2_, ...), custom_call_target="tpu_custom_call" | custom-call | flops 704643072 | bytes 6226944 | tf_op jit(solution)/shard_map/pallas_call | solution.py:75
  266.9 3.6 collective-permute-done.73.refs_4_
  279.9 4.3 collective-permute-done.75.refs_1_.refs_11_
  287.3 3.8 collective-permute-done.78.refs_1_.refs_15_
  302.5 4.2 shard_map.348
  324.6 3.6 collective-permute-done.89.refs_4_
  343.5 6.0 %shard_map.356 = (f32[128,1024]{1,0:T(8,128)S(1)}, f32[128,1024]{1,0:T(8,128)S(1)}, bf16[2,128,1024]{2,1,0:T(8,128)(2,1)S(1)}, bf16[512,384]{1,0:T(8,128)(2,1)S(...) custom-call(s32[1]{0:T(128)} %bitcast.4.side_ref.refs_1_.refs_0_, ...), custom_call_target="tpu_custom_call" | custom-call | flops 738197504 | bytes 6751232 | tf_op jit(solution)/shard_map/pallas_call | solution.py:75
  369.6 5.3 %collective-permute-done.103.refs_5_ = bf16[128,1024]{1,0:T(8,128)(2,1)S(1)} collective-permute-done((bf16[128,1024]{1,0:T(8,128)(2,1)S(1)}, bf16[128,1024]{1,0:T(8,128)(2,1)S(1)}, u32[]{:S(2)}, u32[]{:S(2)}) %collective-permute-start.103) | collective-permute-done | bytes 262176 | tf_op jit(solution)/shard_map/ppermute | solution.py:1285
  384.0 3.9 collective-permute-done.104.refs_0_.refs_11_
  400.2 3.7 shard_map.367
  410.0 6.7 %collective-permute-done.116.refs_5_ = bf16[128,1024]{1,0:T(8,128)(2,1)S(1)} collective-permute-done((bf16[128,1024]{1,0:T(8,128)(2,1)S(1)}, bf16[128,1024]{1,0:T(8,128)(2,1)S(1)}, u32[]{:S(2)}, u32[]{:S(2)}) %collective-permute-start.116) | collective-permute-done | bytes 262176 | tf_op jit(solution)/shard_map/ppermute | solution.py:1285
  437.7 4.1 all-to-all-start.4
  442.0 5.7 %collective-permute-done.117.refs_3_ = bf16[768,256]{1,0:T(8,128)(2,1)} collective-permute-done((bf16[768,256]{1,0:T(8,128)(2,1)}, bf16[768,256]{1,0:T(8,128)(2,1)}, u32[]{:S(2)}, u32[]{:S(2)}) %collective-permute-start.117) | collective-permute-done | bytes 393248 | tf_op jit(solution)/shard_map/ppermute | solution.py:44
  451.1 3.6 shard_map.372
  456.4 4.0 all-to-all-start.5
  (671 shorter events, 345.7 us)
Async XLA Ops:
  7.2 58.9 %all-gather.12.cloned.1.call-start = ((), (), s32[]{:S(2)}) async-start(), calls=%async_computation.16 | async-start | bytes 1310720 | tf_op jit(solution)/shard_map/all_gather | solution.py:1371
  16.6 58.7 %all-gather.10.cloned.1.call-start = ((), (), s32[]{:S(2)}) async-start(), calls=%async_computation.11 | async-start | bytes 1310720 | tf_op jit(solution)/shard_map/all_gather | solution.py:1371
  27.3 20.6 %collective-permute-start.2 = (bf16[128,1024]{1,0:T(8,128)(2,1)S(1)}, bf16[128,1024]{1,0:T(8,128)(2,1)}, u32[]{:S(2)}, u32[]{:S(2)}) collective-permute-start(bf16[128,1024]{1,0:T(8,128)(2,1)S(1)} %copy-done.36), channel_id=1, source_target_pairs={{0,1},{1,0},{2,6},{3,7},{4,5},{5,4},{6,2},{7,3},{8,9},{9,8},{10,14... | collective-permute-start | bytes 786440 | tf_op jit(solution)/shard_map/ppermute | solution.py:1285
  28.8 15.1 %all-to-all-start.2 = ((bf16[8,32,512]{2,1,0:T(8,128)(2,1)}), bf16[8,32,512]{2,1,0:T(8,128)(2,1)S(1)}, u32[]{:S(2)}, u32[]{:S(2)}) async-start(bf16[8,32,512]{2,1,0:T(8,128)(2,1)} %get-tuple-element.338), calls=%async_computation.2 | async-start | bytes 524288 | tf_op jit(solution)/shard_map/all_to_all | solution.py:1365
  34.3 13.8 %collective-permute-start.5 = (bf16[128,1024]{1,0:T(8,128)(2,1)}, bf16[128,1024]{1,0:T(8,128)(2,1)S(1)}, u32[]{:S(2)}, u32[]{:S(2)}) collective-permute-start(bf16[128,1024]{1,0:T(8,128)(2,1)} %collective-permute-done.1.refs_0_), channel_id=1, source_target_pairs={{0,1},{1,0},{2,6},{3,7},{4,5},{5,4},{6,2},{7,3},{8,9},{9,8},{10,14... | collective-permute-start | bytes 786440 | tf_op jit(solution)/shard_map/ppermute | solution.py:1285
  41.4 24.7 %collective-permute-start = (bf16[128,1024]{1,0:T(8,128)(2,1)S(1)}, bf16[128,1024]{1,0:T(8,128)(2,1)S(1)}, u32[]{:S(2)}, u32[]{:S(2)}) collective-permute-start(bf16[128,1024]{1,0:T(8,128)(2,1)S(1)} %copy-done.36), channel_id=1, source_target_pairs={{0,2},{2,0},{1,3},{3,1},{4,6},{6,4},{5,7},{7,5},{8,10},{10,8},{9,1... | collective-permute-start | bytes 786440 | tf_op jit(solution)/shard_map/ppermute | solution.py:44
  44.0 20.6 %all-to-all-start.1 = ((bf16[8,32,768]{2,1,0:T(8,128)(2,1)}), bf16[8,32,768]{2,1,0:T(8,128)(2,1)S(1)}, u32[]{:S(2)}, u32[]{:S(2)}) async-start(bf16[8,32,768]{2,1,0:T(8,128)(2,1)} %get-tuple-element.333), calls=%async_computation.1 | async-start | bytes 786432 | tf_op jit(solution)/shard_map/all_to_all | solution.py:1365
  47.4 65.6 %all-gather.14.cloned.1.call-start = ((), (), s32[]{:S(2)}) async-start(), calls=%async_computation.17 | async-start | bytes 1966080 | tf_op jit(solution)/shard_map/all_gather | solution.py:1371
  47.5 18.6 %collective-permute-start.3 = (bf16[128,1024]{1,0:T(8,128)(2,1)}, bf16[128,1024]{1,0:T(8,128)(2,1)}, u32[]{:S(2)}, u32[]{:S(2)}) collective-permute-start(bf16[128,1024]{1,0:T(8,128)(2,1)} %collective-permute-done.1.refs_0_), channel_id=1, source_target_pairs={{0,2},{2,0},{1,3},{3,1},{4,6},{6,4},{5,7},{7,5},{8,10},{10,8},{9,1... | collective-permute-start | bytes 786440 | tf_op jit(solution)/shard_map/ppermute | solution.py:44
  47.9 18.2 %collective-permute-start.4 = (bf16[128,1024]{1,0:T(8,128)(2,1)}, bf16[128,1024]{1,0:T(8,128)(2,1)}, u32[]{:S(2)}, u32[]{:S(2)}) collective-permute-start(bf16[128,1024]{1,0:T(8,128)(2,1)} %collective-permute-done.2.refs_1_), channel_id=1, source_target_pairs={{0,2},{2,0},{1,3},{3,1},{4,6},{6,4},{5,7},{7,5},{8,10},{10,8},{9,1... | collective-permute-start | bytes 786440 | tf_op jit(solution)/shard_map/ppermute | solution.py:44
  48.1 18.0 %collective-permute-start.6 = (bf16[128,1024]{1,0:T(8,128)(2,1)S(1)}, bf16[128,1024]{1,0:T(8,128)(2,1)S(1)}, u32[]{:S(2)}, u32[]{:S(2)}) collective-permute-start(bf16[128,1024]{1,0:T(8,128)(2,1)S(1)} %collective-permute-done.5.refs_0_), channel_id=1, source_target_pairs={{0,2},{2,0},{1,3},{3,1},{4,6},{6,4},{5,7},{7,5},{8,10},{10,8},{9,1... | collective-permute-start | bytes 786440 | tf_op jit(solution)/shard_map/ppermute | solution.py:44
  75.3 78.2 %all-gather.16.cloned.1.call-start = ((), (), s32[]{:S(2)}) async-start(), calls=%async_computation.18 | async-start | bytes 1310720 | tf_op jit(solution)/shard_map/all_gather | solution.py:1371
  102.4 94.2 %all-gather.18.cloned.1.call-start = ((), (), s32[]{:S(2)}) async-start(), calls=%async_computation.19 | async-start | bytes 2621440 | tf_op jit(solution)/shard_map/all_gather | solution.py:1371
  102.5 12.3 %collective-permute-start.22 = (bf16[128,1024]{1,0:T(8,128)(2,1)S(1)}, bf16[128,1024]{1,0:T(8,128)(2,1)S(1)}, u32[]{:S(2)}, u32[]{:S(2)}) collective-permute-start(bf16[128,1024]{1,0:T(8,128)(2,1)S(1)} %get-tuple-element.363.refs_2_), channel_id=1, source_target_pairs={{0,2},{2,0},{1,3},{3,1},{4,6},{6,4},{5,7},{7,5},{8,10},{10,8},{9,1... | collective-permute-start | bytes 786440 | tf_op jit(solution)/shard_map/ppermute | solution.py:44
  102.6 18.0 %collective-permute-start.20 = (bf16[128,1024]{1,0:T(8,128)(2,1)S(1)}, bf16[128,1024]{1,0:T(8,128)(2,1)}, u32[]{:S(2)}, u32[]{:S(2)}) collective-permute-start(bf16[128,1024]{1,0:T(8,128)(2,1)S(1)} %get-tuple-element.363.refs_2_), channel_id=1, source_target_pairs={{0,4},{1,5},{2,3},{3,2},{4,0},{5,1},{6,7},{7,6},{8,12},{9,13},{10,... | collective-permute-start | bytes 786440 | tf_op jit(solution)/shard_map/ppermute | solution.py:1285
  103.2 17.3 %collective-permute-start.21 = (bf16[128,1024]{1,0:T(8,128)(2,1)S(1)}, bf16[128,1024]{1,0:T(8,128)(2,1)}, u32[]{:S(2)}, u32[]{:S(2)}) collective-permute-start(bf16[128,1024]{1,0:T(8,128)(2,1)S(1)} %get-tuple-element.363.refs_2_), channel_id=1, source_target_pairs={{0,1},{1,0},{2,6},{3,7},{4,5},{5,4},{6,2},{7,3},{8,9},{9,8},{10,14... | collective-permute-start | bytes 786440 | tf_op jit(solution)/shard_map/ppermute | solution.py:1285
  104.7 227.2 %reduce-scatter.5.cloned.1.call-start = ((), (), s32[]{:S(2)}) async-start(), calls=%async_computation.12 | async-start | bytes 2621440 | tf_op jit(solution)/shard_map/reduce_scatter | solution.py:1374
  274.5 103.8 %reduce-scatter.7.cloned.1.call-start = ((), (), s32[]{:S(2)}) async-start(), calls=%async_computation.13 | async-start | bytes 983040 | tf_op jit(solution)/shard_map/reduce_scatter | solution.py:1374
  306.7 11.4 %collective-permute-start.86 = (bf16[2,128,1024]{2,1,0:T(8,128)(2,1)}, bf16[2,128,1024]{2,1,0:T(8,128)(2,1)S(1)}, u32[]{:S(2)}, u32[]{:S(2)}) collective-permute-start(bf16[2,128,1024]{2,1,0:T(8,128)(2,1)} %get-tuple-element.490), channel_id=1, source_target_pairs={{0,2},{2,0},{1,3},{3,1},{4,6},{6,4},{5,7},{7,5},{8,10},{10,8},{9,1... | collective-permute-start | bytes 1572872 | tf_op jit(solution)/shard_map/ppermute | solution.py:44
  332.0 90.3 %reduce-scatter.9.cloned.1.call-start = ((), (), s32[]{:S(2)}) async-start(), calls=%async_computation.14 | async-start | bytes 1966080 | tf_op jit(solution)/shard_map/reduce_scatter | solution.py:1374
  364.1 90.6 %reduce-scatter.11.cloned.1.call-start = ((), (), s32[]{:S(2)}) async-start(), calls=%async_computation.15 | async-start | bytes 2621440 | tf_op jit(solution)/shard_map/reduce_scatter | solution.py:1374
  430.4 17.4 %collective-permute-start.117 = (bf16[768,256]{1,0:T(8,128)(2,1)}, bf16[768,256]{1,0:T(8,128)(2,1)}, u32[]{:S(2)}, u32[]{:S(2)}) collective-permute-start(bf16[768,256]{1,0:T(8,128)(2,1)} %bitcast.55), channel_id=1, source_target_pairs={{0,1},{1,0},{2,3},{3,2},{4,5},{5,4},{6,7},{7,6},{8,9},{9,8},{10,11... | collective-permute-start | bytes 1179656 | tf_op jit(solution)/shard_map/ppermute | solution.py:44
  437.7 17.0 %all-to-all-start.4 = ((bf16[8,32,512]{2,1,0:T(8,128)(2,1)}), bf16[8,32,512]{2,1,0:T(8,128)(2,1)}, u32[]{:S(2)}, u32[]{:S(2)}) async-start(bf16[8,32,512]{2,1,0:T(8,128)(2,1)} %bitcast.15), calls=%async_computation.8 | async-start | bytes 524288 | tf_op jit(solution)/shard_map/all_to_all | solution.py:1365
  456.4 11.8 %all-to-all-start.5 = ((bf16[8,32,512]{2,1,0:T(8,128)(2,1)}), bf16[8,32,512]{2,1,0:T(8,128)(2,1)}, u32[]{:S(2)}, u32[]{:S(2)}) async-start(bf16[8,32,512]{2,1,0:T(8,128)(2,1)} %bitcast.16), calls=%async_computation.9 | async-start | bytes 524288 | tf_op jit(solution)/shard_map/all_to_all | solution.py:1365
  (267 other events, 1739.8 us)
Sparse Core Ops, SparseCore 0:
  10.2 30.6 all-gather.11
  43.0 32.2 all-gather.9
  77.4 35.5 all-gather.13
  115.1 26.8 all-gather.15
  143.9 45.7 all-gather.17
  274.7 43.4 reduce-scatter.4
  332.1 21.4 reduce-scatter.6
  364.2 33.2 reduce-scatter.8
  405.6 43.3 reduce-scatter.10

commit v5 on v4

--- a/solution.py
+++ b/solution.py
@@ -82,6 +82,10 @@
         compiler_params=pltpu.CompilerParams(vmem_limit_bytes=moved + ROOM),
         cost_estimate=pl.CostEstimate(flops=int(flops), bytes_accessed=moved, transcendentals=0),
     )(*scalars, *args)
+
+
+def stay(values):
+    return pltpu.with_memory_space_constraint(values, pltpu.HBM)
 
 
 def store_partial(mine_refs, mate_ref, i, slots, value):
@@ -969,7 +973,7 @@
     return kernel_call(
         functools.partial(join_kernel, len(far), coefficient),
         [shape(own.shape, F32), shape(own.shape, BF16)],
-        [stream, own, mate] + list(far) + [norm],
+        [stay(stream), own, mate] + list(far) + [norm],
     )
 
 
@@ -1022,7 +1026,7 @@
             shape(own.shape, BF16),
             shape((2, own.shape[1]), F32),
         ],
-        [stream, own, mate] + list(far) + [norm, cotangent],
+        [stay(stream), own, mate] + list(far) + [norm, stay(cotangent)],
         scalars=(lengths,),
     )
 
@@ -1046,7 +1050,7 @@
     return kernel_call(
         functools.partial(join_back_kernel, len(far), coefficient, keep),
         outs + [shape(own.shape, BF16), shape((2, own.shape[1]), F32)],
-        [stream, grad, own, mate] + list(far) + [norm],
+        [stay(stream), stay(grad), own, mate] + list(far) + [norm],
     )
 
 
@@ -1224,7 +1228,9 @@
     return kernel_call(
         body,
         [shape(weight.shape, F32)] * 4,
-        [scale] + list(terms) + [weight, moment, average],
+        [scale]
+        + list(terms)
+        + [stay(x) for x in (weight, moment, average)],
         scalars=scalars,
     )
 
@@ -1309,10 +1315,14 @@
             results.append(run(len(results), groups[-1]))
         return groups, results
 
-    def scatter(parts, fill=()):
-        (own,), own_mate = parts[0]
+    def scatter(parts, fill=(), near=None):
         (far,), far_mate = parts[-1]
         out_far = add_call(far, swap(far_mate, "c"), 0)
+        if near is not None:
+            argument, run = near
+            out_far, argument = lax.optimization_barrier((out_far, argument))
+            parts = run(argument)
+        (own,), own_mate = parts[0]
         got_own = swap(own_mate, "c")
         if not wide_team:
             across, fill = lax.optimization_barrier((swap(out_far, "x"), fill))
@@ -1419,14 +1429,14 @@
         chan_low = chan_weight.astype(BF16)
         if head_aligned:
             blocks = [shape((hidden // planes // team * (width // team_hidden), team_hidden), BF16)] * 2
-            down_one, down_two = kernel_call(split_down_kernel, blocks, [down_weight])
+            down_one, down_two = kernel_call(split_down_kernel, blocks, [stay(down_weight)])
             rows_in = up_weight.shape[1]
             blocks = [shape((team, rows_in, team_hidden), BF16)] * 2
-            up_one, up_two = kernel_call(split_up_kernel, blocks, [up_weight])
+            up_one, up_two = kernel_call(split_up_kernel, blocks, [stay(up_weight)])
             columns, mix, conv_out = kernel_call(
                 functools.partial(split_square_kernel, planes, sides, head_size),
                 [shape((team, rows_in, 6 * team_width), BF16)] + [shape((rows_in, width), BF16)] * 2,
-                [square_weight],
+                [stay(square_weight)],
             )
         else:
             up_low = up_weight.astype(BF16)
@@ -1602,19 +1612,28 @@
         groups, grads = spread(low, batch_back)
         local_sums = sum_call(columns_of(grads, 2))
         sums = outer_merge(local_sums, sum_call)
-        results = [
-            gate_back_call(
-                len(groups[i][0]), team_lengths, at[i], grads[i][0], saved_three[i][0], stats, sums,
-                conv_pack, taps, tap_count, slots, width,
-            )
-            for i in reversed(range(len(groups)))
-        ][::-1]
+        def gate_back(sums, numbers):
+            return [
+                gate_back_call(
+                    len(groups[i][0]), team_lengths, at[i], grads[i][0], saved_three[i][0], stats,
+                    sums, conv_pack, taps, tap_count, slots, width,
+                )
+                for i in numbers
+            ]
+
+        results = gate_back(sums, [len(groups) - 1])
+
+        def gate_back_near(sums):
+            results[:0] = gate_back(sums, range(len(groups) - 1))
+            return columns_of(results, 0)
+
+        parts, _ = scatter(columns_of(results, 0), near=(sums, gate_back_near))
         tap_terms = columns_of(columns_of(results, 1), 1)
         conv_term = conv_weight_call(
             columns_of(saved_three, 1), columns_of(columns_of(results, 1), 0), columns_of(grads, 1),
             chunk_order(groups), planes,
         )
-        parts, conv_term = scatter(columns_of(results, 0), conv_term)
+        parts, conv_term = lax.optimization_barrier((parts, conv_term))
         grad_two, low, norm_two = join_back_call(stream_two, grad_three, parts, 1.0, norms[2])
         low, conv_term, second_term = lax.optimization_barrier((low, conv_term, second_term))
         conv_term = plane_reduce(conv_term)

time: 490 us -> 480 us (0.980)
  local copies, waits for them, and re-layouts: 68 us -> 51.1 us
  Pallas kernels: 100 us -> 110 us
    unnamed x308 -> x260, local copies, waits for them, and re-layouts: 64.8 us -> 47.9 us
    pallas_call x84, Pallas kernels: 100 us -> 110 us  [kernel_call(): pl.pallas_call(body, out_shape=tuple(outs), in_specs=[pl.BlockSpec(memory...]
  transfers between devices with their start and end apart: 137 -> 137, of which waited for: 68 -> 66; matrix products, arithmetic and copies ran while one was open for 1% -> 1% of each run, Pallas kernels for 19% -> 21%
where the time goes in v5:
time: 480 us; the launch traced here: 472 us
  waiting for transfers between devices  164 us (34%)
  starting transfers between devices  126 us (26%)
  Pallas kernels  110 us (23%)
  local copies, waits for them, and re-layouts  51.1 us (11%)
  between operations  15.9 us (3%)
    pallas_call x84, Pallas kernels, kernel_call(): pl.pallas_call(body, out_shape=tuple(outs), in_specs=[pl.BlockSpec(memory...  110 us
    ppermute x48, waiting for transfers between devices, turn(): return lax.ppermute(values, team_axes, pairs)  89.9 us
    ppermute x48, starting transfers between devices, turn(): return lax.ppermute(values, team_axes, pairs)  62.4 us
    ppermute x73, waiting for transfers between devices, swap(): return lax.ppermute(values, axis, [(i, i ^ bit) for i in range(size)])  50.8 us
    unnamed x260, local copies, waits for them, and re-layouts  47.9 us
    ppermute x73, starting transfers between devices, swap(): return lax.ppermute(values, axis, [(i, i ^ bit) for i in range(size)])  36.8 us
    all_to_all x7, starting transfers between devices, team_swap(): lax.all_to_all(blocks, team_axes, split_axis=0, concat_axis=0, tiled=True)  25.7 us
    all_gather x5, waiting for transfers between devices, plane_gather(): return lax.all_gather(rows, 'z', axis=0, tiled=False)  16.3 us
  transfers between devices with their start and end apart: 137, of which 66 were waited for; matrix products, arithmetic and copies ran while one was open for 1% of the time, Pallas kernels for 21%

profile of v5, /device:TPU:0, one launch (start us, length us, event | category | flops | bytes accessed | tf_op | source)
XLA Modules:
  0.0 471.7 jit_solution(11824972554959911953)
XLA Ops:
  11.3 5.2 %all-to-all-start = ((bf16[8,32,512]{2,1,0:T(8,128)(2,1)}), bf16[8,32,512]{2,1,0:T(8,128)(2,1)S(1)}, u32[]{:S(2)}, u32[]{:S(2)}) async-start(bf16[8,32,512]{2,1,0:T(8,128)(2,1)} %get-tuple-element.322), calls=%async_computation | async-start | bytes 524288 | tf_op jit(solution)/shard_map/all_to_all | solution.py:1375
  18.8 3.8 all-to-all-done
  35.7 4.0 collective-permute-done.9
  53.1 7.1 %collective-permute-done.12.refs_4_ = bf16[8,48,128]{2,1,0:T(8,128)(2,1)S(1)} collective-permute-done((bf16[8,48,128]{2,1,0:T(8,128)(2,1)S(1)}, bf16[8,48,128]{2,1,0:T(8,128)(2,1)S(1)}, u32[]{:S(2)}, u32[]{:S(2)}) %collective-permute-start.12) | collective-permute-done | bytes 98336 | tf_op jit(solution)/shard_map/ppermute | solution.py:44
  65.4 9.9 %all-gather.10.cloned.1.call-done.refs_3_.refs_5_.refs_2_.refs_4_ = bf16[4,256,512]{2,1,0:T(8,128)(2,1)} async-done(((bf16[1,256,512]{2,1,0:T(8,128)(2,1)}), bf16[4,256,512]{2,1,0:T(8,128)(2,1)}) %all-gather.10.cloned.1.call-update) | async-done | bytes 1048592 | tf_op jit(solution)/shard_map/all_gather | solution.py:1381
  89.2 3.7 collective-permute-done.17.refs_2_
  96.1 5.9 %collective-permute-done.19.refs_4_ = bf16[128,1024]{1,0:T(8,128)(2,1)S(1)} collective-permute-done((bf16[128,1024]{1,0:T(8,128)(2,1)S(1)}, bf16[128,1024]{1,0:T(8,128)(2,1)S(1)}, u32[]{:S(2)}, u32[]{:S(2)}) %collective-permute-start.19) | collective-permute-done | bytes 262176 | tf_op jit(solution)/shard_map/ppermute | solution.py:1291
  106.7 6.4 %all-gather.14.cloned.1.call-done = bf16[3072,256]{1,0:T(8,128)(2,1)} async-done(((bf16[768,256]{1,0:T(8,128)(2,1)}), bf16[3072,256]{1,0:T(8,128)(2,1)}) %all-gather.14.cloned.1.call-update) | async-done | bytes 1572880 | tf_op jit(solution)/shard_map/all_gather | solution.py:1381
  121.6 4.6 shard_map.309
  137.1 3.5 collective-permute-done.30.refs_2_
  267.0 3.6 collective-permute-done.73.refs_4_
  279.3 4.3 collective-permute-done.75.refs_1_.refs_11_
  286.7 3.8 collective-permute-done.78.refs_1_.refs_15_
  319.9 4.1 collective-permute-done.90.refs_5_
  339.3 6.0 %shard_map.356 = (f32[128,1024]{1,0:T(8,128)S(1)}, f32[128,1024]{1,0:T(8,128)S(1)}, bf16[2,128,1024]{2,1,0:T(8,128)(2,1)S(1)}, bf16[512,384]{1,0:T(8,128)(2,1)S(...) custom-call(s32[1]{0:T(128)} %bitcast.4.side_ref.refs_1_.refs_0_, ...), custom_call_target="tpu_custom_call" | custom-call | flops 738197504 | bytes 6751232 | tf_op jit(solution)/shard_map/pallas_call | solution.py:75
  365.6 4.4 collective-permute-done.103.refs_5_
  379.9 3.5 collective-permute-done.104.refs_0_.refs_11_
  395.4 3.7 shard_map.367
  405.3 6.9 %collective-permute-done.116.refs_5_ = bf16[128,1024]{1,0:T(8,128)(2,1)S(1)} collective-permute-done((bf16[128,1024]{1,0:T(8,128)(2,1)S(1)}, bf16[128,1024]{1,0:T(8,128)(2,1)S(1)}, u32[]{:S(2)}, u32[]{:S(2)}) %collective-permute-start.116) | collective-permute-done | bytes 262176 | tf_op jit(solution)/shard_map/ppermute | solution.py:1291
  423.5 3.5 all-to-all-start.3
  438.1 6.6 %collective-permute-done.117.refs_3_ = bf16[768,256]{1,0:T(8,128)(2,1)S(1)} collective-permute-done((bf16[768,256]{1,0:T(8,128)(2,1)}, bf16[768,256]{1,0:T(8,128)(2,1)S(1)}, u32[]{:S(2)}, u32[]{:S(2)}) %collective-permute-start.117) | collective-permute-done | bytes 393248 | tf_op jit(solution)/shard_map/ppermute | solution.py:44
  444.6 4.4 shard_map.372
  456.5 4.1 shard_map.374
  460.6 4.1 shard_map.373
  (623 shorter events, 338.8 us)
Async XLA Ops:
  7.2 58.2 %all-gather.12.cloned.1.call-start = ((), (), s32[]{:S(2)}) async-start(), calls=%async_computation.16 | async-start | bytes 1310720 | tf_op jit(solution)/shard_map/all_gather | solution.py:1381
  11.3 11.2 %all-to-all-start = ((bf16[8,32,512]{2,1,0:T(8,128)(2,1)}), bf16[8,32,512]{2,1,0:T(8,128)(2,1)S(1)}, u32[]{:S(2)}, u32[]{:S(2)}) async-start(bf16[8,32,512]{2,1,0:T(8,128)(2,1)} %get-tuple-element.322), calls=%async_computation | async-start | bytes 524288 | tf_op jit(solution)/shard_map/all_to_all | solution.py:1375
  16.5 58.8 %all-gather.10.cloned.1.call-start = ((), (), s32[]{:S(2)}) async-start(), calls=%async_computation.11 | async-start | bytes 1310720 | tf_op jit(solution)/shard_map/all_gather | solution.py:1381
  27.2 20.6 %collective-permute-start.2 = (bf16[128,1024]{1,0:T(8,128)(2,1)S(1)}, bf16[128,1024]{1,0:T(8,128)(2,1)}, u32[]{:S(2)}, u32[]{:S(2)}) collective-permute-start(bf16[128,1024]{1,0:T(8,128)(2,1)S(1)} %copy-done.30), channel_id=1, source_target_pairs={{0,1},{1,0},{2,6},{3,7},{4,5},{5,4},{6,2},{7,3},{8,9},{9,8},{10,14... | collective-permute-start | bytes 786440 | tf_op jit(solution)/shard_map/ppermute | solution.py:1291
  28.7 15.1 %all-to-all-start.2 = ((bf16[8,32,512]{2,1,0:T(8,128)(2,1)}), bf16[8,32,512]{2,1,0:T(8,128)(2,1)S(1)}, u32[]{:S(2)}, u32[]{:S(2)}) async-start(bf16[8,32,512]{2,1,0:T(8,128)(2,1)} %get-tuple-element.343), calls=%async_computation.2 | async-start | bytes 524288 | tf_op jit(solution)/shard_map/all_to_all | solution.py:1375
  34.2 13.8 %collective-permute-start.5 = (bf16[128,1024]{1,0:T(8,128)(2,1)}, bf16[128,1024]{1,0:T(8,128)(2,1)S(1)}, u32[]{:S(2)}, u32[]{:S(2)}) collective-permute-start(bf16[128,1024]{1,0:T(8,128)(2,1)} %collective-permute-done.1.refs_0_), channel_id=1, source_target_pairs={{0,1},{1,0},{2,6},{3,7},{4,5},{5,4},{6,2},{7,3},{8,9},{9,8},{10,14... | collective-permute-start | bytes 786440 | tf_op jit(solution)/shard_map/ppermute | solution.py:1291
  41.3 24.1 %collective-permute-start = (bf16[128,1024]{1,0:T(8,128)(2,1)S(1)}, bf16[128,1024]{1,0:T(8,128)(2,1)S(1)}, u32[]{:S(2)}, u32[]{:S(2)}) collective-permute-start(bf16[128,1024]{1,0:T(8,128)(2,1)S(1)} %copy-done.30), channel_id=1, source_target_pairs={{0,2},{2,0},{1,3},{3,1},{4,6},{6,4},{5,7},{7,5},{8,10},{10,8},{9,1... | collective-permute-start | bytes 786440 | tf_op jit(solution)/shard_map/ppermute | solution.py:44
  43.9 20.6 %all-to-all-start.1 = ((bf16[8,32,768]{2,1,0:T(8,128)(2,1)}), bf16[8,32,768]{2,1,0:T(8,128)(2,1)S(1)}, u32[]{:S(2)}, u32[]{:S(2)}) async-start(bf16[8,32,768]{2,1,0:T(8,128)(2,1)} %get-tuple-element.338), calls=%async_computation.1 | async-start | bytes 786432 | tf_op jit(solution)/shard_map/all_to_all | solution.py:1375
  47.3 65.8 %all-gather.14.cloned.1.call-start = ((), (), s32[]{:S(2)}) async-start(), calls=%async_computation.17 | async-start | bytes 1966080 | tf_op jit(solution)/shard_map/all_gather | solution.py:1381
  47.4 18.0 %collective-permute-start.3 = (bf16[128,1024]{1,0:T(8,128)(2,1)}, bf16[128,1024]{1,0:T(8,128)(2,1)}, u32[]{:S(2)}, u32[]{:S(2)}) collective-permute-start(bf16[128,1024]{1,0:T(8,128)(2,1)} %collective-permute-done.1.refs_0_), channel_id=1, source_target_pairs={{0,2},{2,0},{1,3},{3,1},{4,6},{6,4},{5,7},{7,5},{8,10},{10,8},{9,1... | collective-permute-start | bytes 786440 | tf_op jit(solution)/shard_map/ppermute | solution.py:44
  47.8 17.5 %collective-permute-start.4 = (bf16[128,1024]{1,0:T(8,128)(2,1)}, bf16[128,1024]{1,0:T(8,128)(2,1)}, u32[]{:S(2)}, u32[]{:S(2)}) collective-permute-start(bf16[128,1024]{1,0:T(8,128)(2,1)} %collective-permute-done.2.refs_1_), channel_id=1, source_target_pairs={{0,2},{2,0},{1,3},{3,1},{4,6},{6,4},{5,7},{7,5},{8,10},{10,8},{9,1... | collective-permute-start | bytes 786440 | tf_op jit(solution)/shard_map/ppermute | solution.py:44
  48.0 17.4 %collective-permute-start.6 = (bf16[128,1024]{1,0:T(8,128)(2,1)S(1)}, bf16[128,1024]{1,0:T(8,128)(2,1)S(1)}, u32[]{:S(2)}, u32[]{:S(2)}) collective-permute-start(bf16[128,1024]{1,0:T(8,128)(2,1)S(1)} %collective-permute-done.5.refs_0_), channel_id=1, source_target_pairs={{0,2},{2,0},{1,3},{3,1},{4,6},{6,4},{5,7},{7,5},{8,10},{10,8},{9,1... | collective-permute-start | bytes 786440 | tf_op jit(solution)/shard_map/ppermute | solution.py:44
  75.3 76.9 %all-gather.16.cloned.1.call-start = ((), (), s32[]{:S(2)}) async-start(), calls=%async_computation.18 | async-start | bytes 1310720 | tf_op jit(solution)/shard_map/all_gather | solution.py:1381
  104.2 92.0 %all-gather.18.cloned.1.call-start = ((), (), s32[]{:S(2)}) async-start(), calls=%async_computation.19 | async-start | bytes 2621440 | tf_op jit(solution)/shard_map/all_gather | solution.py:1381
  104.3 15.3 %collective-permute-start.20 = (bf16[128,1024]{1,0:T(8,128)(2,1)S(1)}, bf16[128,1024]{1,0:T(8,128)(2,1)S(1)}, u32[]{:S(2)}, u32[]{:S(2)}) collective-permute-start(bf16[128,1024]{1,0:T(8,128)(2,1)S(1)} %get-tuple-element.368.refs_2_), channel_id=1, source_target_pairs={{0,4},{1,5},{2,3},{3,2},{4,0},{5,1},{6,7},{7,6},{8,12},{9,13},{10,... | collective-permute-start | bytes 786440 | tf_op jit(solution)/shard_map/ppermute | solution.py:1291
  105.0 14.6 %collective-permute-start.21 = (bf16[128,1024]{1,0:T(8,128)(2,1)S(1)}, bf16[128,1024]{1,0:T(8,128)(2,1)S(1)}, u32[]{:S(2)}, u32[]{:S(2)}) collective-permute-start(bf16[128,1024]{1,0:T(8,128)(2,1)S(1)} %get-tuple-element.368.refs_2_), channel_id=1, source_target_pairs={{0,1},{1,0},{2,6},{3,7},{4,5},{5,4},{6,2},{7,3},{8,9},{9,8},{10,14... | collective-permute-start | bytes 786440 | tf_op jit(solution)/shard_map/ppermute | solution.py:1291
  106.4 221.3 %reduce-scatter.5.cloned.1.call-start = ((), (), s32[]{:S(2)}) async-start(), calls=%async_computation.12 | async-start | bytes 2621440 | tf_op jit(solution)/shard_map/reduce_scatter | solution.py:1384
  247.7 10.6 %collective-permute-start.69 = (bf16[2,128,1024]{2,1,0:T(8,128)(2,1)}, bf16[2,128,1024]{2,1,0:T(8,128)(2,1)}, u32[]{:S(2)}, u32[]{:S(2)}) collective-permute-start(bf16[2,128,1024]{2,1,0:T(8,128)(2,1)} %get-tuple-element.461), channel_id=1, source_target_pairs={{0,2},{2,0},{1,3},{3,1},{4,6},{6,4},{5,7},{7,5},{8,10},{10,8},{9,1... | collective-permute-start | bytes 1572872 | tf_op jit(solution)/shard_map/ppermute | solution.py:44
  273.9 99.9 %reduce-scatter.7.cloned.1.call-start = ((), (), s32[]{:S(2)}) async-start(), calls=%async_computation.13 | async-start | bytes 983040 | tf_op jit(solution)/shard_map/reduce_scatter | solution.py:1384
  327.8 91.1 %reduce-scatter.9.cloned.1.call-start = ((), (), s32[]{:S(2)}) async-start(), calls=%async_computation.14 | async-start | bytes 1966080 | tf_op jit(solution)/shard_map/reduce_scatter | solution.py:1384
  359.9 89.1 %reduce-scatter.11.cloned.1.call-start = ((), (), s32[]{:S(2)}) async-start(), calls=%async_computation.15 | async-start | bytes 2621440 | tf_op jit(solution)/shard_map/reduce_scatter | solution.py:1384
  423.5 10.8 %all-to-all-start.3 = ((bf16[8,32,768]{2,1,0:T(8,128)(2,1)}), bf16[8,32,768]{2,1,0:T(8,128)(2,1)S(1)}, u32[]{:S(2)}, u32[]{:S(2)}) async-start(bf16[8,32,768]{2,1,0:T(8,128)(2,1)} %shard_map.371), calls=%async_computation.7 | async-start | bytes 786432 | tf_op jit(solution)/shard_map/all_to_all | solution.py:1375
  427.0 17.6 %collective-permute-start.117 = (bf16[768,256]{1,0:T(8,128)(2,1)}, bf16[768,256]{1,0:T(8,128)(2,1)S(1)}, u32[]{:S(2)}, u32[]{:S(2)}) collective-permute-start(bf16[768,256]{1,0:T(8,128)(2,1)} %bitcast.55), channel_id=1, source_target_pairs={{0,1},{1,0},{2,3},{3,2},{4,5},{5,4},{6,7},{7,6},{8,9},{9,8},{10,11... | collective-permute-start | bytes 1179656 | tf_op jit(solution)/shard_map/ppermute | solution.py:44
  434.4 14.7 %all-to-all-start.4 = ((bf16[8,32,512]{2,1,0:T(8,128)(2,1)}), bf16[8,32,512]{2,1,0:T(8,128)(2,1)S(1)}, u32[]{:S(2)}, u32[]{:S(2)}) async-start(bf16[8,32,512]{2,1,0:T(8,128)(2,1)} %bitcast.15), calls=%async_computation.8 | async-start | bytes 524288 | tf_op jit(solution)/shard_map/all_to_all | solution.py:1375
  (243 other events, 1567.6 us)
Sparse Core Ops, SparseCore 0:
  10.2 30.6 all-gather.11
  43.0 32.2 all-gather.9
  77.4 35.6 all-gather.13
  115.1 26.8 all-gather.15
  143.9 45.7 all-gather.17
  274.1 43.4 reduce-scatter.4
  327.9 21.3 reduce-scatter.6
  360.1 33.3 reduce-scatter.8
  401.0 43.5 reduce-scatter.10

commit v6 on v5

--- a/solution.py
+++ b/solution.py
@@ -1216,7 +1216,8 @@
     parts = []
     for b in range(blocks):
         at = slice(base + b * head_rows, base + (b + 1) * head_rows)
-        parts.append(mix_ref[at, :].astype(F32) + other_ref[at, :].astype(F32))
+        other_at = slice(b * head_rows, (b + 1) * head_rows)
+        parts.append(mix_ref[at, :].astype(F32) + other_ref[other_at, :].astype(F32))
     whole = jnp.concatenate(parts, axis=1)
     update(scale_ref, RATE_SQUARE, 3, jnp.where(side_ref[0] == 0, whole[:rows], whole[rows:]), refs)
     base = conv_ref.shape[0] - blocks * rows
@@ -1707,7 +1708,12 @@
             square_all = update_call(
                 functools.partial(update_square_kernel, planes, sides, head_size),
                 rate_scale,
-                [team_swap(blocks), mix_term, swap(mix_term, "y"), conv_term],
+                [
+                    team_swap(blocks),
+                    mix_term,
+                    swap(mix_term[4 * team_width // BLOCK * depth :], "y"),
+                    conv_term,
+                ],
                 square_weight,
                 square_moment,
                 square_average,

time: 480 us -> 476 us (level)
  waiting for transfers between devices: 164 us -> 159 us
    ppermute x73, waiting for transfers between devices: 50.8 us -> 44.3 us  [swap(): return lax.ppermute(values, axis, [(i, i ^ bit) for i in range(size)])]
where the time goes in v6:
time: 476 us; the launch traced here: 467 us
  waiting for transfers between devices  159 us (33%)
  starting transfers between devices  126 us (26%)
  Pallas kernels  110 us (23%)
  local copies, waits for them, and re-layouts  52 us (11%)
  between operations  15.9 us (3%)
    pallas_call x84, Pallas kernels, kernel_call(): pl.pallas_call(body, out_shape=tuple(outs), in_specs=[pl.BlockSpec(memory...  110 us
    ppermute x48, waiting for transfers between devices, turn(): return lax.ppermute(values, team_axes, pairs)  89.9 us
    ppermute x48, starting transfers between devices, turn(): return lax.ppermute(values, team_axes, pairs)  62.4 us
    unnamed x260, local copies, waits for them, and re-layouts  47.9 us
    ppermute x73, waiting for transfers between devices, swap(): return lax.ppermute(values, axis, [(i, i ^ bit) for i in range(size)])  44.3 us
    ppermute x73, starting transfers between devices, swap(): return lax.ppermute(values, axis, [(i, i ^ bit) for i in range(size)])  36.9 us
    all_to_all x7, starting transfers between devices, team_swap(): lax.all_to_all(blocks, team_axes, split_axis=0, concat_axis=0, tiled=True)  25.9 us
    all_gather x5, waiting for transfers between devices, plane_gather(): return lax.all_gather(rows, 'z', axis=0, tiled=False)  16.3 us
  transfers between devices with their start and end apart: 137, of which 66 were waited for; matrix products, arithmetic and copies ran while one was open for 1% of the time, Pallas kernels for 21%

profile of v6, /device:TPU:0, one launch (start us, length us, event | category | flops | bytes accessed | tf_op | source)
XLA Modules:
  0.0 467.4 jit_solution(3005309312199815905)
XLA Ops:
  11.3 5.2 %all-to-all-start = ((bf16[8,32,512]{2,1,0:T(8,128)(2,1)}), bf16[8,32,512]{2,1,0:T(8,128)(2,1)S(1)}, u32[]{:S(2)}, u32[]{:S(2)}) async-start(bf16[8,32,512]{2,1,0:T(8,128)(2,1)} %get-tuple-element.322), calls=%async_computation | async-start | bytes 524288 | tf_op jit(solution)/shard_map/all_to_all | solution.py:1376
  18.8 3.8 all-to-all-done
  35.7 4.0 collective-permute-done.9
  53.1 7.1 %collective-permute-done.12.refs_4_ = bf16[8,48,128]{2,1,0:T(8,128)(2,1)S(1)} collective-permute-done((bf16[8,48,128]{2,1,0:T(8,128)(2,1)S(1)}, bf16[8,48,128]{2,1,0:T(8,128)(2,1)S(1)}, u32[]{:S(2)}, u32[]{:S(2)}) %collective-permute-start.12) | collective-permute-done | bytes 98336 | tf_op jit(solution)/shard_map/ppermute | solution.py:44
  65.4 9.9 %all-gather.10.cloned.1.call-done.refs_3_.refs_5_.refs_2_.refs_4_ = bf16[4,256,512]{2,1,0:T(8,128)(2,1)} async-done(((bf16[1,256,512]{2,1,0:T(8,128)(2,1)}), bf16[4,256,512]{2,1,0:T(8,128)(2,1)}) %all-gather.10.cloned.1.call-update) | async-done | bytes 1048592 | tf_op jit(solution)/shard_map/all_gather | solution.py:1382
  89.2 3.7 collective-permute-done.17.refs_2_
  96.1 5.9 %collective-permute-done.19.refs_4_ = bf16[128,1024]{1,0:T(8,128)(2,1)S(1)} collective-permute-done((bf16[128,1024]{1,0:T(8,128)(2,1)S(1)}, bf16[128,1024]{1,0:T(8,128)(2,1)S(1)}, u32[]{:S(2)}, u32[]{:S(2)}) %collective-permute-start.19) | collective-permute-done | bytes 262176 | tf_op jit(solution)/shard_map/ppermute | solution.py:1292
  106.7 6.4 %all-gather.14.cloned.1.call-done = bf16[3072,256]{1,0:T(8,128)(2,1)} async-done(((bf16[768,256]{1,0:T(8,128)(2,1)}), bf16[3072,256]{1,0:T(8,128)(2,1)}) %all-gather.14.cloned.1.call-update) | async-done | bytes 1572880 | tf_op jit(solution)/shard_map/all_gather | solution.py:1382
  121.6 4.6 shard_map.309
  137.1 3.5 collective-permute-done.30.refs_2_
  267.0 3.6 collective-permute-done.73.refs_4_
  279.3 4.3 collective-permute-done.75.refs_1_.refs_11_
  286.7 3.8 collective-permute-done.78.refs_1_.refs_15_
  319.9 4.1 collective-permute-done.90.refs_5_
  339.3 6.0 %shard_map.356 = (f32[128,1024]{1,0:T(8,128)S(1)}, f32[128,1024]{1,0:T(8,128)S(1)}, bf16[2,128,1024]{2,1,0:T(8,128)(2,1)S(1)}, bf16[512,384]{1,0:T(8,128)(2,1)S(...) custom-call(s32[1]{0:T(128)} %bitcast.4.side_ref.refs_1_.refs_0_, ...), custom_call_target="tpu_custom_call" | custom-call | flops 738197504 | bytes 6751232 | tf_op jit(solution)/shard_map/pallas_call | solution.py:75
  365.6 4.4 collective-permute-done.103.refs_5_
  379.9 3.5 collective-permute-done.104.refs_0_.refs_11_
  395.4 3.7 shard_map.367
  405.3 6.9 %collective-permute-done.116.refs_5_ = bf16[128,1024]{1,0:T(8,128)(2,1)S(1)} collective-permute-done((bf16[128,1024]{1,0:T(8,128)(2,1)S(1)}, bf16[128,1024]{1,0:T(8,128)(2,1)S(1)}, u32[]{:S(2)}, u32[]{:S(2)}) %collective-permute-start.116) | collective-permute-done | bytes 262176 | tf_op jit(solution)/shard_map/ppermute | solution.py:1292
  423.5 3.5 all-to-all-start.3
  438.8 4.4 shard_map.372
  446.3 3.7 all-to-all-start.5
  452.3 4.1 shard_map.374
  456.4 4.1 shard_map.373
  (624 shorter events, 337.5 us)
Async XLA Ops:
  7.2 58.2 %all-gather.12.cloned.1.call-start = ((), (), s32[]{:S(2)}) async-start(), calls=%async_computation.16 | async-start | bytes 1310720 | tf_op jit(solution)/shard_map/all_gather | solution.py:1382
  11.3 11.2 %all-to-all-start = ((bf16[8,32,512]{2,1,0:T(8,128)(2,1)}), bf16[8,32,512]{2,1,0:T(8,128)(2,1)S(1)}, u32[]{:S(2)}, u32[]{:S(2)}) async-start(bf16[8,32,512]{2,1,0:T(8,128)(2,1)} %get-tuple-element.322), calls=%async_computation | async-start | bytes 524288 | tf_op jit(solution)/shard_map/all_to_all | solution.py:1376
  16.5 58.8 %all-gather.10.cloned.1.call-start = ((), (), s32[]{:S(2)}) async-start(), calls=%async_computation.11 | async-start | bytes 1310720 | tf_op jit(solution)/shard_map/all_gather | solution.py:1382
  27.2 20.6 %collective-permute-start.2 = (bf16[128,1024]{1,0:T(8,128)(2,1)S(1)}, bf16[128,1024]{1,0:T(8,128)(2,1)}, u32[]{:S(2)}, u32[]{:S(2)}) collective-permute-start(bf16[128,1024]{1,0:T(8,128)(2,1)S(1)} %copy-done.30), channel_id=1, source_target_pairs={{0,1},{1,0},{2,6},{3,7},{4,5},{5,4},{6,2},{7,3},{8,9},{9,8},{10,14... | collective-permute-start | bytes 786440 | tf_op jit(solution)/shard_map/ppermute | solution.py:1292
  28.7 15.1 %all-to-all-start.2 = ((bf16[8,32,512]{2,1,0:T(8,128)(2,1)}), bf16[8,32,512]{2,1,0:T(8,128)(2,1)S(1)}, u32[]{:S(2)}, u32[]{:S(2)}) async-start(bf16[8,32,512]{2,1,0:T(8,128)(2,1)} %get-tuple-element.343), calls=%async_computation.2 | async-start | bytes 524288 | tf_op jit(solution)/shard_map/all_to_all | solution.py:1376
  34.2 13.8 %collective-permute-start.5 = (bf16[128,1024]{1,0:T(8,128)(2,1)}, bf16[128,1024]{1,0:T(8,128)(2,1)S(1)}, u32[]{:S(2)}, u32[]{:S(2)}) collective-permute-start(bf16[128,1024]{1,0:T(8,128)(2,1)} %collective-permute-done.1.refs_0_), channel_id=1, source_target_pairs={{0,1},{1,0},{2,6},{3,7},{4,5},{5,4},{6,2},{7,3},{8,9},{9,8},{10,14... | collective-permute-start | bytes 786440 | tf_op jit(solution)/shard_map/ppermute | solution.py:1292
  41.3 24.1 %collective-permute-start = (bf16[128,1024]{1,0:T(8,128)(2,1)S(1)}, bf16[128,1024]{1,0:T(8,128)(2,1)S(1)}, u32[]{:S(2)}, u32[]{:S(2)}) collective-permute-start(bf16[128,1024]{1,0:T(8,128)(2,1)S(1)} %copy-done.30), channel_id=1, source_target_pairs={{0,2},{2,0},{1,3},{3,1},{4,6},{6,4},{5,7},{7,5},{8,10},{10,8},{9,1... | collective-permute-start | bytes 786440 | tf_op jit(solution)/shard_map/ppermute | solution.py:44
  43.9 20.6 %all-to-all-start.1 = ((bf16[8,32,768]{2,1,0:T(8,128)(2,1)}), bf16[8,32,768]{2,1,0:T(8,128)(2,1)S(1)}, u32[]{:S(2)}, u32[]{:S(2)}) async-start(bf16[8,32,768]{2,1,0:T(8,128)(2,1)} %get-tuple-element.338), calls=%async_computation.1 | async-start | bytes 786432 | tf_op jit(solution)/shard_map/all_to_all | solution.py:1376
  47.3 65.8 %all-gather.14.cloned.1.call-start = ((), (), s32[]{:S(2)}) async-start(), calls=%async_computation.17 | async-start | bytes 1966080 | tf_op jit(solution)/shard_map/all_gather | solution.py:1382
  47.4 18.0 %collective-permute-start.3 = (bf16[128,1024]{1,0:T(8,128)(2,1)}, bf16[128,1024]{1,0:T(8,128)(2,1)}, u32[]{:S(2)}, u32[]{:S(2)}) collective-permute-start(bf16[128,1024]{1,0:T(8,128)(2,1)} %collective-permute-done.1.refs_0_), channel_id=1, source_target_pairs={{0,2},{2,0},{1,3},{3,1},{4,6},{6,4},{5,7},{7,5},{8,10},{10,8},{9,1... | collective-permute-start | bytes 786440 | tf_op jit(solution)/shard_map/ppermute | solution.py:44
  47.8 17.5 %collective-permute-start.4 = (bf16[128,1024]{1,0:T(8,128)(2,1)}, bf16[128,1024]{1,0:T(8,128)(2,1)}, u32[]{:S(2)}, u32[]{:S(2)}) collective-permute-start(bf16[128,1024]{1,0:T(8,128)(2,1)} %collective-permute-done.2.refs_1_), channel_id=1, source_target_pairs={{0,2},{2,0},{1,3},{3,1},{4,6},{6,4},{5,7},{7,5},{8,10},{10,8},{9,1... | collective-permute-start | bytes 786440 | tf_op jit(solution)/shard_map/ppermute | solution.py:44
  48.0 17.4 %collective-permute-start.6 = (bf16[128,1024]{1,0:T(8,128)(2,1)S(1)}, bf16[128,1024]{1,0:T(8,128)(2,1)S(1)}, u32[]{:S(2)}, u32[]{:S(2)}) collective-permute-start(bf16[128,1024]{1,0:T(8,128)(2,1)S(1)} %collective-permute-done.5.refs_0_), channel_id=1, source_target_pairs={{0,2},{2,0},{1,3},{3,1},{4,6},{6,4},{5,7},{7,5},{8,10},{10,8},{9,1... | collective-permute-start | bytes 786440 | tf_op jit(solution)/shard_map/ppermute | solution.py:44
  75.3 76.9 %all-gather.16.cloned.1.call-start = ((), (), s32[]{:S(2)}) async-start(), calls=%async_computation.18 | async-start | bytes 1310720 | tf_op jit(solution)/shard_map/all_gather | solution.py:1382
  104.2 92.0 %all-gather.18.cloned.1.call-start = ((), (), s32[]{:S(2)}) async-start(), calls=%async_computation.19 | async-start | bytes 2621440 | tf_op jit(solution)/shard_map/all_gather | solution.py:1382
  104.3 15.3 %collective-permute-start.20 = (bf16[128,1024]{1,0:T(8,128)(2,1)S(1)}, bf16[128,1024]{1,0:T(8,128)(2,1)S(1)}, u32[]{:S(2)}, u32[]{:S(2)}) collective-permute-start(bf16[128,1024]{1,0:T(8,128)(2,1)S(1)} %get-tuple-element.368.refs_2_), channel_id=1, source_target_pairs={{0,4},{1,5},{2,3},{3,2},{4,0},{5,1},{6,7},{7,6},{8,12},{9,13},{10,... | collective-permute-start | bytes 786440 | tf_op jit(solution)/shard_map/ppermute | solution.py:1292
  105.0 14.6 %collective-permute-start.21 = (bf16[128,1024]{1,0:T(8,128)(2,1)S(1)}, bf16[128,1024]{1,0:T(8,128)(2,1)S(1)}, u32[]{:S(2)}, u32[]{:S(2)}) collective-permute-start(bf16[128,1024]{1,0:T(8,128)(2,1)S(1)} %get-tuple-element.368.refs_2_), channel_id=1, source_target_pairs={{0,1},{1,0},{2,6},{3,7},{4,5},{5,4},{6,2},{7,3},{8,9},{9,8},{10,14... | collective-permute-start | bytes 786440 | tf_op jit(solution)/shard_map/ppermute | solution.py:1292
  106.4 221.3 %reduce-scatter.5.cloned.1.call-start = ((), (), s32[]{:S(2)}) async-start(), calls=%async_computation.12 | async-start | bytes 2621440 | tf_op jit(solution)/shard_map/reduce_scatter | solution.py:1385
  247.7 10.6 %collective-permute-start.69 = (bf16[2,128,1024]{2,1,0:T(8,128)(2,1)}, bf16[2,128,1024]{2,1,0:T(8,128)(2,1)}, u32[]{:S(2)}, u32[]{:S(2)}) collective-permute-start(bf16[2,128,1024]{2,1,0:T(8,128)(2,1)} %get-tuple-element.461), channel_id=1, source_target_pairs={{0,2},{2,0},{1,3},{3,1},{4,6},{6,4},{5,7},{7,5},{8,10},{10,8},{9,1... | collective-permute-start | bytes 1572872 | tf_op jit(solution)/shard_map/ppermute | solution.py:44
  273.9 99.9 %reduce-scatter.7.cloned.1.call-start = ((), (), s32[]{:S(2)}) async-start(), calls=%async_computation.13 | async-start | bytes 983040 | tf_op jit(solution)/shard_map/reduce_scatter | solution.py:1385
  327.8 91.1 %reduce-scatter.9.cloned.1.call-start = ((), (), s32[]{:S(2)}) async-start(), calls=%async_computation.14 | async-start | bytes 1966080 | tf_op jit(solution)/shard_map/reduce_scatter | solution.py:1385
  359.9 84.7 %reduce-scatter.11.cloned.1.call-start = ((), (), s32[]{:S(2)}) async-start(), calls=%async_computation.15 | async-start | bytes 2621440 | tf_op jit(solution)/shard_map/reduce_scatter | solution.py:1385
  423.5 11.6 %all-to-all-start.3 = ((bf16[8,32,768]{2,1,0:T(8,128)(2,1)}), bf16[8,32,768]{2,1,0:T(8,128)(2,1)S(1)}, u32[]{:S(2)}, u32[]{:S(2)}) async-start(bf16[8,32,768]{2,1,0:T(8,128)(2,1)} %shard_map.371), calls=%async_computation.7 | async-start | bytes 786432 | tf_op jit(solution)/shard_map/all_to_all | solution.py:1376
  427.1 11.5 %collective-permute-start.118 = (f32[45,128]{1,0:T(8,128)S(1)}, f32[45,128]{1,0:T(8,128)S(1)}, u32[]{:S(2)}, u32[]{:S(2)}) collective-permute-start(f32[45,128]{1,0:T(8,128)S(1)} %shard_map.376.refs_0_), channel_id=1, source_target_pairs={{0,8},{8,0},{16,24},{24,16},{1,9},{9,1},{17,25},{25,17},{2,10},{10... | collective-permute-start | bytes 69128 | tf_op jit(solution)/shard_map/ppermute | solution.py:44
  427.1 11.5 %collective-permute-start.119 = (f32[45,128]{1,0:T(8,128)S(1)}, f32[45,128]{1,0:T(8,128)S(1)}, u32[]{:S(2)}, u32[]{:S(2)}) collective-permute-start(f32[45,128]{1,0:T(8,128)S(1)} %shard_map.376.refs_0_), channel_id=1, source_target_pairs={{0,16},{8,24},{16,0},{24,8},{1,17},{9,25},{17,1},{25,9},{2,18},{10... | collective-permute-start | bytes 69128 | tf_op jit(solution)/shard_map/ppermute | solution.py:44
  (243 other events, 1543.0 us)
Sparse Core Ops, SparseCore 0:
  10.2 30.6 all-gather.11
  43.0 32.2 all-gather.9
  77.4 35.6 all-gather.13
  115.1 26.8 all-gather.15
  143.9 45.7 all-gather.17
  274.1 43.4 reduce-scatter.4
  327.9 21.3 reduce-scatter.6
  360.1 33.3 reduce-scatter.8
  401.0 43.5 reduce-scatter.10
